TPU v7x, 32 devices: a whole 2x2x4 slice. The times are simulated.
32 devices in a mesh: groups: 2 (over x), view: 16 (over z, y, core).
Axes of the slice: x: 2, y: 2, z: 4, core: 2. Of those that a mesh axis runs over, the one named last changes fastest.
Arguments:
- query_vectors: bfloat16 [32, 16, 8, 4096], P(('groups', 'view')), parts along dimension 0, may hold values from -6 to 6
- key_vectors: bfloat16 [32, 16, 8, 4096], P(('groups', 'view')), parts along dimension 0, may hold values from -6 to 6
- value_vectors: bfloat16 [32, 16, 8, 4096], P(('groups', 'view')), parts along dimension 0, may hold values from -6 to 6
- request_of_slot: int32 [8], P('groups'), parts along dimension 0, may hold values from 0 to 2, as said below
Outputs:
- attended: bfloat16 [32, 16, 8, 4096], P(('groups', 'view')), parts along dimension 0
There are 2 independent parts, one for each index of `groups`. A program takes and returns all parts, laid end to end along the dimension named above; each array names one. Nothing has to cross between parts.
Inputs may be any that keep to these rules, and one draw needn't show every extreme that they name: `request_of_slot`: each request holds 1 to 2 slots, not necessarily consecutive, and one holds exactly 2.
All inputs are finite; a program needn't handle non-finite values.
Results may differ from a plain program's by a relative error of at most 0.0044.
Values may be sent and summed in bfloat16 or wider, within the bound.
No kernel may reach another device: no remote copies, remote signals or barrier semaphores. Data moves between devices by JAX's collectives and lax.ppermute only.
A program may use at most 64 MiB of HBM per device.

v0:
```python
import jax
import jax.numpy as jnp
from jax import lax
from jax.sharding import PartitionSpec as P

HEADS = 32
HS = 128
ROWS = 16
COLS = 8


NEG_FILL = -1e30


def partner(value, axis, distance):
    return lax.ppermute(value, axis, [(i, i ^ 1 << distance) for i in range(lax.axis_size(axis))])


def masked_softmax(scores, allowed):
    scores = jnp.where(allowed, scores, NEG_FILL)
    maximum = jnp.max(scores, axis=-1)
    raised = jnp.exp(scores - maximum[..., None])
    totals = jnp.sum(raised, axis=-1)
    return (maximum, totals, raised.astype(jnp.bfloat16))


def combine(first_part, second_part):
    highest = jnp.maximum(first_part[0], second_part[0])
    first_scale = jnp.exp(first_part[0] - highest)
    second_scale = jnp.exp(second_part[0] - highest)
    denominator = first_part[1] * first_scale + second_part[1] * second_scale
    numerator = first_part[2] * first_scale[..., None] + second_part[2] * second_scale[..., None]
    return (numerator / denominator[..., None]).astype(jnp.bfloat16)


def into_rows(tensor, row_blocks, head_groups):
    trailing = tensor.shape[3:]
    block_rows = tensor.shape[0] // row_blocks
    width_cols = tensor.shape[1]
    group_heads = tensor.shape[2] // head_groups
    shaped = tensor.reshape(
        (row_blocks, block_rows, width_cols, head_groups, group_heads) + trailing
    )
    permuted = (0, 3, 1, 2, 4) + tuple(range(5, 5 + len(trailing)))
    return shaped.transpose(permuted).reshape(
        (row_blocks * head_groups, block_rows, width_cols, group_heads) + trailing
    )


def into_tokens(tensor, row_blocks, head_groups):
    trailing = tensor.shape[4:]
    block_rows = tensor.shape[1]
    width_cols = tensor.shape[2]
    group_heads = tensor.shape[3]
    shaped = tensor.reshape(
        (row_blocks, head_groups, block_rows, width_cols, group_heads) + trailing
    )
    permuted = (0, 2, 3, 1, 4) + tuple(range(5, 5 + len(trailing)))
    return shaped.transpose(permuted).reshape(
        (row_blocks * block_rows * width_cols, head_groups * group_heads) + trailing
    )


def shards(query_vectors, key_vectors, value_vectors, request_of_slot):
    scaling = HS ** (-0.5)
    token_count = ROWS * COLS
    partner_key, partner_value = partner((key_vectors, value_vectors), "view", 0)
    head_blocks = 4
    block_heads = HEADS // head_blocks
    own_query = query_vectors.reshape(token_count, head_blocks, block_heads, HS)
    both_keys = jnp.concatenate(
        [
            key_vectors.reshape(token_count, head_blocks, block_heads, HS),
            partner_key.reshape(token_count, head_blocks, block_heads, HS),
        ],
        axis=0,
    )
    both_values = jnp.concatenate(
        [
            value_vectors.reshape(token_count, head_blocks, block_heads, HS),
            partner_value.reshape(token_count, head_blocks, block_heads, HS),
        ],
        axis=0,
    )
    query_row = jnp.arange(token_count) // COLS
    key_row = jnp.arange(2 * token_count) % token_count // COLS
    local_allowed = query_row[:, None] != key_row[None, :]

    def local_block(triple):
        block_scores = (
            jnp.einsum("nhx,khx->hnk", triple[0], triple[1], preferred_element_type=jnp.float32)
            * scaling
        )
        block_peak, block_total, block_weights = masked_softmax(block_scores, local_allowed[None])
        block_sum = jnp.einsum(
            "hnk,khx->nhx", block_weights, triple[2], preferred_element_type=jnp.float32
        )
        return (block_peak.T, block_total.T, block_sum)

    block_peaks, block_totals, block_sums = lax.map(
        local_block,
        (
            jnp.moveaxis(own_query, 1, 0),
            jnp.moveaxis(both_keys, 1, 0),
            jnp.moveaxis(both_values, 1, 0),
        ),
    )
    local_peak = jnp.moveaxis(block_peaks, 0, 1).reshape(token_count, HEADS)
    local_total = jnp.moveaxis(block_totals, 0, 1).reshape(token_count, HEADS)
    local_sum = jnp.moveaxis(block_sums, 0, 1).reshape(token_count, HEADS, HS)
    device_count = lax.axis_size("view")
    slot_count = device_count // 4
    pass_images = device_count // 2
    head_groups = 8
    row_blocks = device_count // head_groups
    block_rows = ROWS // row_blocks
    slot_request = jnp.broadcast_to(
        request_of_slot[:, None], (request_of_slot.shape[0], 2 * COLS)
    ).reshape(-1)
    row_allowed = slot_request[:, None] == slot_request[None, :]

    def arrange(tensor):
        shaped = tensor.reshape(slot_count, 2, 2, block_rows, COLS, HS).transpose(1, 3, 0, 2, 4, 5)
        return shaped.reshape(2 * block_rows, pass_images * COLS, HS)

    def restore(tensor):
        trailing = tensor.shape[2:]
        shaped = tensor.reshape((2, block_rows, slot_count, 2, COLS) + trailing)
        permuted = (2, 0, 3, 1, 4) + tuple(range(5, 5 + len(trailing)))
        return shaped.transpose(permuted).reshape((device_count, block_rows, COLS) + trailing)

    def one_head(triple):
        row_scores = (
            jnp.einsum(
                "bnx,bkx->bnk",
                arrange(triple[0]),
                arrange(triple[1]),
                preferred_element_type=jnp.float32,
            )
            * scaling
        )
        row_peak, row_total, row_weights = masked_softmax(row_scores, row_allowed[None])
        row_sum = jnp.einsum(
            "bnk,bkx->bnx", row_weights, arrange(triple[2]), preferred_element_type=jnp.float32
        )
        return (restore(row_peak), restore(row_total), restore(row_sum))

    query_rows = into_rows(query_vectors.reshape(ROWS, COLS, HEADS, HS), row_blocks, head_groups)
    key_rows = into_rows(key_vectors.reshape(ROWS, COLS, HEADS, HS), row_blocks, head_groups)
    value_rows = into_rows(value_vectors.reshape(ROWS, COLS, HEADS, HS), row_blocks, head_groups)
    by_head = (
        jnp.moveaxis(
            lax.all_to_all(query_rows, "view", split_axis=0, concat_axis=0, tiled=True), 3, 0
        ),
        jnp.moveaxis(
            lax.all_to_all(key_rows, "view", split_axis=0, concat_axis=0, tiled=True), 3, 0
        ),
        jnp.moveaxis(
            lax.all_to_all(value_rows, "view", split_axis=0, concat_axis=0, tiled=True), 3, 0
        ),
    )
    row_peaks, row_totals, row_sums = lax.map(one_head, by_head)
    peak_part = jnp.moveaxis(row_peaks, 0, 3)
    total_part = jnp.moveaxis(row_totals, 0, 3)
    sum_part = jnp.moveaxis(row_sums, 0, 3)
    row_peak = lax.all_to_all(peak_part, "view", split_axis=0, concat_axis=0, tiled=True)
    row_total = lax.all_to_all(total_part, "view", split_axis=0, concat_axis=0, tiled=True)
    row_sum = lax.all_to_all(sum_part, "view", split_axis=0, concat_axis=0, tiled=True)
    row_peak = into_tokens(row_peak, row_blocks, head_groups)
    row_total = into_tokens(row_total, row_blocks, head_groups)
    row_sum = into_tokens(row_sum, row_blocks, head_groups)
    attended = combine((local_peak, local_total, local_sum), (row_peak, row_total, row_sum))
    return attended.reshape(1, ROWS, COLS, HEADS * HS)


def solution(mesh):
    return jax.shard_map(
        shards,
        mesh=mesh,
        in_specs=(
            P(("groups", "view"), None, None, None),
            P(("groups", "view"), None, None, None),
            P(("groups", "view"), None, None, None),
            P("groups"),
        ),
        out_specs=P(("groups", "view"), None, None, None),
        check_vma=False,
    )
```

profile of v0, /device:TPU:10, one launch (start us, length us, event | category | flops | bytes accessed | tf_op | source)
XLA Modules:
  0.0 189.0 jit_solution(3276017524597650835)
XLA Ops:
  0.0 2.5 %copy.68 = bf16[2,8,8,8,4,128]{5,2,1,4,3,0:T(8,128)(2,1)} copy(bf16[2,8,8,8,4,128]{5,2,4,3,1,0:T(8,128)(2,1)} %bitcast.210) | data formatting | bytes 2097152 | tf_op jit(solution)/shard_map/reshape;reshape | solution.py:41
  2.5 6.3 %all-to-all-start = ((bf16[16,8,8,4,128]{4,2,1,3,0:T(8,128)(2,1)}), bf16[16,8,8,4,128]{4,2,1,3,0:T(8,128)(2,1)S(1)}, u32[]{:S(2)}, u32[]{:S(2)}) async-start(bf16[16,8,8,4,128]{4,2,1,3,0:T(8,128)(2,1)} %bitcast.9), calls=%async_computation | async-start | bytes 2097152 | tf_op jit(solution)/shard_map/all_to_all | solution.py:153
  8.8 2.5 %copy.69 = bf16[2,8,8,8,4,128]{5,2,1,4,3,0:T(8,128)(2,1)} copy(bf16[2,8,8,8,4,128]{5,2,4,3,1,0:T(8,128)(2,1)} %bitcast.11) | data formatting | bytes 2097152 | tf_op jit(solution)/shard_map/reshape;reshape | solution.py:41
  11.3 21.6 %all-to-all-done = bf16[16,8,8,4,128]{4,2,1,3,0:T(8,128)(2,1)S(1)} async-done(((bf16[16,8,8,4,128]{4,2,1,3,0:T(8,128)(2,1)}), bf16[16,8,8,4,128]{4,2,1,3,0:T(8,128)(2,1)S(1)}, u32[]{:S(2)}, u32[]{:S(2)}) %all-to-all-start) | async-done | bytes 1048608 | tf_op jit(solution)/shard_map/all_to_all | solution.py:153
  32.9 5.6 %all-to-all-start.1 = ((bf16[16,8,8,4,128]{4,2,1,3,0:T(8,128)(2,1)}), bf16[16,8,8,4,128]{4,2,1,3,0:T(8,128)(2,1)}, u32[]{:S(2)}, u32[]{:S(2)}) async-start(bf16[16,8,8,4,128]{4,2,1,3,0:T(8,128)(2,1)} %bitcast.13), calls=%async_computation.1 | async-start | bytes 2097152 | tf_op jit(solution)/shard_map/all_to_all | solution.py:156
  38.5 2.6 %copy.70 = bf16[2,8,8,8,4,128]{5,2,1,4,3,0:T(8,128)(2,1)} copy(bf16[2,8,8,8,4,128]{5,2,4,3,1,0:T(8,128)(2,1)} %bitcast.15) | data formatting | bytes 2097152 | tf_op jit(solution)/shard_map/reshape;reshape | solution.py:41
  41.1 21.6 %all-to-all-done.1 = bf16[16,8,8,4,128]{4,2,1,3,0:T(8,128)(2,1)} async-done(((bf16[16,8,8,4,128]{4,2,1,3,0:T(8,128)(2,1)}), bf16[16,8,8,4,128]{4,2,1,3,0:T(8,128)(2,1)}, u32[]{:S(2)}, u32[]{:S(2)}) %all-to-all-start.1) | async-done | bytes 1048608 | tf_op jit(solution)/shard_map/all_to_all | solution.py:156
  62.7 5.6 %all-to-all-start.2 = ((bf16[16,8,8,4,128]{4,2,1,3,0:T(8,128)(2,1)}), bf16[16,8,8,4,128]{4,2,1,3,0:T(8,128)(2,1)}, u32[]{:S(2)}, u32[]{:S(2)}) async-start(bf16[16,8,8,4,128]{4,2,1,3,0:T(8,128)(2,1)} %bitcast.17), calls=%async_computation.2 | async-start | bytes 2097152 | tf_op jit(solution)/shard_map/all_to_all | solution.py:159
  69.1 2.4 %copy.97 = bf16[16,8,32,128]{3,2,1,0:T(8,128)(2,1)} copy(bf16[16,8,32,128]{3,1,2,0:T(8,128)(2,1)} %bitcast.87) | data formatting | bytes 2097152
  71.5 2.4 %copy.99 = bf16[16,8,32,128]{3,2,1,0:T(8,128)(2,1)} copy(bf16[16,8,32,128]{3,1,2,0:T(8,128)(2,1)} %bitcast.97) | data formatting | bytes 2097152
  74.1 2.4 %copy.98 = bf16[16,8,32,128]{3,2,1,0:T(8,128)(2,1)} copy(bf16[16,8,32,128]{3,1,2,0:T(8,128)(2,1)} %bitcast.92) | data formatting | bytes 2097152
  76.5 2.4 %copy.100 = bf16[16,8,32,128]{3,2,1,0:T(8,128)(2,1)} copy(bf16[16,8,32,128]{3,1,2,0:T(8,128)(2,1)} %bitcast.102) | data formatting | bytes 2097152
  79.0 13.5 %all-to-all-done.2 = bf16[16,8,8,4,128]{4,2,1,3,0:T(8,128)(2,1)} async-done(((bf16[16,8,8,4,128]{4,2,1,3,0:T(8,128)(2,1)}), bf16[16,8,8,4,128]{4,2,1,3,0:T(8,128)(2,1)}, u32[]{:S(2)}, u32[]{:S(2)}) %all-to-all-start.2) | async-done | bytes 1048608 | tf_op jit(solution)/shard_map/all_to_all | solution.py:159
  92.4 15.7 %while.31 = (s32[]{:T(128)}, f32[4,16,8,8]{3,2,0,1:T(8,128)S(1)}, f32[4,16,8,8]{3,2,0,1:T(8,128)}, f32[4,16,8,8,128]{4,3,2,0,1:T(8,128)}, bf16[4,16,8,8,128]{4,3...) while((s32[]{:T(128)}, f32[4,16,8,8]{3,2,0,1:T(8,128)S(1)}, ...), condition=%wide.region_7.8_spmd.clone, body=%wide.region_4.7_spmd.clone.sunk | while | flops 34015232 | bytes 7598457 | solution.py:162
  92.5 1.1 constant_dynamic-slice_fusion.15
  94.5 0.6 constant_dynamic-update-slice_fusion.7
  95.5 0.8 constant_dynamic-update-slice_fusion.8
  96.4 1.1 constant_dynamic-slice_fusion.15
  98.4 0.6 constant_dynamic-update-slice_fusion.7
  99.5 0.8 constant_dynamic-update-slice_fusion.8
  100.4 1.1 constant_dynamic-slice_fusion.15
  102.3 0.6 constant_dynamic-update-slice_fusion.7
  103.4 0.9 constant_dynamic-update-slice_fusion.8
  104.3 1.1 constant_dynamic-slice_fusion.15
  106.3 0.6 constant_dynamic-update-slice_fusion.7
  107.3 0.8 constant_dynamic-update-slice_fusion.8
  108.2 1.1 bitcast_bitcast_fusion
  109.2 0.8 reshape.262
  110.0 5.6 %all-to-all-start.5 = ((f32[16,1,256]{2,1,0:T(1,128)}), f32[16,1,256]{2,1,0:T(1,128)S(1)}, u32[]{:S(2)}, u32[]{:S(2)}) async-start(f32[16,1,256]{2,1,0:T(1,128)} %reshape.262), calls=%async_computation.5 | async-start | bytes 32768 | tf_op jit(solution)/shard_map/all_to_all | solution.py:167
  115.6 0.8 reshape.260
  116.4 4.2 %all-to-all-done.5 = f32[16,1,256]{2,1,0:T(1,128)S(1)} async-done(((f32[16,1,256]{2,1,0:T(1,128)}), f32[16,1,256]{2,1,0:T(1,128)S(1)}, u32[]{:S(2)}, u32[]{:S(2)}) %all-to-all-start.5) | async-done | bytes 16416 | tf_op jit(solution)/shard_map/all_to_all | solution.py:167
  120.6 4.8 %all-to-all-start.3 = ((f32[16,1,256]{2,1,0:T(1,128)}), f32[16,1,256]{2,1,0:T(1,128)S(1)}, u32[]{:S(2)}, u32[]{:S(2)}) async-start(f32[16,1,256]{2,1,0:T(1,128)} %reshape.260), calls=%async_computation.3 | async-start | bytes 32768 | tf_op jit(solution)/shard_map/all_to_all | solution.py:166
  125.5 4.2 %maximum_bitcast_fusion = (bf16[4,256,8,128]{3,2,0,1:T(8,128)(2,1)}, bf16[4,256,8,128]{3,2,0,1:T(8,128)(2,1)}) fusion(bf16[128,4,8,128]{3,2,1,0:T(8,128)(2,1)} %bitcast.214, bf16[128,4,8,128]{3,2,1,0:T(8,128)(2,1)S(1)} %bitcast.212, bf16[128,4,8,128]{3,2,1,0:T(8,128)(2,1)} %bitcast.215, bf16[128,4,8,128]{3,2,1,0:T(8,128)(2,1)} %bitcast.213), kind=kLoop, calls=%fused_computation.33 | loop fusion | flops 2097152 | bytes 8388608 | tf_op jit(solution)/shard_map/transpose | solution.py:104
  129.7 0.9 all-to-all-done.3
  130.6 5.8 %all-to-all-start.4 = ((f32[16,8,8,4,128]{4,2,1,3,0:T(8,128)}), f32[16,8,8,4,128]{4,2,1,3,0:T(8,128)}, u32[]{:S(2)}, u32[]{:S(2)}) async-start(f32[16,8,8,4,128]{4,2,1,3,0:T(8,128)} %bitcast.217), calls=%async_computation.4 | async-start | bytes 4194304 | tf_op jit(solution)/shard_map/all_to_all | solution.py:168
  136.3 18.6 %while.30 = (s32[]{:T(128)}, f32[4,128,8]{1,2,0:T(8,128)S(1)}, f32[4,128,8]{1,2,0:T(8,128)S(1)}, f32[4,128,8,128]{1,3,2,0:T(8,128)}, bf16[4,128,8,128]{3,2,0,1:T...) while((s32[]{:T(128)}, f32[4,128,8]{1,2,0:T(8,128)S(1)}, ...), condition=%wide.region_3.4_spmd.clone, body=%wide.region_0.3_spmd.clone.sunk | while | flops 136083456 | bytes 8750721 | solution.py:100
  136.3 1.1 constant_dynamic-slice_fusion.11
  138.4 1.1 constant_dynamic-slice_fusion.13
  139.8 1.2 fusion.43
  141.0 1.1 constant_dynamic-slice_fusion.11
  143.0 1.1 constant_dynamic-slice_fusion.13
  144.5 1.2 fusion.43
  145.6 1.1 constant_dynamic-slice_fusion.11
  147.7 1.1 constant_dynamic-slice_fusion.13
  149.1 1.2 fusion.43
  150.3 1.1 constant_dynamic-slice_fusion.11
  151.5 0.4 fusion.41
  152.3 1.1 constant_dynamic-slice_fusion.13
  153.8 1.2 fusion.43
  154.9 2.4 %copy.67 = f32[128,4,8,128]{3,2,1,0:T(8,128)S(1)} copy(f32[128,4,8,128]{0,3,2,1:T(8,128)} %bitcast.216) | data formatting | bytes 4194304 | tf_op jit(solution)/shard_map/transpose | solution.py:110
  157.3 1.6 reshape.239
  158.9 0.5 broadcast.109
  159.4 0.7 reduce
  160.4 0.7 reduce.1
  161.6 0.6 div.43
  162.2 1.5 div.44
  163.8 0.6 mul.57
  164.4 1.5 mul.58
  166.1 0.6 mul.54
  166.7 1.5 mul.55
  168.2 14.0 %all-to-all-done.4 = f32[16,8,8,4,128]{4,2,1,3,0:T(8,128)} async-done(((f32[16,8,8,4,128]{4,2,1,3,0:T(8,128)}), f32[16,8,8,4,128]{4,2,1,3,0:T(8,128)}, u32[]{:S(2)}, u32[]{:S(2)}) %all-to-all-start.4) | async-done | bytes 2097184 | tf_op jit(solution)/shard_map/all_to_all | solution.py:168
  182.2 2.0 %copy.78 = f32[2,8,8,8,4,128]{5,2,4,3,1,0:T(8,128)S(1)} copy(f32[2,8,8,8,4,128]{5,2,1,4,3,0:T(8,128)} %bitcast.24) | data formatting | bytes 4194304 | tf_op jit(solution)/shard_map/transpose | solution.py:59
  184.4 0.6 copy-done.1
  185.1 3.9 %divide_convert_fusion = bf16[1,16,8,4096]{3,2,1,0:T(8,128)(2,1)} fusion(f32[1,16,8,4096]{3,2,1,0:T(8,128)S(1)} %copy-done.1, f32[1,16,8,4096]{3,2,1,0:T(8,128)S(1)} %bitcast.203, f32[1,16,8,4096]{3,2,1,0:T(8,128)} %mul.58, f32[1,16,8,4096]{3,2,1,0:T(8,128)S(1)} %copy-done, f32[1,16,8,4096]{3,2,1,0:T(8,128)} %mul.55), kind=kLoop, calls=%fused_computation.35 | loop fusion | flops 2621440 | bytes 11534336 | tf_op jit(solution)/shard_map/convert_element_type | solution.py:33
  (114 shorter events, 11.8 us)
Async XLA Ops:
  2.5 30.4 %all-to-all-start = ((bf16[16,8,8,4,128]{4,2,1,3,0:T(8,128)(2,1)}), bf16[16,8,8,4,128]{4,2,1,3,0:T(8,128)(2,1)S(1)}, u32[]{:S(2)}, u32[]{:S(2)}) async-start(bf16[16,8,8,4,128]{4,2,1,3,0:T(8,128)(2,1)} %bitcast.9), calls=%async_computation | async-start | bytes 2097152 | tf_op jit(solution)/shard_map/all_to_all | solution.py:153
  32.9 29.8 %all-to-all-start.1 = ((bf16[16,8,8,4,128]{4,2,1,3,0:T(8,128)(2,1)}), bf16[16,8,8,4,128]{4,2,1,3,0:T(8,128)(2,1)}, u32[]{:S(2)}, u32[]{:S(2)}) async-start(bf16[16,8,8,4,128]{4,2,1,3,0:T(8,128)(2,1)} %bitcast.13), calls=%async_computation.1 | async-start | bytes 2097152 | tf_op jit(solution)/shard_map/all_to_all | solution.py:156
  38.5 30.3 %copy-start.2 = (bf16[1,16,8,4096]{3,2,1,0:T(8,128)(2,1)S(1)}, bf16[1,16,8,4096]{3,2,1,0:T(8,128)(2,1)}, u32[]{:S(2)}) copy-start(bf16[1,16,8,4096]{3,2,1,0:T(8,128)(2,1)} %param.8) | copy-start | bytes 3145732
  62.7 29.8 %all-to-all-start.2 = ((bf16[16,8,8,4,128]{4,2,1,3,0:T(8,128)(2,1)}), bf16[16,8,8,4,128]{4,2,1,3,0:T(8,128)(2,1)}, u32[]{:S(2)}, u32[]{:S(2)}) async-start(bf16[16,8,8,4,128]{4,2,1,3,0:T(8,128)(2,1)} %bitcast.17), calls=%async_computation.2 | async-start | bytes 2097152 | tf_op jit(solution)/shard_map/all_to_all | solution.py:159
  68.3 5.8 %collective-permute-start = (bf16[1,16,8,4096]{3,2,1,0:T(8,128)(2,1)}, bf16[1,16,8,4096]{3,2,1,0:T(8,128)(2,1)}, u32[]{:S(2)}, u32[]{:S(2)}) collective-permute-start(bf16[1,16,8,4096]{3,2,1,0:T(8,128)(2,1)} %param.9), channel_id=1, source_target_pairs={{0,1},{1,0},{2,3},{3,2},{4,5},{5,4},{6,7},{7,6},{8,9},{9,8},{10,11... | collective-permute-start | bytes 3145736 | tf_op jit(solution)/shard_map/ppermute | solution.py:16
  68.4 8.1 %collective-permute-start.1 = (bf16[1,16,8,4096]{3,2,1,0:T(8,128)(2,1)}, bf16[1,16,8,4096]{3,2,1,0:T(8,128)(2,1)}, u32[]{:S(2)}, u32[]{:S(2)}) collective-permute-start(bf16[1,16,8,4096]{3,2,1,0:T(8,128)(2,1)} %param.10), channel_id=1, source_target_pairs={{0,1},{1,0},{2,3},{3,2},{4,5},{5,4},{6,7},{7,6},{8,9},{9,8},{10,11... | collective-permute-start | bytes 3145736 | tf_op jit(solution)/shard_map/ppermute | solution.py:16
  69.0 4.9 %copy-start.4 = (s32[4]{0:T(128)S(1)}, s32[4]{0:T(128)}, u32[]{:S(2)}) copy-start(s32[4]{0:T(128)} %param.11) | copy-start | bytes 52
  108.2 17.3 %copy-start.3 = (bf16[16,8,32,128]{3,2,1,0:T(8,128)(2,1)S(1)}, bf16[16,8,32,128]{3,2,1,0:T(8,128)(2,1)}, u32[]{:S(2)}) copy-start(bf16[16,8,32,128]{3,2,1,0:T(8,128)(2,1)} %copy.97) | copy-start | bytes 3145732
  110.0 10.6 %all-to-all-start.5 = ((f32[16,1,256]{2,1,0:T(1,128)}), f32[16,1,256]{2,1,0:T(1,128)S(1)}, u32[]{:S(2)}, u32[]{:S(2)}) async-start(f32[16,1,256]{2,1,0:T(1,128)} %reshape.262), calls=%async_computation.5 | async-start | bytes 32768 | tf_op jit(solution)/shard_map/all_to_all | solution.py:167
  120.6 9.9 %all-to-all-start.3 = ((f32[16,1,256]{2,1,0:T(1,128)}), f32[16,1,256]{2,1,0:T(1,128)S(1)}, u32[]{:S(2)}, u32[]{:S(2)}) async-start(f32[16,1,256]{2,1,0:T(1,128)} %reshape.260), calls=%async_computation.3 | async-start | bytes 32768 | tf_op jit(solution)/shard_map/all_to_all | solution.py:166
  130.6 51.6 %all-to-all-start.4 = ((f32[16,8,8,4,128]{4,2,1,3,0:T(8,128)}), f32[16,8,8,4,128]{4,2,1,3,0:T(8,128)}, u32[]{:S(2)}, u32[]{:S(2)}) async-start(f32[16,8,8,4,128]{4,2,1,3,0:T(8,128)} %bitcast.217), calls=%async_computation.4 | async-start | bytes 4194304 | tf_op jit(solution)/shard_map/all_to_all | solution.py:168
  182.2 2.2 %copy-start = (f32[1,16,8,4096]{3,2,1,0:T(8,128)S(1)}, f32[1,16,8,4096]{3,2,1,0:T(8,128)}, u32[]{:S(2)}) copy-start(f32[1,16,8,4096]{3,2,1,0:T(8,128)} %reshape.239) | copy-start | bytes 6291460
  182.2 2.9 %copy-start.1 = (f32[1,16,8,4096]{3,2,1,0:T(8,128)S(1)}, f32[1,16,8,4096]{3,2,1,0:T(8,128)}, u32[]{:S(2)}) copy-start(f32[1,16,8,4096]{3,2,1,0:T(8,128)} %div.44) | copy-start | bytes 6291460
where the time goes:
time: 192 us; the launch traced here: 189 us
  waiting for transfers between devices  75.7 us (39%)
  local copies, waits for them, and re-layouts  57.5 us (30%)
  starting transfers between devices  34.3 us (18%)
  other arithmetic  12.1 us (6%)
  matrix products  8.65 us (5%)
    all_to_all x1, waiting for transfers between devices, shards(): lax.all_to_all(query_rows, 'view', split_axis=0, concat_axis=0, tiled=True)  21.6 us
    all_to_all x1, waiting for transfers between devices, shards(): lax.all_to_all(key_rows, 'view', split_axis=0, concat_axis=0, tiled=True)  21.6 us
    all_to_all x1, waiting for transfers between devices, shards(): lax.all_to_all(sum_part, 'view', split_axis=0, concat_axis=0, tiled=True)  14 us
    unnamed x21, local copies, waits for them, and re-layouts  13.7 us
    all_to_all x1, waiting for transfers between devices, shards(): lax.all_to_all(value_rows, 'view', split_axis=0, concat_axis=0, tiled=True)  13.5 us
    dynamic_slice x16, local copies, waits for them, and re-layouts, shards(): lax.map(local_block, (jnp.moveaxis(own_query, 1, 0), jnp.moveaxis(both_ke...  10.1 us
    another operation x3, local copies, waits for them, and re-layouts, into_rows(): tensor.reshape((row_blocks, block_rows, width_cols, head_groups, group_he...  7.58 us
    all_to_all x1, starting transfers between devices, shards(): lax.all_to_all(query_rows, 'view', split_axis=0, concat_axis=0, tiled=True)  6.3 us
  transfers between devices with their start and end apart: 8, of which 6 were waited for; matrix products, arithmetic and copies ran while one was open for 27% of the time, Pallas kernels for 0%

commit v1 on v0

--- a/solution.py
+++ b/solution.py
@@ -1,6 +1,10 @@
+import functools
+
 import jax
 import jax.numpy as jnp
 from jax import lax
+from jax.experimental import pallas as pl
+from jax.experimental.pallas import tpu as pltpu
 from jax.sharding import PartitionSpec as P
 
 HEADS = 32
@@ -61,7 +65,7 @@
     )
 
 
-def shards(query_vectors, key_vectors, value_vectors, request_of_slot):
+def many_slots(query_vectors, key_vectors, value_vectors, request_of_slot):
     scaling = HS ** (-0.5)
     token_count = ROWS * COLS
     partner_key, partner_value = partner((key_vectors, value_vectors), "view", 0)
@@ -173,6 +177,236 @@
     return attended.reshape(1, ROWS, COLS, HEADS * HS)
 
 
+SCALING = HS ** (-0.5)
+LANES = 128
+PIECES = 3
+CHUNKS = 2
+
+
+def scores_of(query, keys):
+    return lax.dot_general(query, keys, (((1,), (1,)), ((), ())), preferred_element_type=jnp.float32)
+
+
+def own_kernel(query_ref, first_key, second_key, first_value, second_value, mean_ref, lse_ref):
+    step = pl.program_id(0)
+    block_heads = query_ref.shape[1] // HS
+    lane = lax.broadcasted_iota(jnp.int32, lse_ref.shape, 1)
+
+    @pl.when(step == 0)
+    def _():
+        lse_ref[...] = jnp.zeros_like(lse_ref)
+
+    found = lse_ref[...]
+    for head in range(block_heads):
+        at = slice(head * HS, (head + 1) * HS)
+        first = scores_of(query_ref[:, at], first_key[:, at])
+        second = scores_of(query_ref[:, at], second_key[:, at])
+        peak = jnp.max(jnp.maximum(first, second), axis=1, keepdims=True)
+        first = jnp.exp((first - peak) * SCALING)
+        second = jnp.exp((second - peak) * SCALING)
+        total = jnp.sum(first + second, axis=1, keepdims=True)
+        summed = jnp.dot(
+            first.astype(jnp.bfloat16), first_value[:, at], preferred_element_type=jnp.float32
+        ) + jnp.dot(
+            second.astype(jnp.bfloat16), second_value[:, at], preferred_element_type=jnp.float32
+        )
+        mean_ref[:, at] = summed / total
+        lse = peak * SCALING + jnp.log(total)
+        found = jnp.where(lane == step * block_heads + head, lse, found)
+    lse_ref[...] = found
+
+
+def own_attention(query, keys, values, block_heads=2):
+    tokens, width = query.shape
+    heads = width // HS
+    block = pl.BlockSpec((tokens, block_heads * HS), lambda i: (0, i))
+    return pl.pallas_call(
+        own_kernel,
+        grid=(heads // block_heads,),
+        in_specs=[block] * 5,
+        out_specs=[block, pl.BlockSpec((tokens, LANES), lambda i: (0, 0))],
+        out_shape=[
+            jax.ShapeDtypeStruct((tokens, width), jnp.float32),
+            jax.ShapeDtypeStruct((tokens, LANES), jnp.float32),
+        ],
+        cost_estimate=pl.CostEstimate(
+            flops=8 * tokens * tokens * width, bytes_accessed=14 * tokens * width, transcendentals=0
+        ),
+        name="own_attention",
+    )(query, *keys, *values)
+
+
+def guest_kernel(query_ref, first_key, second_key, first_value, second_value, sent_ref):
+    tokens, width = query_ref.shape
+    query_row = lax.broadcasted_iota(jnp.int32, (tokens, tokens), 0) // COLS
+    key_row = lax.broadcasted_iota(jnp.int32, (tokens, tokens), 1) // COLS
+    same_row = query_row == key_row
+    lane = lax.broadcasted_iota(jnp.int32, (tokens, LANES), 1)
+    heads = width // HS
+
+    def one_head(head, found):
+        at = pl.ds(pl.multiple_of(head * HS, HS), HS)
+        query = query_ref[:, at]
+        first = jnp.where(same_row, scores_of(query, first_key[:, at]), NEG_FILL)
+        second = jnp.where(same_row, scores_of(query, second_key[:, at]), NEG_FILL)
+        peak = jnp.max(jnp.maximum(first, second), axis=1, keepdims=True)
+        first = jnp.exp((first - peak) * SCALING)
+        second = jnp.exp((second - peak) * SCALING)
+        total = jnp.sum(first + second, axis=1, keepdims=True)
+        summed = jnp.dot(
+            first.astype(jnp.bfloat16), first_value[:, at], preferred_element_type=jnp.float32
+        ) + jnp.dot(
+            second.astype(jnp.bfloat16), second_value[:, at], preferred_element_type=jnp.float32
+        )
+        sent_ref[:, at] = (summed / total).astype(jnp.bfloat16)
+        left = peak * SCALING + jnp.log(total)
+        for piece in range(PIECES):
+            part = left.astype(jnp.bfloat16).astype(jnp.float32)
+            left = left - part
+            found = jnp.where(lane == piece * heads + head, part, found)
+        return found
+
+    found = lax.fori_loop(0, heads, one_head, jnp.zeros((tokens, LANES), jnp.float32), unroll=2)
+    sent_ref[:, width:] = found.astype(jnp.bfloat16)
+
+
+def guest_attention(query, keys, values, chunk):
+    tokens, width = query.shape
+    whole = pl.BlockSpec((tokens, width), lambda i: (0, 0))
+    block = pl.BlockSpec((tokens, width), lambda i: (chunk, 0))
+    return pl.pallas_call(
+        guest_kernel,
+        grid=(1,),
+        in_specs=[whole] + [block] * 4,
+        out_specs=pl.BlockSpec((tokens, width + LANES), lambda i: (0, 0)),
+        out_shape=jax.ShapeDtypeStruct((tokens, width + LANES), jnp.bfloat16),
+        cost_estimate=pl.CostEstimate(
+            flops=8 * tokens * tokens * width, bytes_accessed=12 * tokens * width, transcendentals=0
+        ),
+        name="guest_attention",
+    )(query, *keys, *values)
+
+
+def merge_kernel(has_guest, mean_ref, lse_ref, sent_ref, *rest):
+    out_ref = rest[-1]
+    width = mean_ref.shape[1]
+    heads = width // HS
+    pieces = sent_ref[:, width:].astype(jnp.float32)
+    lse = pieces
+    for piece in range(1, PIECES):
+        lse = lse + pltpu.roll(pieces, LANES - piece * heads, 1)
+    lse = jnp.where(has_guest[0] > 0, lse, NEG_FILL)
+    share = 1.0 / (1.0 + jnp.exp(lse_ref[...] - lse))
+    for head in range(heads):
+        at = slice(head * HS, (head + 1) * HS)
+        own = mean_ref[:, at]
+        guest = sent_ref[:, at].astype(jnp.float32)
+        out_ref[:, at] = (own + share[:, head : head + 1] * (guest - own)).astype(jnp.bfloat16)
+
+
+def merge(has_guest, mean, lse, sent, chunk, before, steps=4):
+    tokens, width = mean.shape
+    part_tokens = sent.shape[0]
+    block_tokens = part_tokens // steps
+    here = lambda i, flag: (chunk * steps + i, 0)
+    return pl.pallas_call(
+        merge_kernel,
+        grid_spec=pltpu.PrefetchScalarGridSpec(
+            num_scalar_prefetch=1,
+            grid=(steps,),
+            in_specs=[
+                pl.BlockSpec((block_tokens, width), here),
+                pl.BlockSpec((block_tokens, LANES), here),
+                pl.BlockSpec((block_tokens, width + LANES), lambda i, flag: (i, 0)),
+            ]
+            + [pl.BlockSpec(memory_space=pl.ANY)] * len(before),
+            out_specs=pl.BlockSpec((block_tokens, width), here),
+        ),
+        out_shape=jax.ShapeDtypeStruct((tokens, width), jnp.bfloat16),
+        input_output_aliases={4: 0} if before else {},
+        cost_estimate=pl.CostEstimate(
+            flops=4 * part_tokens * width, bytes_accessed=8 * part_tokens * width, transcendentals=0
+        ),
+        name="merge",
+    )(has_guest, mean, lse, sent, *before)
+
+
+def matchings(slots):
+    if len(slots) < 2:
+        return [[]]
+    first, rest = slots[0], slots[1:]
+    found = list(matchings(rest))
+    for other in rest:
+        left = [slot for slot in rest if slot != other]
+        found += [[(first, other)] + more for more in matchings(left)]
+    return found
+
+
+def device_pairs(matching, slot_devices):
+    ways = [way for pair in matching for way in (pair, pair[::-1])]
+    return [
+        (source * slot_devices + inner, target * slot_devices + inner)
+        for source, target in ways
+        for inner in range(slot_devices)
+    ]
+
+
+def few_slots(query_vectors, key_vectors, value_vectors, request_of_slot):
+    device_count = lax.axis_size("view")
+    slot_count = request_of_slot.shape[0]
+    slot_devices = device_count // slot_count
+    token_count = ROWS * COLS
+    width = HEADS * HS
+    chunk_tokens = token_count // CHUNKS
+    query = query_vectors.reshape(token_count, width)
+    key = key_vectors.reshape(token_count, width)
+    value = value_vectors.reshape(token_count, width)
+    query_parts = [
+        lax.slice_in_dim(query, part * chunk_tokens, (part + 1) * chunk_tokens)
+        for part in range(CHUNKS)
+    ]
+    requests = [request_of_slot[slot] for slot in range(slot_count)]
+    every = [matching for matching in matchings(list(range(slot_count))) if matching]
+    branch = jnp.int32(0)
+    for number, matching in enumerate(every):
+        fits = functools.reduce(
+            jnp.logical_and, [requests[one] == requests[other] for one, other in matching]
+        )
+        branch = jnp.where(fits, jnp.int32(number), branch)
+    my_slot = lax.axis_index("view") // slot_devices
+
+    def exchange(matching):
+        pairs = device_pairs(matching, slot_devices)
+        members = [slot for pair in matching for slot in pair]
+
+        def run(key, value, query, *parts):
+            guests = [lax.ppermute(part, "view", pairs) for part in parts]
+            keys = (key, partner(key, "view", 0))
+            values = (value, partner(value, "view", 0))
+            mean, lse = own_attention(query, keys, values)
+            backs = [
+                lax.ppermute(guest_attention(guest, keys, values, part), "view", pairs)
+                for part, guest in enumerate(guests)
+            ]
+            has_guest = functools.reduce(jnp.logical_or, [my_slot == slot for slot in members])
+            has_guest = has_guest.astype(jnp.int32).reshape(1)
+            out = ()
+            for part, back in enumerate(backs):
+                out = (merge(has_guest, mean, lse, back, part, out),)
+            return out[0]
+
+        return run
+
+    attended = lax.switch(branch, [exchange(matching) for matching in every], key, value, query, *query_parts)
+    return attended.reshape(1, ROWS, COLS, HEADS * HS)
+
+
+def shards(query_vectors, key_vectors, value_vectors, request_of_slot):
+    most_views = request_of_slot.shape[0] // 2
+    path = few_slots if most_views == 2 else many_slots
+    return path(query_vectors, key_vectors, value_vectors, request_of_slot)
+
+
 def solution(mesh):
     return jax.shard_map(
         shards,

time: 192 us -> 85.5 us (0.45)
  the two profiles are of different devices: /device:TPU:10 before, /device:TPU:0 now
where the time goes in v1:
time: 85.5 us; the launch traced here: 84.1 us
  Pallas kernels  45.2 us (53%)
  starting transfers between devices  15.3 us (18%)
  waiting for transfers between devices  10.8 us (13%)
  between operations  7.34 us (9%)
  local copies, waits for them, and re-layouts  5.28 us (6%)
    pallas_call x2, Pallas kernels, guest_attention(): pl.pallas_call(guest_kernel, grid=(1,), in_specs=[whole] + [block] * 4, o...  23.2 us
    pallas_call x1, Pallas kernels, own_attention(): pl.pallas_call(own_kernel, grid=(heads // block_heads,), in_specs=[block]...  14.2 us
    ppermute x2, waiting for transfers between devices, run(): guests = [lax.ppermute(part, 'view', pairs) for part in parts]  10.8 us
    ppermute x2, starting transfers between devices, run(): guests = [lax.ppermute(part, 'view', pairs) for part in parts]  7.86 us
    pallas_call x2, Pallas kernels, merge(): pl.pallas_call(merge_kernel, grid_spec=pltpu.PrefetchScalarGridSpec(num_s...  7.77 us
    ppermute x2, starting transfers between devices, run(): lax.ppermute(guest_attention(guest, keys, values, part), 'view', pairs)  6.85 us
    slice x1, local copies, waits for them, and re-layouts, few_slots(): lax.slice_in_dim(query, part * chunk_tokens, (part + 1) * chunk_tokens)  2.06 us
    cond x10, local copies, waits for them, and re-layouts  1.77 us
  transfers between devices with their start and end apart: 6, of which 1 were waited for; matrix products, arithmetic and copies ran while one was open for 2% of the time, Pallas kernels for 49%

profile of v1, /device:TPU:0, one launch (start us, length us, event | category | flops | bytes accessed | tf_op | source)
XLA Modules:
  0.0 84.1 jit_solution(18046597253371825105)
XLA Ops:
  0.0 1.5 %fusion = (s32[1]{0:T(128)}, s32[1]{0:T(128)}, s32[1]{0:T(128)}, s32[1]{0:T(128)}) fusion(s32[4]{0:T(128)} %param.16), kind=kLoop, calls=%fused_computation.18 | loop fusion | bytes 32 | tf_op jit(solution)/shard_map/slice | solution.py:368
  8.8 75.3 %conditional.1 = (bf16[1,16,8,4096]{3,2,1,0:T(8,128)(2,1)}) conditional(s32[]{:T(128)} %clamp.3, (s32[]{:T(128)}, s32[]{:T(128)}, pred[]{:T(512)}, pred[]{:T(512)}, bf16[1,16,8,4096]{3,2,1,0:T(8,128)(2,1)}, /*index=5*/bf16[1,16,8,4096]{3,2,1,0:T(8,128)(2,1)}, bf16[1,16,8,4096]{3,2,1,0:T(8,128)(2,1)}, s32[]{:T(128)}, ...), branch_computations={%region_0.1_spmd, %region_1.2_spmd, %region_2.3_spmd, %region_3.4_... | conditional | flops 807403520 | bytes 55706148 | solution.py:400
  8.8 0.0 copy-start.5
  8.8 0.0 copy-start.14
  8.9 0.6 collective-permute-start.31
  9.4 0.1 collective-permute-start.30
  9.5 2.1 %slice_bitcast_fusion.10 = (bf16[64,4096]{1,0:T(8,128)(2,1)S(1)}, bf16[64,4096]{1,0:T(8,128)(2,1)}) fusion(bf16[1,16,8,4096]{3,2,1,0:T(8,128)(2,1)} %get-tuple-element.508), kind=kLoop, calls=%fused_computation.10 | loop fusion | bytes 2097152 | tf_op jit(solution)/shard_map/slice | solution.py:365
  11.6 5.9 %collective-permute-start.34 = (bf16[64,4096]{1,0:T(8,128)(2,1)S(1)}, bf16[64,4096]{1,0:T(8,128)(2,1)S(1)}, u32[]{:S(2)}, u32[]{:S(2)}) collective-permute-start(bf16[64,4096]{1,0:T(8,128)(2,1)S(1)} %get-tuple-element.540), channel_id=1, source_target_pairs={{0,8},{1,9},{2,10},{3,11},{8,0},{9,1},{10,2},{11,3},{16,24},{17,25... | collective-permute-start | bytes 1572872 | tf_op jit(solution)/shard_map/cond/branch_5_fun/ppermute | solution.py:383
  17.5 1.9 %collective-permute-start.32 = (bf16[64,4096]{1,0:T(8,128)(2,1)}, bf16[64,4096]{1,0:T(8,128)(2,1)}, u32[]{:S(2)}, u32[]{:S(2)}) collective-permute-start(bf16[64,4096]{1,0:T(8,128)(2,1)} %get-tuple-element.541), channel_id=1, source_target_pairs={{0,8},{1,9},{2,10},{3,11},{8,0},{9,1},{10,2},{11,3},{16,24},{17,25... | collective-permute-start | bytes 1572872 | tf_op jit(solution)/shard_map/cond/branch_5_fun/ppermute | solution.py:383
  19.4 10.8 %collective-permute-done.34.query_ref = bf16[64,4096]{1,0:T(8,128)(2,1)S(1)} collective-permute-done((bf16[64,4096]{1,0:T(8,128)(2,1)S(1)}, bf16[64,4096]{1,0:T(8,128)(2,1)S(1)}, u32[]{:S(2)}, u32[]{:S(2)}) %collective-permute-start.34) | collective-permute-done | bytes 524320 | tf_op jit(solution)/shard_map/cond/branch_5_fun/ppermute | solution.py:383
  30.3 0.0 copy-start.41
  30.3 0.0 collective-permute-done.31.second_value
  30.3 0.8 copy-done.41
  31.0 0.0 copy-start.33
  31.0 0.0 collective-permute-done.30.second_key
  31.0 1.0 %copy-done.33 = bf16[128,4096]{1,0:T(8,128)(2,1)} copy-done((bf16[128,4096]{1,0:T(8,128)(2,1)}, bf16[128,4096]{1,0:T(8,128)(2,1)S(1)}, u32[]{:S(2)}) %copy-start.33) | copy-done | bytes 1048600 | tf_op jit(solution)/shard_map/cond
  32.0 0.0 copy-done.5
  32.0 0.0 copy-done.14
  32.0 11.6 %guest_attention.29 = bf16[64,4224]{1,0:T(8,128)(2,1)} custom-call(bf16[64,4096]{1,0:T(8,128)(2,1)} %copy-done.41, bf16[128,4096]{1,0:T(8,128)(2,1)S(1)} %bitcast.108, bf16[128,4096]{1,0:T(8,128)(2,1)} %collective-permute-done.30.second_key, bf16[128,4096]{1,0:T(8,128)(2,1)S(1)} %bitcast.144, bf16[128,4096]{1,0:T(8,128)(2,1)} %copy-done.33), custom_call_target="tpu_custom_call" | custom-call | flops 134217728 | bytes 3145728 | tf_op jit(solution)/shard_map/cond/branch_5_fun/guest_attention/pallas_call | solution.py:277
  43.6 0.0 copy-start.23
  43.6 4.9 %collective-permute-start.35 = (bf16[64,4224]{1,0:T(8,128)(2,1)}, bf16[64,4224]{1,0:T(8,128)(2,1)}, u32[]{:S(2)}, u32[]{:S(2)}) collective-permute-start(bf16[64,4224]{1,0:T(8,128)(2,1)} %guest_attention.29), channel_id=1, source_target_pairs={{0,8},{1,9},{2,10},{3,11},{8,0},{9,1},{10,2},{11,3},{16,24},{17,25... | collective-permute-start | bytes 1622024 | tf_op jit(solution)/shard_map/cond/branch_5_fun/ppermute | solution.py:388
  48.6 0.0 collective-permute-done.32.query_ref
  48.6 11.6 %guest_attention.28 = bf16[64,4224]{1,0:T(8,128)(2,1)} custom-call(bf16[64,4096]{1,0:T(8,128)(2,1)} %collective-permute-done.32.query_ref, bf16[128,4096]{1,0:T(8,128)(2,1)S(1)} %bitcast.109, bf16[128,4096]{1,0:T(8,128)(2,1)} %collective-permute-done.30.second_key, bf16[128,4096]{1,0:T(8,128)(2,1)S(1)} %bitcast.145, bf16[128,4096]{1,0:T(8,128)(2,1)} %copy-done.33), custom_call_target="tpu_custom_call" | custom-call | flops 134217728 | bytes 3145728 | tf_op jit(solution)/shard_map/cond/branch_5_fun/guest_attention/pallas_call | solution.py:277
  60.2 1.9 %collective-permute-start.33 = (bf16[64,4224]{1,0:T(8,128)(2,1)}, bf16[64,4224]{1,0:T(8,128)(2,1)}, u32[]{:S(2)}, u32[]{:S(2)}) collective-permute-start(bf16[64,4224]{1,0:T(8,128)(2,1)} %guest_attention.28), channel_id=1, source_target_pairs={{0,8},{1,9},{2,10},{3,11},{8,0},{9,1},{10,2},{11,3},{16,24},{17,25... | collective-permute-start | bytes 1622024 | tf_op jit(solution)/shard_map/cond/branch_5_fun/ppermute | solution.py:388
  62.1 0.0 copy-done.23
  62.1 14.2 %own_attention.14 = (f32[128,4096]{1,0:T(8,128)}, f32[128,128]{1,0:T(8,128)}) custom-call(bf16[128,4096]{1,0:T(8,128)(2,1)S(1)} %bitcast.164, bf16[128,4096]{1,0:T(8,128)(2,1)S(1)} %bitcast.110, bf16[128,4096]{1,0:T(8,128)(2,1)} %collective-permute-done.30.second_key, bf16[128,4096]{1,0:T(8,128)(2,1)S(1)} %bitcast.146, bf16[128,4096]{1,0:T(8,128)(2,1)} %copy-done.33), custom_call_target="tpu_custom_call" | custom-call | flops 536870912 | bytes 7340032 | tf_op jit(solution)/shard_map/cond/branch_5_fun/own_attention/pallas_call | solution.py:223
  76.4 0.0 collective-permute-done.35.sent_ref
  76.4 3.9 %merge.28.rest_0_ = bf16[128,4096]{1,0:T(8,128)(2,1)} custom-call(s32[1]{0:T(128)} %bitcast.35.has_guest, f32[128,4096]{1,0:T(8,128)} %get-tuple-element.392.mean_ref, f32[128,128]{1,0:T(8,128)} %get-tuple-element.393.lse_ref, bf16[64,4224]{1,0:T(8,128)(2,1)} %collective-permute-done.35.sent_ref), custom_call_target="tpu_custom_call" | custom-call | flops 1048576 | bytes 2097152 | tf_op jit(solution)/shard_map/cond/branch_5_fun/merge/pallas_call | solution.py:312
  80.2 0.0 collective-permute-done.33.sent_ref
  80.2 3.9 %merge.29 = bf16[128,4096]{1,0:T(8,128)(2,1)} custom-call(s32[1]{0:T(128)} %bitcast.35.has_guest, f32[128,4096]{1,0:T(8,128)} %get-tuple-element.392.mean_ref, f32[128,128]{1,0:T(8,128)} %get-tuple-element.393.lse_ref, bf16[64,4224]{1,0:T(8,128)(2,1)} %collective-permute-done.33.sent_ref, ...), custom_call_target="tpu_custom_call", output_to_operand_aliasing={{}: (4, {})} | custom-call | flops 1048576 | bytes 2097152 | tf_op jit(solution)/shard_map/cond/branch_5_fun/merge/pallas_call | solution.py:312
Async XLA Ops:
  8.8 23.2 %copy-start.5 = (bf16[1,16,8,4096]{3,2,1,0:T(8,128)(2,1)S(1)}, bf16[1,16,8,4096]{3,2,1,0:T(8,128)(2,1)}, u32[]{:S(2)}) copy-start(bf16[1,16,8,4096]{3,2,1,0:T(8,128)(2,1)} %get-tuple-element.517) | copy-start | bytes 3145732 | tf_op jit(solution)/shard_map/cond
  8.8 23.2 %copy-start.14 = (bf16[1,16,8,4096]{3,2,1,0:T(8,128)(2,1)S(1)}, bf16[1,16,8,4096]{3,2,1,0:T(8,128)(2,1)}, u32[]{:S(2)}) copy-start(bf16[1,16,8,4096]{3,2,1,0:T(8,128)(2,1)} %get-tuple-element.526) | copy-start | bytes 3145732 | tf_op jit(solution)/shard_map/cond
  8.9 21.4 %collective-permute-start.31 = (bf16[128,4096]{1,0:T(8,128)(2,1)}, bf16[128,4096]{1,0:T(8,128)(2,1)S(1)}, u32[]{:S(2)}, u32[]{:S(2)}) collective-permute-start(bf16[128,4096]{1,0:T(8,128)(2,1)} %bitcast.143), channel_id=1, source_target_pairs={{0,1},{1,0},{2,3},{3,2},{4,5},{5,4},{6,7},{7,6},{8,9},{9,8},{10,11... | collective-permute-start | bytes 3145736 | tf_op jit(solution)/shard_map/cond/branch_5_fun/ppermute | solution.py:20
  9.4 21.6 %collective-permute-start.30 = (bf16[128,4096]{1,0:T(8,128)(2,1)}, bf16[128,4096]{1,0:T(8,128)(2,1)}, u32[]{:S(2)}, u32[]{:S(2)}) collective-permute-start(bf16[128,4096]{1,0:T(8,128)(2,1)} %bitcast.107), channel_id=1, source_target_pairs={{0,1},{1,0},{2,3},{3,2},{4,5},{5,4},{6,7},{7,6},{8,9},{9,8},{10,11... | collective-permute-start | bytes 3145736 | tf_op jit(solution)/shard_map/cond/branch_5_fun/ppermute | solution.py:20
  11.6 18.7 %collective-permute-start.34 = (bf16[64,4096]{1,0:T(8,128)(2,1)S(1)}, bf16[64,4096]{1,0:T(8,128)(2,1)S(1)}, u32[]{:S(2)}, u32[]{:S(2)}) collective-permute-start(bf16[64,4096]{1,0:T(8,128)(2,1)S(1)} %get-tuple-element.540), channel_id=1, source_target_pairs={{0,8},{1,9},{2,10},{3,11},{8,0},{9,1},{10,2},{11,3},{16,24},{17,25... | collective-permute-start | bytes 1572872 | tf_op jit(solution)/shard_map/cond/branch_5_fun/ppermute | solution.py:383
  17.5 31.1 %collective-permute-start.32 = (bf16[64,4096]{1,0:T(8,128)(2,1)}, bf16[64,4096]{1,0:T(8,128)(2,1)}, u32[]{:S(2)}, u32[]{:S(2)}) collective-permute-start(bf16[64,4096]{1,0:T(8,128)(2,1)} %get-tuple-element.541), channel_id=1, source_target_pairs={{0,8},{1,9},{2,10},{3,11},{8,0},{9,1},{10,2},{11,3},{16,24},{17,25... | collective-permute-start | bytes 1572872 | tf_op jit(solution)/shard_map/cond/branch_5_fun/ppermute | solution.py:383
  30.3 0.8 copy-start.41
  31.0 1.0 %copy-start.33 = (bf16[128,4096]{1,0:T(8,128)(2,1)}, bf16[128,4096]{1,0:T(8,128)(2,1)S(1)}, u32[]{:S(2)}) copy-start(bf16[128,4096]{1,0:T(8,128)(2,1)S(1)} %collective-permute-done.31.second_value) | copy-start | bytes 3145732 | tf_op jit(solution)/shard_map/cond
  43.6 18.5 %copy-start.23 = (bf16[1,16,8,4096]{3,2,1,0:T(8,128)(2,1)S(1)}, bf16[1,16,8,4096]{3,2,1,0:T(8,128)(2,1)}, u32[]{:S(2)}) copy-start(bf16[1,16,8,4096]{3,2,1,0:T(8,128)(2,1)} %get-tuple-element.508) | copy-start | bytes 3145732 | tf_op jit(solution)/shard_map/cond
  43.6 32.7 %collective-permute-start.35 = (bf16[64,4224]{1,0:T(8,128)(2,1)}, bf16[64,4224]{1,0:T(8,128)(2,1)}, u32[]{:S(2)}, u32[]{:S(2)}) collective-permute-start(bf16[64,4224]{1,0:T(8,128)(2,1)} %guest_attention.29), channel_id=1, source_target_pairs={{0,8},{1,9},{2,10},{3,11},{8,0},{9,1},{10,2},{11,3},{16,24},{17,25... | collective-permute-start | bytes 1622024 | tf_op jit(solution)/shard_map/cond/branch_5_fun/ppermute | solution.py:388
  60.2 20.1 %collective-permute-start.33 = (bf16[64,4224]{1,0:T(8,128)(2,1)}, bf16[64,4224]{1,0:T(8,128)(2,1)}, u32[]{:S(2)}, u32[]{:S(2)}) collective-permute-start(bf16[64,4224]{1,0:T(8,128)(2,1)} %guest_attention.28), channel_id=1, source_target_pairs={{0,8},{1,9},{2,10},{3,11},{8,0},{9,1},{10,2},{11,3},{16,24},{17,25... | collective-permute-start | bytes 1622024 | tf_op jit(solution)/shard_map/cond/branch_5_fun/ppermute | solution.py:388

commit v2 on v1

--- a/solution.py
+++ b/solution.py
@@ -181,54 +181,70 @@
 LANES = 128
 PIECES = 3
 CHUNKS = 2
+GROUP = 8
 
 
 def scores_of(query, keys):
     return lax.dot_general(query, keys, (((1,), (1,)), ((), ())), preferred_element_type=jnp.float32)
 
 
+def lanes_of(head):
+    return pl.ds(pl.multiple_of(head * HS, HS), HS)
+
+
+def partial_softmax(heads, query_ref, key_refs, value_refs, allowed):
+    scores = []
+    for head in heads:
+        at = lanes_of(head)
+        keys = jnp.concatenate([ref[:, at] for ref in key_refs], axis=0)
+        scores.append(scores_of(query_ref[:, at], keys))
+    if allowed is not None:
+        scores = [jnp.where(allowed, score, NEG_FILL) for score in scores]
+    peaks = [jnp.max(score, axis=1, keepdims=True) for score in scores]
+    weights = [
+        jnp.exp((score - peak) * SCALING).astype(jnp.bfloat16)
+        for score, peak in zip(scores, peaks)
+    ]
+    results = []
+    for head, peak, weight in zip(heads, peaks, weights):
+        at = lanes_of(head)
+        values = jnp.concatenate([ref[:, at] for ref in value_refs], axis=0)
+        ones = jnp.ones_like(values)
+        both = jnp.dot(
+            weight, jnp.concatenate([values, ones], axis=1), preferred_element_type=jnp.float32
+        )
+        total = both[:, HS:]
+        results.append((both[:, :HS] / total, peak * SCALING + jnp.log(total)))
+    return results
+
+
 def own_kernel(query_ref, first_key, second_key, first_value, second_value, mean_ref, lse_ref):
-    step = pl.program_id(0)
-    block_heads = query_ref.shape[1] // HS
+    heads = query_ref.shape[1] // HS
     lane = lax.broadcasted_iota(jnp.int32, lse_ref.shape, 1)
 
-    @pl.when(step == 0)
-    def _():
-        lse_ref[...] = jnp.zeros_like(lse_ref)
-
-    found = lse_ref[...]
-    for head in range(block_heads):
-        at = slice(head * HS, (head + 1) * HS)
-        first = scores_of(query_ref[:, at], first_key[:, at])
-        second = scores_of(query_ref[:, at], second_key[:, at])
-        peak = jnp.max(jnp.maximum(first, second), axis=1, keepdims=True)
-        first = jnp.exp((first - peak) * SCALING)
-        second = jnp.exp((second - peak) * SCALING)
-        total = jnp.sum(first + second, axis=1, keepdims=True)
-        summed = jnp.dot(
-            first.astype(jnp.bfloat16), first_value[:, at], preferred_element_type=jnp.float32
-        ) + jnp.dot(
-            second.astype(jnp.bfloat16), second_value[:, at], preferred_element_type=jnp.float32
-        )
-        mean_ref[:, at] = summed / total
-        lse = peak * SCALING + jnp.log(total)
-        found = jnp.where(lane == step * block_heads + head, lse, found)
-    lse_ref[...] = found
-
-
-def own_attention(query, keys, values, block_heads=2):
+    def one_group(group, found):
+        numbers = [group * GROUP + inner for inner in range(GROUP)]
+        results = partial_softmax(
+            numbers, query_ref, (first_key, second_key), (first_value, second_value), None
+        )
+        for head, (mean, lse) in zip(numbers, results):
+            mean_ref[:, lanes_of(head)] = mean
+            found = jnp.where(lane == head, lse, found)
+        return found
+
+    zeros = jnp.zeros(lse_ref.shape, jnp.float32)
+    lse_ref[...] = lax.fori_loop(0, heads // GROUP, one_group, zeros)
+
+
+def own_attention(query, keys, values):
     tokens, width = query.shape
-    heads = width // HS
-    block = pl.BlockSpec((tokens, block_heads * HS), lambda i: (0, i))
     return pl.pallas_call(
         own_kernel,
-        grid=(heads // block_heads,),
-        in_specs=[block] * 5,
-        out_specs=[block, pl.BlockSpec((tokens, LANES), lambda i: (0, 0))],
         out_shape=[
             jax.ShapeDtypeStruct((tokens, width), jnp.float32),
             jax.ShapeDtypeStruct((tokens, LANES), jnp.float32),
         ],
+        compiler_params=pltpu.CompilerParams(vmem_limit_bytes=24 * 2**20),
         cost_estimate=pl.CostEstimate(
             flops=8 * tokens * tokens * width, bytes_accessed=14 * tokens * width, transcendentals=0
         ),
@@ -236,60 +252,55 @@
     )(query, *keys, *values)
 
 
-def guest_kernel(query_ref, first_key, second_key, first_value, second_value, sent_ref):
+def guest_kernel(query_ref, first_key, second_key, first_value, second_value, _, sent_ref):
     tokens, width = query_ref.shape
-    query_row = lax.broadcasted_iota(jnp.int32, (tokens, tokens), 0) // COLS
-    key_row = lax.broadcasted_iota(jnp.int32, (tokens, tokens), 1) // COLS
+    shape = (tokens, 2 * tokens)
+    query_row = lax.broadcasted_iota(jnp.int32, shape, 0) // COLS
+    key_row = lax.broadcasted_iota(jnp.int32, shape, 1) % tokens // COLS
     same_row = query_row == key_row
     lane = lax.broadcasted_iota(jnp.int32, (tokens, LANES), 1)
     heads = width // HS
 
-    def one_head(head, found):
-        at = pl.ds(pl.multiple_of(head * HS, HS), HS)
-        query = query_ref[:, at]
-        first = jnp.where(same_row, scores_of(query, first_key[:, at]), NEG_FILL)
-        second = jnp.where(same_row, scores_of(query, second_key[:, at]), NEG_FILL)
-        peak = jnp.max(jnp.maximum(first, second), axis=1, keepdims=True)
-        first = jnp.exp((first - peak) * SCALING)
-        second = jnp.exp((second - peak) * SCALING)
-        total = jnp.sum(first + second, axis=1, keepdims=True)
-        summed = jnp.dot(
-            first.astype(jnp.bfloat16), first_value[:, at], preferred_element_type=jnp.float32
-        ) + jnp.dot(
-            second.astype(jnp.bfloat16), second_value[:, at], preferred_element_type=jnp.float32
-        )
-        sent_ref[:, at] = (summed / total).astype(jnp.bfloat16)
-        left = peak * SCALING + jnp.log(total)
-        for piece in range(PIECES):
-            part = left.astype(jnp.bfloat16).astype(jnp.float32)
-            left = left - part
-            found = jnp.where(lane == piece * heads + head, part, found)
+    def one_group(group, found):
+        numbers = [group * GROUP + inner for inner in range(GROUP)]
+        results = partial_softmax(
+            numbers, query_ref, (first_key, second_key), (first_value, second_value), same_row
+        )
+        for head, (mean, lse) in zip(numbers, results):
+            sent_ref[:, lanes_of(head)] = mean.astype(jnp.bfloat16)
+            found = jnp.where(lane % heads == head, lse, found)
         return found
 
-    found = lax.fori_loop(0, heads, one_head, jnp.zeros((tokens, LANES), jnp.float32), unroll=2)
-    sent_ref[:, width:] = found.astype(jnp.bfloat16)
-
-
-def guest_attention(query, keys, values, chunk):
+    left = lax.fori_loop(0, heads // GROUP, one_group, jnp.zeros((tokens, LANES), jnp.float32))
+    packed = jnp.zeros((tokens, LANES), jnp.bfloat16)
+    for piece in range(PIECES):
+        part = left.astype(jnp.bfloat16)
+        left = left - part.astype(jnp.float32)
+        packed = jnp.where(lane // heads == piece, part.astype(jnp.float32), packed.astype(jnp.float32)).astype(jnp.bfloat16)
+    sent_ref[:, width:] = packed
+
+
+def guest_attention(query, keys, values, chunk, after):
     tokens, width = query.shape
     whole = pl.BlockSpec((tokens, width), lambda i: (0, 0))
     block = pl.BlockSpec((tokens, width), lambda i: (chunk, 0))
     return pl.pallas_call(
         guest_kernel,
         grid=(1,),
-        in_specs=[whole] + [block] * 4,
+        in_specs=[whole] + [block] * 4 + [pl.BlockSpec(memory_space=pl.ANY)],
         out_specs=pl.BlockSpec((tokens, width + LANES), lambda i: (0, 0)),
         out_shape=jax.ShapeDtypeStruct((tokens, width + LANES), jnp.bfloat16),
+        compiler_params=pltpu.CompilerParams(vmem_limit_bytes=24 * 2**20),
         cost_estimate=pl.CostEstimate(
             flops=8 * tokens * tokens * width, bytes_accessed=12 * tokens * width, transcendentals=0
         ),
         name="guest_attention",
-    )(query, *keys, *values)
+    )(query, *keys, *values, after)
 
 
 def merge_kernel(has_guest, mean_ref, lse_ref, sent_ref, *rest):
     out_ref = rest[-1]
-    width = mean_ref.shape[1]
+    tokens, width = mean_ref.shape
     heads = width // HS
     pieces = sent_ref[:, width:].astype(jnp.float32)
     lse = pieces
@@ -297,33 +308,38 @@
         lse = lse + pltpu.roll(pieces, LANES - piece * heads, 1)
     lse = jnp.where(has_guest[0] > 0, lse, NEG_FILL)
     share = 1.0 / (1.0 + jnp.exp(lse_ref[...] - lse))
-    for head in range(heads):
-        at = slice(head * HS, (head + 1) * HS)
-        own = mean_ref[:, at]
-        guest = sent_ref[:, at].astype(jnp.float32)
-        out_ref[:, at] = (own + share[:, head : head + 1] * (guest - own)).astype(jnp.bfloat16)
-
-
-def merge(has_guest, mean, lse, sent, chunk, before, steps=4):
+
+    def one_group(group, share):
+        for inner in range(GROUP):
+            at = lanes_of(group * GROUP + inner)
+            own = mean_ref[:, at]
+            guest = sent_ref[:, at].astype(jnp.float32)
+            out_ref[:, at] = (own + share[:, inner : inner + 1] * (guest - own)).astype(jnp.bfloat16)
+        return pltpu.roll(share, LANES - GROUP, 1)
+
+    lax.fori_loop(0, heads // GROUP, one_group, share)
+
+
+def merge(has_guest, mean, lse, sent, chunk, before):
     tokens, width = mean.shape
     part_tokens = sent.shape[0]
-    block_tokens = part_tokens // steps
-    here = lambda i, flag: (chunk * steps + i, 0)
+    here = lambda i, flag: (chunk, 0)
     return pl.pallas_call(
         merge_kernel,
         grid_spec=pltpu.PrefetchScalarGridSpec(
             num_scalar_prefetch=1,
-            grid=(steps,),
+            grid=(1,),
             in_specs=[
-                pl.BlockSpec((block_tokens, width), here),
-                pl.BlockSpec((block_tokens, LANES), here),
-                pl.BlockSpec((block_tokens, width + LANES), lambda i, flag: (i, 0)),
+                pl.BlockSpec((part_tokens, width), here),
+                pl.BlockSpec((part_tokens, LANES), here),
+                pl.BlockSpec((part_tokens, width + LANES), lambda i, flag: (0, 0)),
             ]
             + [pl.BlockSpec(memory_space=pl.ANY)] * len(before),
-            out_specs=pl.BlockSpec((block_tokens, width), here),
+            out_specs=pl.BlockSpec((part_tokens, width), here),
         ),
         out_shape=jax.ShapeDtypeStruct((tokens, width), jnp.bfloat16),
         input_output_aliases={4: 0} if before else {},
+        compiler_params=pltpu.CompilerParams(vmem_limit_bytes=16 * 2**20),
         cost_estimate=pl.CostEstimate(
             flops=4 * part_tokens * width, bytes_accessed=8 * part_tokens * width, transcendentals=0
         ),
@@ -349,6 +365,25 @@
         for source, target in ways
         for inner in range(slot_devices)
     ]
+
+
+def which_matching(request_of_slot, every):
+    def kernel(request_ref, number_ref):
+        chosen = jnp.int32(0)
+        for number, matching in enumerate(every):
+            fits = functools.reduce(
+                jnp.logical_and, [request_ref[one] == request_ref[other] for one, other in matching]
+            )
+            chosen = jnp.where(fits, jnp.int32(number), chosen)
+        number_ref[0] = chosen
+
+    return pl.pallas_call(
+        kernel,
+        in_specs=[pl.BlockSpec(memory_space=pltpu.SMEM)],
+        out_specs=pl.BlockSpec(memory_space=pltpu.SMEM),
+        out_shape=jax.ShapeDtypeStruct((1,), jnp.int32),
+        name="which_matching",
+    )(request_of_slot)[0]
 
 
 def few_slots(query_vectors, key_vectors, value_vectors, request_of_slot):
@@ -361,31 +396,25 @@
     query = query_vectors.reshape(token_count, width)
     key = key_vectors.reshape(token_count, width)
     value = value_vectors.reshape(token_count, width)
-    query_parts = [
-        lax.slice_in_dim(query, part * chunk_tokens, (part + 1) * chunk_tokens)
-        for part in range(CHUNKS)
-    ]
-    requests = [request_of_slot[slot] for slot in range(slot_count)]
     every = [matching for matching in matchings(list(range(slot_count))) if matching]
-    branch = jnp.int32(0)
-    for number, matching in enumerate(every):
-        fits = functools.reduce(
-            jnp.logical_and, [requests[one] == requests[other] for one, other in matching]
-        )
-        branch = jnp.where(fits, jnp.int32(number), branch)
+    branch = which_matching(request_of_slot, every)
     my_slot = lax.axis_index("view") // slot_devices
 
     def exchange(matching):
         pairs = device_pairs(matching, slot_devices)
         members = [slot for pair in matching for slot in pair]
 
-        def run(key, value, query, *parts):
-            guests = [lax.ppermute(part, "view", pairs) for part in parts]
+        def run(key, value, query):
+            guests, source = [], query
+            for part in range(CHUNKS):
+                sent = lax.slice_in_dim(source, part * chunk_tokens, (part + 1) * chunk_tokens)
+                source, sent = lax.optimization_barrier((source, sent))
+                guests.append(lax.ppermute(sent, "view", pairs))
             keys = (key, partner(key, "view", 0))
             values = (value, partner(value, "view", 0))
             mean, lse = own_attention(query, keys, values)
             backs = [
-                lax.ppermute(guest_attention(guest, keys, values, part), "view", pairs)
+                lax.ppermute(guest_attention(guest, keys, values, part, lse), "view", pairs)
                 for part, guest in enumerate(guests)
             ]
             has_guest = functools.reduce(jnp.logical_or, [my_slot == slot for slot in members])
@@ -397,7 +426,7 @@
 
         return run
 
-    attended = lax.switch(branch, [exchange(matching) for matching in every], key, value, query, *query_parts)
+    attended = lax.switch(branch, [exchange(matching) for matching in every], key, value, query)
     return attended.reshape(1, ROWS, COLS, HEADS * HS)
 
 

time: 85.5 us -> 57.3 us (0.67)
  the two profiles are of different devices: /device:TPU:0 before, /device:TPU:10 now
where the time goes in v2:
time: 57.3 us; the launch traced here: 56.2 us
  waiting for transfers between devices  22.7 us (40%)
  starting transfers between devices  16.3 us (28%)
  Pallas kernels  14.1 us (25%)
  local copies, waits for them, and re-layouts  2.2 us (4%)
  between operations  0.66 us (1%)
    ppermute x2, waiting for transfers between devices, run(): lax.ppermute(guest_attention(guest, keys, values, part, lse), 'view', pairs)  13.2 us
    ppermute x2, waiting for transfers between devices, run(): guests.append(lax.ppermute(sent, 'view', pairs))  9.51 us
    ppermute x2, starting transfers between devices, run(): lax.ppermute(guest_attention(guest, keys, values, part, lse), 'view', pairs)  8.97 us
    ppermute x2, starting transfers between devices, run(): guests.append(lax.ppermute(sent, 'view', pairs))  6.74 us
    pallas_call x2, Pallas kernels, guest_attention(): pl.pallas_call(guest_kernel, grid=(1,), in_specs=[whole] + [block] * 4 +...  6.03 us
    pallas_call x1, Pallas kernels, own_attention(): pl.pallas_call(own_kernel, out_shape=[jax.ShapeDtypeStruct((tokens, width...  3.92 us
    pallas_call x2, Pallas kernels, merge(): pl.pallas_call(merge_kernel, grid_spec=pltpu.PrefetchScalarGridSpec(num_s...  2.99 us
    slice x2, local copies, waits for them, and re-layouts, run(): lax.slice_in_dim(source, part * chunk_tokens, (part + 1) * chunk_tokens)  2.19 us
  transfers between devices with their start and end apart: 6, of which 4 were waited for; matrix products, arithmetic and copies ran while one was open for 4% of the time, Pallas kernels for 20%

profile of v2, /device:TPU:10, one launch (start us, length us, event | category | flops | bytes accessed | tf_op | source)
XLA Modules:
  0.0 56.2 jit_solution(1696539874083752666)
XLA Ops:
  0.0 1.2 %which_matching.1 = s32[1]{0:T(128)} custom-call(s32[4]{0:T(128)} %request_ref.1), custom_call_target="tpu_custom_call" | custom-call | tf_op jit(solution)/shard_map/which_matching/pallas_call | solution.py:380
  1.8 54.3 %conditional.1 = (bf16[1,16,8,4096]{3,2,1,0:T(8,128)(2,1)}) conditional(s32[]{:T(128)} %bitcast.54, (s32[]{:T(128)}, s32[]{:T(128)}, pred[]{:T(512)}, pred[]{:T(512)}, bf16[1,16,8,4096]{3,2,1,0:T(8,128)(2,1)}, /*index=5*/bf16[1,16,8,4096]{3,2,1,0:T(8,128)(2,1)}, bf16[1,16,8,4096]{3,2,1,0:T(8,128)(2,1)}, (), ...), branch_computations={%region_0.1_spmd, %region_1.2_spmd, %region_2.3_spmd, %region_3.4_... | conditional | flops 807403520 | bytes 45220312 | solution.py:429
  1.9 0.0 copy-start.2
  1.9 0.0 copy-start.11
  1.9 0.1 collective-permute-start.12
  2.0 0.5 collective-permute-start.13
  2.5 1.1 %slice_bitcast_fusion.2 = bf16[64,4096]{1,0:T(8,128)(2,1)S(1)} fusion(bf16[1,16,8,4096]{3,2,1,0:T(8,128)(2,1)} %get-tuple-element.478), kind=kLoop, calls=%fused_computation.2 | loop fusion | bytes 1048576 | tf_op jit(solution)/shard_map/cond/branch_2_fun/slice | solution.py:410
  3.6 4.5 %collective-permute-start.16 = (bf16[64,4096]{1,0:T(8,128)(2,1)S(1)}, bf16[64,4096]{1,0:T(8,128)(2,1)S(1)}, u32[]{:S(2)}, u32[]{:S(2)}) collective-permute-start(bf16[64,4096]{1,0:T(8,128)(2,1)S(1)} %slice_bitcast_fusion.2), channel_id=1, source_target_pairs={{4,12},{5,13},{6,14},{7,15},{12,4},{13,5},{14,6},{15,7},{20,28},{2... | collective-permute-start | bytes 1572872 | tf_op jit(solution)/shard_map/cond/branch_2_fun/ppermute | solution.py:412
  8.1 1.1 %slice.62 = bf16[64,4096]{1,0:T(8,128)(2,1)S(1)} slice(bf16[128,4096]{1,0:T(8,128)(2,1)} %bitcast.140), slice={[64:128], [0:4096]} | slice | bytes 1048576 | tf_op jit(solution)/shard_map/cond/branch_2_fun/slice | solution.py:410
  9.2 2.2 %collective-permute-start.14 = (bf16[64,4096]{1,0:T(8,128)(2,1)S(1)}, bf16[64,4096]{1,0:T(8,128)(2,1)S(1)}, u32[]{:S(2)}, u32[]{:S(2)}) collective-permute-start(bf16[64,4096]{1,0:T(8,128)(2,1)S(1)} %slice.62), channel_id=1, source_target_pairs={{4,12},{5,13},{6,14},{7,15},{12,4},{13,5},{14,6},{15,7},{20,28},{2... | collective-permute-start | bytes 1572872 | tf_op jit(solution)/shard_map/cond/branch_2_fun/ppermute | solution.py:412
  11.4 0.0 collective-permute-done.12.second_key
  11.4 0.0 collective-permute-done.13.second_value
  11.4 0.0 copy-done.2
  11.5 0.0 copy-done.11
  11.5 3.9 %own_attention.11 = (f32[128,4096]{1,0:T(8,128)S(1)}, f32[128,128]{1,0:T(8,128)S(1)}) custom-call(bf16[128,4096]{1,0:T(8,128)(2,1)} %bitcast.141, bf16[128,4096]{1,0:T(8,128)(2,1)S(1)} %bitcast.73, bf16[128,4096]{1,0:T(8,128)(2,1)S(1)} %collective-permute-done.12.second_key, bf16[128,4096]{1,0:T(8,128)(2,1)S(1)} %bitcast.109, ...), custom_call_target="tpu_custom_call" | custom-call | flops 536870912 | bytes 7340032 | tf_op jit(solution)/shard_map/cond/branch_2_fun/own_attention/pallas_call | solution.py:241
  15.4 5.8 %collective-permute-done.16.query_ref = bf16[64,4096]{1,0:T(8,128)(2,1)S(1)} collective-permute-done((bf16[64,4096]{1,0:T(8,128)(2,1)S(1)}, bf16[64,4096]{1,0:T(8,128)(2,1)S(1)}, u32[]{:S(2)}, u32[]{:S(2)}) %collective-permute-start.16) | collective-permute-done | bytes 524320 | tf_op jit(solution)/shard_map/cond/branch_2_fun/ppermute | solution.py:412
  21.2 3.0 %guest_attention.23 = bf16[64,4224]{1,0:T(8,128)(2,1)} custom-call(bf16[64,4096]{1,0:T(8,128)(2,1)S(1)} %collective-permute-done.16.query_ref, bf16[128,4096]{1,0:T(8,128)(2,1)S(1)} %bitcast.74, bf16[128,4096]{1,0:T(8,128)(2,1)S(1)} %collective-permute-done.12.second_key, bf16[128,4096]{1,0:T(8,128)(2,1)S(1)} %bitcast.110, ...), custom_call_target="tpu_custom_call" | custom-call | flops 134217728 | bytes 3145728 | tf_op jit(solution)/shard_map/cond/branch_2_fun/guest_attention/pallas_call | solution.py:287
  24.2 4.5 %collective-permute-start.17 = (bf16[64,4224]{1,0:T(8,128)(2,1)}, bf16[64,4224]{1,0:T(8,128)(2,1)S(1)}, u32[]{:S(2)}, u32[]{:S(2)}) collective-permute-start(bf16[64,4224]{1,0:T(8,128)(2,1)} %guest_attention.23), channel_id=1, source_target_pairs={{4,12},{5,13},{6,14},{7,15},{12,4},{13,5},{14,6},{15,7},{20,28},{2... | collective-permute-start | bytes 1622024 | tf_op jit(solution)/shard_map/cond/branch_2_fun/ppermute | solution.py:417
  28.7 3.7 %collective-permute-done.14.query_ref = bf16[64,4096]{1,0:T(8,128)(2,1)S(1)} collective-permute-done((bf16[64,4096]{1,0:T(8,128)(2,1)S(1)}, bf16[64,4096]{1,0:T(8,128)(2,1)S(1)}, u32[]{:S(2)}, u32[]{:S(2)}) %collective-permute-start.14) | collective-permute-done | bytes 524320 | tf_op jit(solution)/shard_map/cond/branch_2_fun/ppermute | solution.py:412
  32.4 3.0 %guest_attention.22 = bf16[64,4224]{1,0:T(8,128)(2,1)} custom-call(bf16[64,4096]{1,0:T(8,128)(2,1)S(1)} %collective-permute-done.14.query_ref, bf16[128,4096]{1,0:T(8,128)(2,1)S(1)} %bitcast.75, bf16[128,4096]{1,0:T(8,128)(2,1)S(1)} %collective-permute-done.12.second_key, bf16[128,4096]{1,0:T(8,128)(2,1)S(1)} %bitcast.111, ...), custom_call_target="tpu_custom_call" | custom-call | flops 134217728 | bytes 3145728 | tf_op jit(solution)/shard_map/cond/branch_2_fun/guest_attention/pallas_call | solution.py:287
  35.4 4.5 %collective-permute-start.15 = (bf16[64,4224]{1,0:T(8,128)(2,1)}, bf16[64,4224]{1,0:T(8,128)(2,1)S(1)}, u32[]{:S(2)}, u32[]{:S(2)}) collective-permute-start(bf16[64,4224]{1,0:T(8,128)(2,1)} %guest_attention.22), channel_id=1, source_target_pairs={{4,12},{5,13},{6,14},{7,15},{12,4},{13,5},{14,6},{15,7},{20,28},{2... | collective-permute-start | bytes 1622024 | tf_op jit(solution)/shard_map/cond/branch_2_fun/ppermute | solution.py:417
  40.0 4.0 %collective-permute-done.17.sent_ref = bf16[64,4224]{1,0:T(8,128)(2,1)S(1)} collective-permute-done((bf16[64,4224]{1,0:T(8,128)(2,1)}, bf16[64,4224]{1,0:T(8,128)(2,1)S(1)}, u32[]{:S(2)}, u32[]{:S(2)}) %collective-permute-start.17) | collective-permute-done | bytes 540704 | tf_op jit(solution)/shard_map/cond/branch_2_fun/ppermute | solution.py:417
  44.0 1.5 %merge.22.rest_0_ = bf16[128,4096]{1,0:T(8,128)(2,1)} custom-call(s32[1]{0:T(128)} %bitcast.12.has_guest, f32[128,4096]{1,0:T(8,128)S(1)} %get-tuple-element.317.mean_ref, f32[128,128]{1,0:T(8,128)S(1)} %get-tuple-element.318._.lse_ref, bf16[64,4224]{1,0:T(8,128)(2,1)S(1)} %collective-permute-done.17.sent_ref), custom_call_target="tpu_custom_call" | custom-call | flops 1048576 | bytes 2097152 | tf_op jit(solution)/shard_map/cond/branch_2_fun/merge/pallas_call | solution.py:327
  45.5 9.2 %collective-permute-done.15.sent_ref = bf16[64,4224]{1,0:T(8,128)(2,1)S(1)} collective-permute-done((bf16[64,4224]{1,0:T(8,128)(2,1)}, bf16[64,4224]{1,0:T(8,128)(2,1)S(1)}, u32[]{:S(2)}, u32[]{:S(2)}) %collective-permute-start.15) | collective-permute-done | bytes 540704 | tf_op jit(solution)/shard_map/cond/branch_2_fun/ppermute | solution.py:417
  54.7 1.5 %merge.23 = bf16[128,4096]{1,0:T(8,128)(2,1)} custom-call(s32[1]{0:T(128)} %bitcast.12.has_guest, f32[128,4096]{1,0:T(8,128)S(1)} %get-tuple-element.317.mean_ref, f32[128,128]{1,0:T(8,128)S(1)} %get-tuple-element.318._.lse_ref, bf16[64,4224]{1,0:T(8,128)(2,1)S(1)} %collective-permute-done.15.sent_ref, ...), custom_call_target="tpu_custom_call", output_to_operand_aliasing={{}: (4, {})} | custom-call | flops 1048576 | bytes 2097152 | tf_op jit(solution)/shard_map/cond/branch_2_fun/merge/pallas_call | solution.py:327
Async XLA Ops:
  1.9 9.6 %copy-start.2 = (bf16[1,16,8,4096]{3,2,1,0:T(8,128)(2,1)S(1)}, bf16[1,16,8,4096]{3,2,1,0:T(8,128)(2,1)}, u32[]{:S(2)}) copy-start(bf16[1,16,8,4096]{3,2,1,0:T(8,128)(2,1)} %get-tuple-element.487) | copy-start | bytes 3145732 | tf_op jit(solution)/shard_map/cond
  1.9 9.6 %copy-start.11 = (bf16[1,16,8,4096]{3,2,1,0:T(8,128)(2,1)S(1)}, bf16[1,16,8,4096]{3,2,1,0:T(8,128)(2,1)}, u32[]{:S(2)}) copy-start(bf16[1,16,8,4096]{3,2,1,0:T(8,128)(2,1)} %get-tuple-element.496) | copy-start | bytes 3145732 | tf_op jit(solution)/shard_map/cond
  1.9 9.5 %collective-permute-start.12 = (bf16[128,4096]{1,0:T(8,128)(2,1)}, bf16[128,4096]{1,0:T(8,128)(2,1)S(1)}, u32[]{:S(2)}, u32[]{:S(2)}) collective-permute-start(bf16[128,4096]{1,0:T(8,128)(2,1)} %bitcast.72), channel_id=1, source_target_pairs={{0,1},{1,0},{2,3},{3,2},{4,5},{5,4},{6,7},{7,6},{8,9},{9,8},{10,11... | collective-permute-start | bytes 3145736 | tf_op jit(solution)/shard_map/cond/branch_2_fun/ppermute | solution.py:20
  2.0 9.5 %collective-permute-start.13 = (bf16[128,4096]{1,0:T(8,128)(2,1)}, bf16[128,4096]{1,0:T(8,128)(2,1)S(1)}, u32[]{:S(2)}, u32[]{:S(2)}) collective-permute-start(bf16[128,4096]{1,0:T(8,128)(2,1)} %bitcast.108), channel_id=1, source_target_pairs={{0,1},{1,0},{2,3},{3,2},{4,5},{5,4},{6,7},{7,6},{8,9},{9,8},{10,11... | collective-permute-start | bytes 3145736 | tf_op jit(solution)/shard_map/cond/branch_2_fun/ppermute | solution.py:20
  3.6 17.6 %collective-permute-start.16 = (bf16[64,4096]{1,0:T(8,128)(2,1)S(1)}, bf16[64,4096]{1,0:T(8,128)(2,1)S(1)}, u32[]{:S(2)}, u32[]{:S(2)}) collective-permute-start(bf16[64,4096]{1,0:T(8,128)(2,1)S(1)} %slice_bitcast_fusion.2), channel_id=1, source_target_pairs={{4,12},{5,13},{6,14},{7,15},{12,4},{13,5},{14,6},{15,7},{20,28},{2... | collective-permute-start | bytes 1572872 | tf_op jit(solution)/shard_map/cond/branch_2_fun/ppermute | solution.py:412
  9.2 23.2 %collective-permute-start.14 = (bf16[64,4096]{1,0:T(8,128)(2,1)S(1)}, bf16[64,4096]{1,0:T(8,128)(2,1)S(1)}, u32[]{:S(2)}, u32[]{:S(2)}) collective-permute-start(bf16[64,4096]{1,0:T(8,128)(2,1)S(1)} %slice.62), channel_id=1, source_target_pairs={{4,12},{5,13},{6,14},{7,15},{12,4},{13,5},{14,6},{15,7},{20,28},{2... | collective-permute-start | bytes 1572872 | tf_op jit(solution)/shard_map/cond/branch_2_fun/ppermute | solution.py:412
  24.2 19.8 %collective-permute-start.17 = (bf16[64,4224]{1,0:T(8,128)(2,1)}, bf16[64,4224]{1,0:T(8,128)(2,1)S(1)}, u32[]{:S(2)}, u32[]{:S(2)}) collective-permute-start(bf16[64,4224]{1,0:T(8,128)(2,1)} %guest_attention.23), channel_id=1, source_target_pairs={{4,12},{5,13},{6,14},{7,15},{12,4},{13,5},{14,6},{15,7},{20,28},{2... | collective-permute-start | bytes 1622024 | tf_op jit(solution)/shard_map/cond/branch_2_fun/ppermute | solution.py:417
  35.4 19.2 %collective-permute-start.15 = (bf16[64,4224]{1,0:T(8,128)(2,1)}, bf16[64,4224]{1,0:T(8,128)(2,1)S(1)}, u32[]{:S(2)}, u32[]{:S(2)}) collective-permute-start(bf16[64,4224]{1,0:T(8,128)(2,1)} %guest_attention.22), channel_id=1, source_target_pairs={{4,12},{5,13},{6,14},{7,15},{12,4},{13,5},{14,6},{15,7},{20,28},{2... | collective-permute-start | bytes 1622024 | tf_op jit(solution)/shard_map/cond/branch_2_fun/ppermute | solution.py:417

commit v3 on v2

--- a/solution.py
+++ b/solution.py
@@ -6,6 +6,7 @@
 from jax.experimental import pallas as pl
 from jax.experimental.pallas import tpu as pltpu
 from jax.sharding import PartitionSpec as P
+
 
 HEADS = 32
 HS = 128
@@ -180,8 +181,11 @@
 SCALING = HS ** (-0.5)
 LANES = 128
 PIECES = 3
-CHUNKS = 2
 GROUP = 8
+QUERY_ROWS = (8, 8)
+RETURN_ROWS = ((8,), (6, 2))
+IN_VMEM = pl.BlockSpec(memory_space=pltpu.VMEM)
+IN_PLACE = pl.BlockSpec(memory_space=pl.ANY)
 
 
 def scores_of(query, keys):
@@ -192,11 +196,11 @@
     return pl.ds(pl.multiple_of(head * HS, HS), HS)
 
 
-def partial_softmax(heads, query_ref, key_refs, value_refs, allowed):
+def partial_softmax(heads, query_ref, key_refs, value_refs, rows, allowed):
     scores = []
     for head in heads:
         at = lanes_of(head)
-        keys = jnp.concatenate([ref[:, at] for ref in key_refs], axis=0)
+        keys = jnp.concatenate([ref[rows, at] for ref in key_refs], axis=0)
         scores.append(scores_of(query_ref[:, at], keys))
     if allowed is not None:
         scores = [jnp.where(allowed, score, NEG_FILL) for score in scores]
@@ -208,7 +212,7 @@
     results = []
     for head, peak, weight in zip(heads, peaks, weights):
         at = lanes_of(head)
-        values = jnp.concatenate([ref[:, at] for ref in value_refs], axis=0)
+        values = jnp.concatenate([ref[rows, at] for ref in value_refs], axis=0)
         ones = jnp.ones_like(values)
         both = jnp.dot(
             weight, jnp.concatenate([values, ones], axis=1), preferred_element_type=jnp.float32
@@ -225,7 +229,7 @@
     def one_group(group, found):
         numbers = [group * GROUP + inner for inner in range(GROUP)]
         results = partial_softmax(
-            numbers, query_ref, (first_key, second_key), (first_value, second_value), None
+            numbers, query_ref, (first_key, second_key), (first_value, second_value), slice(None), None
         )
         for head, (mean, lse) in zip(numbers, results):
             mean_ref[:, lanes_of(head)] = mean
@@ -252,8 +256,9 @@
     )(query, *keys, *values)
 
 
-def guest_kernel(query_ref, first_key, second_key, first_value, second_value, _, sent_ref):
+def guest_kernel(start, query_ref, first_key, second_key, first_value, second_value, _, *sent_refs):
     tokens, width = query_ref.shape
+    rows = slice(start, start + tokens)
     shape = (tokens, 2 * tokens)
     query_row = lax.broadcasted_iota(jnp.int32, shape, 0) // COLS
     key_row = lax.broadcasted_iota(jnp.int32, shape, 1) % tokens // COLS
@@ -261,35 +266,40 @@
     lane = lax.broadcasted_iota(jnp.int32, (tokens, LANES), 1)
     heads = width // HS
 
+    def store(at, value):
+        start = 0
+        for sent_ref in sent_refs:
+            size = sent_ref.shape[0]
+            sent_ref[:, at] = value[start : start + size].astype(jnp.bfloat16)
+            start += size
+
     def one_group(group, found):
         numbers = [group * GROUP + inner for inner in range(GROUP)]
         results = partial_softmax(
-            numbers, query_ref, (first_key, second_key), (first_value, second_value), same_row
+            numbers, query_ref, (first_key, second_key), (first_value, second_value), rows, same_row
         )
         for head, (mean, lse) in zip(numbers, results):
-            sent_ref[:, lanes_of(head)] = mean.astype(jnp.bfloat16)
+            store(lanes_of(head), mean)
             found = jnp.where(lane % heads == head, lse, found)
         return found
 
     left = lax.fori_loop(0, heads // GROUP, one_group, jnp.zeros((tokens, LANES), jnp.float32))
-    packed = jnp.zeros((tokens, LANES), jnp.bfloat16)
+    packed = jnp.zeros((tokens, LANES), jnp.float32)
     for piece in range(PIECES):
-        part = left.astype(jnp.bfloat16)
-        left = left - part.astype(jnp.float32)
-        packed = jnp.where(lane // heads == piece, part.astype(jnp.float32), packed.astype(jnp.float32)).astype(jnp.bfloat16)
-    sent_ref[:, width:] = packed
-
-
-def guest_attention(query, keys, values, chunk, after):
+        part = left.astype(jnp.bfloat16).astype(jnp.float32)
+        left = left - part
+        packed = jnp.where(lane // heads == piece, part, packed)
+    packed = jnp.where(lane == LANES - 1, 1.0, packed)
+    store(slice(width, width + LANES), packed)
+
+
+def guest_attention(query, keys, values, start, sizes, after):
     tokens, width = query.shape
-    whole = pl.BlockSpec((tokens, width), lambda i: (0, 0))
-    block = pl.BlockSpec((tokens, width), lambda i: (chunk, 0))
     return pl.pallas_call(
-        guest_kernel,
-        grid=(1,),
-        in_specs=[whole] + [block] * 4 + [pl.BlockSpec(memory_space=pl.ANY)],
-        out_specs=pl.BlockSpec((tokens, width + LANES), lambda i: (0, 0)),
-        out_shape=jax.ShapeDtypeStruct((tokens, width + LANES), jnp.bfloat16),
+        functools.partial(guest_kernel, start),
+        in_specs=[IN_VMEM] * 5 + [IN_PLACE],
+        out_specs=[IN_VMEM] * len(sizes),
+        out_shape=[jax.ShapeDtypeStruct((size, width + LANES), jnp.bfloat16) for size in sizes],
         compiler_params=pltpu.CompilerParams(vmem_limit_bytes=24 * 2**20),
         cost_estimate=pl.CostEstimate(
             flops=8 * tokens * tokens * width, bytes_accessed=12 * tokens * width, transcendentals=0
@@ -298,15 +308,15 @@
     )(query, *keys, *values, after)
 
 
-def merge_kernel(has_guest, mean_ref, lse_ref, sent_ref, *rest):
+def merge_kernel(mean_ref, lse_ref, sent_ref, *rest):
     out_ref = rest[-1]
-    tokens, width = mean_ref.shape
+    _, width = mean_ref.shape
     heads = width // HS
     pieces = sent_ref[:, width:].astype(jnp.float32)
     lse = pieces
     for piece in range(1, PIECES):
         lse = lse + pltpu.roll(pieces, LANES - piece * heads, 1)
-    lse = jnp.where(has_guest[0] > 0, lse, NEG_FILL)
+    lse = jnp.where(pieces[:, LANES - 1 :] > 0, lse, NEG_FILL)
     share = 1.0 / (1.0 + jnp.exp(lse_ref[...] - lse))
 
     def one_group(group, share):
@@ -320,31 +330,31 @@
     lax.fori_loop(0, heads // GROUP, one_group, share)
 
 
-def merge(has_guest, mean, lse, sent, chunk, before):
+def merge(mean, lse, sent, start, before):
     tokens, width = mean.shape
     part_tokens = sent.shape[0]
-    here = lambda i, flag: (chunk, 0)
+
+    def rows(lanes):
+        return pl.BlockSpec((pl.Element(part_tokens), pl.Element(lanes)), lambda i: (start, 0))
+
     return pl.pallas_call(
         merge_kernel,
-        grid_spec=pltpu.PrefetchScalarGridSpec(
-            num_scalar_prefetch=1,
-            grid=(1,),
-            in_specs=[
-                pl.BlockSpec((part_tokens, width), here),
-                pl.BlockSpec((part_tokens, LANES), here),
-                pl.BlockSpec((part_tokens, width + LANES), lambda i, flag: (0, 0)),
-            ]
-            + [pl.BlockSpec(memory_space=pl.ANY)] * len(before),
-            out_specs=pl.BlockSpec((part_tokens, width), here),
-        ),
+        grid=(1,),
+        in_specs=[
+            rows(width),
+            rows(LANES),
+            pl.BlockSpec((part_tokens, width + LANES), lambda i: (0, 0)),
+        ]
+        + [IN_PLACE] * len(before),
+        out_specs=rows(width),
         out_shape=jax.ShapeDtypeStruct((tokens, width), jnp.bfloat16),
-        input_output_aliases={4: 0} if before else {},
+        input_output_aliases={3: 0} if before else {},
         compiler_params=pltpu.CompilerParams(vmem_limit_bytes=16 * 2**20),
         cost_estimate=pl.CostEstimate(
             flops=4 * part_tokens * width, bytes_accessed=8 * part_tokens * width, transcendentals=0
         ),
         name="merge",
-    )(has_guest, mean, lse, sent, *before)
+    )(mean, lse, sent, *before)
 
 
 def matchings(slots):
@@ -367,8 +377,17 @@
     ]
 
 
-def which_matching(request_of_slot, every):
-    def kernel(request_ref, number_ref):
+def prepare(request_of_slot, query, every):
+    width = query.shape[1]
+    part = QUERY_ROWS[0] * COLS
+
+    def kernel(request_hbm, query_hbm, number_hbm, part_ref, request_ref, number_ref, sems):
+        asked = pltpu.make_async_copy(request_hbm, request_ref, sems.at[0])
+        taken = pltpu.make_async_copy(query_hbm.at[pl.ds(0, part)], part_ref, sems.at[1])
+        told = pltpu.make_async_copy(number_ref, number_hbm, sems.at[2])
+        asked.start()
+        taken.start()
+        asked.wait()
         chosen = jnp.int32(0)
         for number, matching in enumerate(every):
             fits = functools.reduce(
@@ -376,14 +395,26 @@
             )
             chosen = jnp.where(fits, jnp.int32(number), chosen)
         number_ref[0] = chosen
-
-    return pl.pallas_call(
+        told.start()
+        taken.wait()
+        told.wait()
+
+    number, first_part = pl.pallas_call(
         kernel,
-        in_specs=[pl.BlockSpec(memory_space=pltpu.SMEM)],
-        out_specs=pl.BlockSpec(memory_space=pltpu.SMEM),
-        out_shape=jax.ShapeDtypeStruct((1,), jnp.int32),
-        name="which_matching",
-    )(request_of_slot)[0]
+        in_specs=[IN_PLACE] * 2,
+        out_specs=[IN_PLACE, IN_VMEM],
+        out_shape=[
+            jax.ShapeDtypeStruct((1,), jnp.int32),
+            jax.ShapeDtypeStruct((part, width), query.dtype),
+        ],
+        scratch_shapes=[
+            pltpu.SMEM(request_of_slot.shape, jnp.int32),
+            pltpu.SMEM((1,), jnp.int32),
+            pltpu.SemaphoreType.DMA((3,)),
+        ],
+        name="prepare",
+    )(request_of_slot, query)
+    return number[0], first_part
 
 
 def few_slots(query_vectors, key_vectors, value_vectors, request_of_slot):
@@ -392,41 +423,44 @@
     slot_devices = device_count // slot_count
     token_count = ROWS * COLS
     width = HEADS * HS
-    chunk_tokens = token_count // CHUNKS
     query = query_vectors.reshape(token_count, width)
     key = key_vectors.reshape(token_count, width)
     value = value_vectors.reshape(token_count, width)
     every = [matching for matching in matchings(list(range(slot_count))) if matching]
-    branch = which_matching(request_of_slot, every)
-    my_slot = lax.axis_index("view") // slot_devices
+    branch, first_part = prepare(request_of_slot, query, every)
 
     def exchange(matching):
         pairs = device_pairs(matching, slot_devices)
-        members = [slot for pair in matching for slot in pair]
-
-        def run(key, value, query):
-            guests, source = [], query
-            for part in range(CHUNKS):
-                sent = lax.slice_in_dim(source, part * chunk_tokens, (part + 1) * chunk_tokens)
-                source, sent = lax.optimization_barrier((source, sent))
+
+        def run(key, value, query, first_part):
+            return pair_attention(key, value, query, first_part)
+
+        def pair_attention(key, value, query, first_part):
+            guests = [lax.ppermute(first_part, "view", pairs)]
+            start = first_part.shape[0]
+            for rows in QUERY_ROWS[1:]:
+                sent = lax.slice_in_dim(query, start, start + rows * COLS)
                 guests.append(lax.ppermute(sent, "view", pairs))
+                start += rows * COLS
             keys = (key, partner(key, "view", 0))
             values = (value, partner(value, "view", 0))
             mean, lse = own_attention(query, keys, values)
-            backs = [
-                lax.ppermute(guest_attention(guest, keys, values, part, lse), "view", pairs)
-                for part, guest in enumerate(guests)
-            ]
-            has_guest = functools.reduce(jnp.logical_or, [my_slot == slot for slot in members])
-            has_guest = has_guest.astype(jnp.int32).reshape(1)
-            out = ()
-            for part, back in enumerate(backs):
-                out = (merge(has_guest, mean, lse, back, part, out),)
+            backs, start = [], 0
+            for guest, rows in zip(guests, RETURN_ROWS):
+                sizes = [row * COLS for row in rows]
+                for sent in guest_attention(guest, keys, values, start, sizes, lse):
+                    backs.append(lax.ppermute(sent, "view", pairs))
+                start += guest.shape[0]
+            out, start = (), 0
+            for back in backs:
+                out = (merge(mean, lse, back, start, out),)
+                start += back.shape[0]
             return out[0]
 
         return run
 
-    attended = lax.switch(branch, [exchange(matching) for matching in every], key, value, query)
+    branches = [exchange(matching) for matching in every]
+    attended = lax.switch(branch, branches, key, value, query, first_part)
     return attended.reshape(1, ROWS, COLS, HEADS * HS)
 
 

time: 57.3 us -> 55 us (0.960); the launches traced: 56.2 us -> 54.7 us
  waiting for transfers between devices: 22.7 us -> 20 us
  starting transfers between devices: 16.3 us -> 18.7 us
  local copies, waits for them, and re-layouts: 2.2 us -> 1.09 us
    ppermute x4 -> x5, waiting for transfers between devices: 22.7 us -> 20 us  [the longest x3 10.5 us: pair_attention(): backs.append(lax.ppermute(sent, 'view', pairs))]
    ppermute x4 -> x5, starting transfers between devices: 15.7 us -> 18.1 us  [the longest x3 11.2 us: pair_attention(): backs.append(lax.ppermute(sent, 'view', pairs))]
    slice x2 -> x1, local copies, waits for them, and re-layouts: 2.19 us -> 1.08 us  [pair_attention(): sent = lax.slice_in_dim(query, start, start + rows * COLS)]
    pallas_call x5 -> x6, Pallas kernels: 10.2 us -> 9.58 us  [the longest x2 4.37 us: guest_attention(): pl.pallas_call(functools.partial(guest_kernel, start), in_specs=[IN_VMEM]...]
    pallas_call x1, Pallas kernels: 3.92 us -> 4.54 us  [own_attention(): pl.pallas_call(own_kernel, out_shape=[jax.ShapeDtypeStruct((tokens, width...]
  transfers between devices with their start and end apart: 6 -> 7, of which waited for: 4 -> 5; matrix products, arithmetic and copies ran while one was open for 4% -> 2% of each run, Pallas kernels for 20% -> 22%
where the time goes in v3:
time: 55 us; the launch traced here: 54.7 us
  waiting for transfers between devices  20 us (36%)
  starting transfers between devices  18.7 us (34%)
  Pallas kernels  14.1 us (26%)
  local copies, waits for them, and re-layouts  1.09 us (2%)
  between operations  0.66 us (1%)
    ppermute x3, starting transfers between devices, pair_attention(): backs.append(lax.ppermute(sent, 'view', pairs))  11.2 us
    ppermute x3, waiting for transfers between devices, pair_attention(): backs.append(lax.ppermute(sent, 'view', pairs))  10.5 us
    ppermute x1, waiting for transfers between devices, pair_attention(): guests = [lax.ppermute(first_part, 'view', pairs)]  5.02 us
    pallas_call x1, Pallas kernels, own_attention(): pl.pallas_call(own_kernel, out_shape=[jax.ShapeDtypeStruct((tokens, width...  4.54 us
    ppermute x1, waiting for transfers between devices, pair_attention(): guests.append(lax.ppermute(sent, 'view', pairs))  4.53 us
    ppermute x1, starting transfers between devices, pair_attention(): guests = [lax.ppermute(first_part, 'view', pairs)]  4.49 us
    pallas_call x2, Pallas kernels, guest_attention(): pl.pallas_call(functools.partial(guest_kernel, start), in_specs=[IN_VMEM]...  4.37 us
    pallas_call x3, Pallas kernels, merge(): pl.pallas_call(merge_kernel, grid=(1,), in_specs=[rows(width), rows(LANES...  4 us
  transfers between devices with their start and end apart: 7, of which 5 were waited for; matrix products, arithmetic and copies ran while one was open for 2% of the time, Pallas kernels for 22%

profile of v3, /device:TPU:10, one launch (start us, length us, event | category | flops | bytes accessed | tf_op | source)
XLA Modules:
  0.0 54.7 jit_solution(10856036931282177439)
XLA Ops:
  0.0 1.2 %prepare.1 = (s32[1]{0:T(128)}, bf16[64,4096]{1,0:T(8,128)(2,1)S(1)}) custom-call(s32[4]{0:T(128)} %request_hbm.1, bf16[128,4096]{1,0:T(8,128)(2,1)} %bitcast.101), custom_call_target="tpu_custom_call" | custom-call | tf_op jit(solution)/shard_map/prepare/pallas_call | solution.py:402
  1.9 52.8 %conditional.1 = (bf16[1,16,8,4096]{3,2,1,0:T(8,128)(2,1)}) conditional(s32[]{:T(128)} %bitcast.28, (bf16[1,16,8,4096]{3,2,1,0:T(8,128)(2,1)}, bf16[1,16,8,4096]{3,2,1,0:T(8,128)(2,1)}, bf16[128,4096]{1,0:T(8,128)(2,1)}, bf16[64,4096]{1,0:T(8,128)(2,1)S(1)}) %tuple.60, (bf16[1,16,8,4096]{3,2,1,0:T(8,128)(2,1)}, ...), branch_computations={%region_0.0_spmd, %region_1.0_spmd, %region_2.0_spmd, %region_3.0_... | conditional | flops 807403520 | bytes 44171608 | solution.py:463
  1.9 0.1 collective-permute-start.14
  2.0 0.5 collective-permute-start.15
  2.5 4.5 %collective-permute-start.19 = (bf16[64,4096]{1,0:T(8,128)(2,1)S(1)}, bf16[64,4096]{1,0:T(8,128)(2,1)S(1)}, u32[]{:S(2)}, u32[]{:S(2)}) collective-permute-start(bf16[64,4096]{1,0:T(8,128)(2,1)S(1)} %get-tuple-element.129), channel_id=1, source_target_pairs={{4,12},{5,13},{6,14},{7,15},{12,4},{13,5},{14,6},{15,7},{20,28},{2... | collective-permute-start | bytes 1572872 | tf_op jit(solution)/shard_map/cond/branch_2_fun/ppermute | solution.py:439
  7.0 1.1 %slice.20 = bf16[64,4096]{1,0:T(8,128)(2,1)S(1)} slice(bf16[128,4096]{1,0:T(8,128)(2,1)} %get-tuple-element.122.query_ref), slice={[64:128], [0:4096]} | slice | bytes 1048576 | tf_op jit(solution)/shard_map/cond/branch_2_fun/slice | solution.py:442
  8.1 0.0 copy-start.2
  8.1 0.0 copy-start.11
  8.1 2.4 %collective-permute-start.16 = (bf16[64,4096]{1,0:T(8,128)(2,1)S(1)}, bf16[64,4096]{1,0:T(8,128)(2,1)S(1)}, u32[]{:S(2)}, u32[]{:S(2)}) collective-permute-start(bf16[64,4096]{1,0:T(8,128)(2,1)S(1)} %slice.20), channel_id=1, source_target_pairs={{4,12},{5,13},{6,14},{7,15},{12,4},{13,5},{14,6},{15,7},{20,28},{2... | collective-permute-start | bytes 1572872 | tf_op jit(solution)/shard_map/cond/branch_2_fun/ppermute | solution.py:443
  10.5 0.0 collective-permute-done.14.second_key
  10.5 0.0 collective-permute-done.15.second_value
  10.5 4.5 %own_attention.11 = (f32[128,4096]{1,0:T(8,128)S(1)}, f32[128,128]{1,0:T(8,128)S(1)}) custom-call(bf16[128,4096]{1,0:T(8,128)(2,1)} %get-tuple-element.122.query_ref, bf16[128,4096]{1,0:T(8,128)(2,1)} %bitcast.38, bf16[128,4096]{1,0:T(8,128)(2,1)S(1)} %collective-permute-done.14.second_key, bf16[128,4096]{1,0:T(8,128)(2,1)} %bitcast.74, ...), custom_call_target="tpu_custom_call" | custom-call | flops 536870912 | bytes 7340032 | tf_op jit(solution)/shard_map/cond/branch_2_fun/own_attention/pallas_call | solution.py:245
  15.0 5.0 %collective-permute-done.19.query_ref = bf16[64,4096]{1,0:T(8,128)(2,1)S(1)} collective-permute-done((bf16[64,4096]{1,0:T(8,128)(2,1)S(1)}, bf16[64,4096]{1,0:T(8,128)(2,1)S(1)}, u32[]{:S(2)}, u32[]{:S(2)}) %collective-permute-start.19) | collective-permute-done | bytes 524320 | tf_op jit(solution)/shard_map/cond/branch_2_fun/ppermute | solution.py:439
  20.1 0.0 copy-done.2
  20.1 0.0 copy-done.11
  20.1 2.2 %guest_attention.23 = bf16[64,4224]{1,0:T(8,128)(2,1)S(1)} custom-call(bf16[64,4096]{1,0:T(8,128)(2,1)S(1)} %collective-permute-done.19.query_ref, bf16[128,4096]{1,0:T(8,128)(2,1)S(1)} %bitcast.39, bf16[128,4096]{1,0:T(8,128)(2,1)S(1)} %collective-permute-done.14.second_key, bf16[128,4096]{1,0:T(8,128)(2,1)S(1)} %bitcast.75, ...), custom_call_target="tpu_custom_call" | custom-call | flops 134217728 | bytes 3145728 | tf_op jit(solution)/shard_map/cond/branch_2_fun/guest_attention/pallas_call | solution.py:298
  22.2 4.5 %collective-permute-start.20 = (bf16[64,4224]{1,0:T(8,128)(2,1)S(1)}, bf16[64,4224]{1,0:T(8,128)(2,1)S(1)}, u32[]{:S(2)}, u32[]{:S(2)}) collective-permute-start(bf16[64,4224]{1,0:T(8,128)(2,1)S(1)} %guest_attention.23), channel_id=1, source_target_pairs={{4,12},{5,13},{6,14},{7,15},{12,4},{13,5},{14,6},{15,7},{20,28},{2... | collective-permute-start | bytes 1622024 | tf_op jit(solution)/shard_map/cond/branch_2_fun/ppermute | solution.py:452
  26.8 4.5 %collective-permute-done.16.query_ref = bf16[64,4096]{1,0:T(8,128)(2,1)S(1)} collective-permute-done((bf16[64,4096]{1,0:T(8,128)(2,1)S(1)}, bf16[64,4096]{1,0:T(8,128)(2,1)S(1)}, u32[]{:S(2)}, u32[]{:S(2)}) %collective-permute-start.16) | collective-permute-done | bytes 524320 | tf_op jit(solution)/shard_map/cond/branch_2_fun/ppermute | solution.py:443
  31.3 2.2 %guest_attention.22 = (bf16[48,4224]{1,0:T(8,128)(2,1)S(1)}, bf16[16,4224]{1,0:T(8,128)(2,1)S(1)}) custom-call(bf16[64,4096]{1,0:T(8,128)(2,1)S(1)} %collective-permute-done.16.query_ref, bf16[128,4096]{1,0:T(8,128)(2,1)S(1)} %bitcast.40, bf16[128,4096]{1,0:T(8,128)(2,1)S(1)} %collective-permute-done.14.second_key, bf16[128,4096]{1,0:T(8,128)(2,1)S(1)} %bitcast.76, ...), custom_call_target="tpu_custom_call" | custom-call | flops 134217728 | bytes 3145728 | tf_op jit(solution)/shard_map/cond/branch_2_fun/guest_attention/pallas_call | solution.py:298
  33.5 4.5 %collective-permute-start.18 = (bf16[48,4224]{1,0:T(8,128)(2,1)S(1)}, bf16[48,4224]{1,0:T(8,128)(2,1)S(1)}, u32[]{:S(2)}, u32[]{:S(2)}) collective-permute-start(bf16[48,4224]{1,0:T(8,128)(2,1)S(1)} %get-tuple-element.128), channel_id=1, source_target_pairs={{4,12},{5,13},{6,14},{7,15},{12,4},{13,5},{14,6},{15,7},{20,28},{2... | collective-permute-start | bytes 1216520 | tf_op jit(solution)/shard_map/cond/branch_2_fun/ppermute | solution.py:452
  38.0 2.2 %collective-permute-start.17 = (bf16[16,4224]{1,0:T(8,128)(2,1)S(1)}, bf16[16,4224]{1,0:T(8,128)(2,1)S(1)}, u32[]{:S(2)}, u32[]{:S(2)}) collective-permute-start(bf16[16,4224]{1,0:T(8,128)(2,1)S(1)} %get-tuple-element.127), channel_id=1, source_target_pairs={{4,12},{5,13},{6,14},{7,15},{12,4},{13,5},{14,6},{15,7},{20,28},{2... | collective-permute-start | bytes 405512 | tf_op jit(solution)/shard_map/cond/branch_2_fun/ppermute | solution.py:452
  40.2 2.6 %collective-permute-done.20.sent_ref = bf16[64,4224]{1,0:T(8,128)(2,1)S(1)} collective-permute-done((bf16[64,4224]{1,0:T(8,128)(2,1)S(1)}, bf16[64,4224]{1,0:T(8,128)(2,1)S(1)}, u32[]{:S(2)}, u32[]{:S(2)}) %collective-permute-start.20) | collective-permute-done | bytes 540704 | tf_op jit(solution)/shard_map/cond/branch_2_fun/ppermute | solution.py:452
  42.9 1.5 %merge.33.rest_0_ = bf16[128,4096]{1,0:T(8,128)(2,1)} custom-call(f32[128,4096]{1,0:T(8,128)S(1)} %get-tuple-element.125.mean_ref, f32[128,128]{1,0:T(8,128)S(1)} %get-tuple-element.126._.lse_ref, bf16[64,4224]{1,0:T(8,128)(2,1)S(1)} %collective-permute-done.20.sent_ref), custom_call_target="tpu_custom_call" | custom-call | flops 1048576 | bytes 2097152 | tf_op jit(solution)/shard_map/cond/branch_2_fun/merge/pallas_call | solution.py:340
  44.4 7.2 %collective-permute-done.18.sent_ref = bf16[48,4224]{1,0:T(8,128)(2,1)S(1)} collective-permute-done((bf16[48,4224]{1,0:T(8,128)(2,1)S(1)}, bf16[48,4224]{1,0:T(8,128)(2,1)S(1)}, u32[]{:S(2)}, u32[]{:S(2)}) %collective-permute-start.18) | collective-permute-done | bytes 405536 | tf_op jit(solution)/shard_map/cond/branch_2_fun/ppermute | solution.py:452
  51.6 1.4 %merge.34.rest_0_ = bf16[128,4096]{1,0:T(8,128)(2,1)} custom-call(f32[128,4096]{1,0:T(8,128)S(1)} %get-tuple-element.125.mean_ref, f32[128,128]{1,0:T(8,128)S(1)} %get-tuple-element.126._.lse_ref, bf16[48,4224]{1,0:T(8,128)(2,1)S(1)} %collective-permute-done.18.sent_ref, bf16[128,4096]{1,0:T(8,128)(2,1)} %merge.33.rest_0_), custom_call_target="tpu_custom_call", output_to_operand_aliasing={{}: (3, {})} | custom-call | flops 786432 | bytes 1572864 | tf_op jit(solution)/shard_map/cond/branch_2_fun/merge/pallas_call | solution.py:340
  52.9 0.6 %collective-permute-done.17.sent_ref = bf16[16,4224]{1,0:T(8,128)(2,1)S(1)} collective-permute-done((bf16[16,4224]{1,0:T(8,128)(2,1)S(1)}, bf16[16,4224]{1,0:T(8,128)(2,1)S(1)}, u32[]{:S(2)}, u32[]{:S(2)}) %collective-permute-start.17) | collective-permute-done | bytes 135200 | tf_op jit(solution)/shard_map/cond/branch_2_fun/ppermute | solution.py:452
  53.6 1.1 %merge.35 = bf16[128,4096]{1,0:T(8,128)(2,1)} custom-call(f32[128,4096]{1,0:T(8,128)S(1)} %get-tuple-element.125.mean_ref, f32[128,128]{1,0:T(8,128)S(1)} %get-tuple-element.126._.lse_ref, bf16[16,4224]{1,0:T(8,128)(2,1)S(1)} %collective-permute-done.17.sent_ref, bf16[128,4096]{1,0:T(8,128)(2,1)} %merge.34.rest_0_), custom_call_target="tpu_custom_call", output_to_operand_aliasing={{}: (3, {})} | custom-call | flops 262144 | bytes 524288 | tf_op jit(solution)/shard_map/cond/branch_2_fun/merge/pallas_call | solution.py:340
Async XLA Ops:
  1.9 8.6 %collective-permute-start.14 = (bf16[128,4096]{1,0:T(8,128)(2,1)}, bf16[128,4096]{1,0:T(8,128)(2,1)S(1)}, u32[]{:S(2)}, u32[]{:S(2)}) collective-permute-start(bf16[128,4096]{1,0:T(8,128)(2,1)} %bitcast.37), channel_id=1, source_target_pairs={{0,1},{1,0},{2,3},{3,2},{4,5},{5,4},{6,7},{7,6},{8,9},{9,8},{10,11... | collective-permute-start | bytes 3145736 | tf_op jit(solution)/shard_map/cond/branch_2_fun/ppermute | solution.py:21
  2.0 8.5 %collective-permute-start.15 = (bf16[128,4096]{1,0:T(8,128)(2,1)}, bf16[128,4096]{1,0:T(8,128)(2,1)S(1)}, u32[]{:S(2)}, u32[]{:S(2)}) collective-permute-start(bf16[128,4096]{1,0:T(8,128)(2,1)} %bitcast.73), channel_id=1, source_target_pairs={{0,1},{1,0},{2,3},{3,2},{4,5},{5,4},{6,7},{7,6},{8,9},{9,8},{10,11... | collective-permute-start | bytes 3145736 | tf_op jit(solution)/shard_map/cond/branch_2_fun/ppermute | solution.py:21
  2.5 17.6 %collective-permute-start.19 = (bf16[64,4096]{1,0:T(8,128)(2,1)S(1)}, bf16[64,4096]{1,0:T(8,128)(2,1)S(1)}, u32[]{:S(2)}, u32[]{:S(2)}) collective-permute-start(bf16[64,4096]{1,0:T(8,128)(2,1)S(1)} %get-tuple-element.129), channel_id=1, source_target_pairs={{4,12},{5,13},{6,14},{7,15},{12,4},{13,5},{14,6},{15,7},{20,28},{2... | collective-permute-start | bytes 1572872 | tf_op jit(solution)/shard_map/cond/branch_2_fun/ppermute | solution.py:439
  8.1 12.0 %copy-start.2 = (bf16[1,16,8,4096]{3,2,1,0:T(8,128)(2,1)S(1)}, bf16[1,16,8,4096]{3,2,1,0:T(8,128)(2,1)}, u32[]{:S(2)}) copy-start(bf16[1,16,8,4096]{3,2,1,0:T(8,128)(2,1)} %get-tuple-element.203) | copy-start | bytes 3145732 | tf_op jit(solution)/shard_map/cond
  8.1 12.0 %copy-start.11 = (bf16[1,16,8,4096]{3,2,1,0:T(8,128)(2,1)S(1)}, bf16[1,16,8,4096]{3,2,1,0:T(8,128)(2,1)}, u32[]{:S(2)}) copy-start(bf16[1,16,8,4096]{3,2,1,0:T(8,128)(2,1)} %get-tuple-element.212) | copy-start | bytes 3145732 | tf_op jit(solution)/shard_map/cond
  8.1 23.2 %collective-permute-start.16 = (bf16[64,4096]{1,0:T(8,128)(2,1)S(1)}, bf16[64,4096]{1,0:T(8,128)(2,1)S(1)}, u32[]{:S(2)}, u32[]{:S(2)}) collective-permute-start(bf16[64,4096]{1,0:T(8,128)(2,1)S(1)} %slice.20), channel_id=1, source_target_pairs={{4,12},{5,13},{6,14},{7,15},{12,4},{13,5},{14,6},{15,7},{20,28},{2... | collective-permute-start | bytes 1572872 | tf_op jit(solution)/shard_map/cond/branch_2_fun/ppermute | solution.py:443
  22.2 20.6 %collective-permute-start.20 = (bf16[64,4224]{1,0:T(8,128)(2,1)S(1)}, bf16[64,4224]{1,0:T(8,128)(2,1)S(1)}, u32[]{:S(2)}, u32[]{:S(2)}) collective-permute-start(bf16[64,4224]{1,0:T(8,128)(2,1)S(1)} %guest_attention.23), channel_id=1, source_target_pairs={{4,12},{5,13},{6,14},{7,15},{12,4},{13,5},{14,6},{15,7},{20,28},{2... | collective-permute-start | bytes 1622024 | tf_op jit(solution)/shard_map/cond/branch_2_fun/ppermute | solution.py:452
  33.5 18.1 %collective-permute-start.18 = (bf16[48,4224]{1,0:T(8,128)(2,1)S(1)}, bf16[48,4224]{1,0:T(8,128)(2,1)S(1)}, u32[]{:S(2)}, u32[]{:S(2)}) collective-permute-start(bf16[48,4224]{1,0:T(8,128)(2,1)S(1)} %get-tuple-element.128), channel_id=1, source_target_pairs={{4,12},{5,13},{6,14},{7,15},{12,4},{13,5},{14,6},{15,7},{20,28},{2... | collective-permute-start | bytes 1216520 | tf_op jit(solution)/shard_map/cond/branch_2_fun/ppermute | solution.py:452
  38.0 15.6 %collective-permute-start.17 = (bf16[16,4224]{1,0:T(8,128)(2,1)S(1)}, bf16[16,4224]{1,0:T(8,128)(2,1)S(1)}, u32[]{:S(2)}, u32[]{:S(2)}) collective-permute-start(bf16[16,4224]{1,0:T(8,128)(2,1)S(1)} %get-tuple-element.127), channel_id=1, source_target_pairs={{4,12},{5,13},{6,14},{7,15},{12,4},{13,5},{14,6},{15,7},{20,28},{2... | collective-permute-start | bytes 405512 | tf_op jit(solution)/shard_map/cond/branch_2_fun/ppermute | solution.py:452

commit v4 on v3

--- a/solution.py
+++ b/solution.py
@@ -180,7 +180,7 @@
 
 SCALING = HS ** (-0.5)
 LANES = 128
-PIECES = 3
+MARKER = 8
 GROUP = 8
 QUERY_ROWS = (8, 8)
 RETURN_ROWS = ((8,), (6, 2))
@@ -256,22 +256,23 @@
     )(query, *keys, *values)
 
 
+def rows_of(head, tokens):
+    return pl.ds(pl.multiple_of(head * tokens, tokens), tokens)
+
+
 def guest_kernel(start, query_ref, first_key, second_key, first_value, second_value, _, *sent_refs):
     tokens, width = query_ref.shape
+    heads = width // HS
     rows = slice(start, start + tokens)
     shape = (tokens, 2 * tokens)
     query_row = lax.broadcasted_iota(jnp.int32, shape, 0) // COLS
     key_row = lax.broadcasted_iota(jnp.int32, shape, 1) % tokens // COLS
     same_row = query_row == key_row
     lane = lax.broadcasted_iota(jnp.int32, (tokens, LANES), 1)
-    heads = width // HS
-
-    def store(at, value):
-        start = 0
-        for sent_ref in sent_refs:
-            size = sent_ref.shape[0]
-            sent_ref[:, at] = value[start : start + size].astype(jnp.bfloat16)
-            start += size
+    firsts = [0]
+    for sent_ref in sent_refs[1:]:
+        firsts.append(tokens - sent_ref.shape[0] // heads)
+    sizes = [stop - first for first, stop in zip(firsts, firsts[1:] + [tokens])]
 
     def one_group(group, found):
         numbers = [group * GROUP + inner for inner in range(GROUP)]
@@ -279,27 +280,31 @@
             numbers, query_ref, (first_key, second_key), (first_value, second_value), rows, same_row
         )
         for head, (mean, lse) in zip(numbers, results):
-            store(lanes_of(head), mean)
+            for sent_ref, first, size in zip(sent_refs, firsts, sizes):
+                part = mean[first : first + size].astype(jnp.bfloat16)
+                sent_ref[rows_of(head, size), :] = part
             found = jnp.where(lane % heads == head, lse, found)
         return found
 
-    left = lax.fori_loop(0, heads // GROUP, one_group, jnp.zeros((tokens, LANES), jnp.float32))
-    packed = jnp.zeros((tokens, LANES), jnp.float32)
-    for piece in range(PIECES):
-        part = left.astype(jnp.bfloat16).astype(jnp.float32)
-        left = left - part
-        packed = jnp.where(lane // heads == piece, part, packed)
-    packed = jnp.where(lane == LANES - 1, 1.0, packed)
-    store(slice(width, width + LANES), packed)
+    found = lax.fori_loop(0, heads // GROUP, one_group, jnp.zeros((tokens, LANES), jnp.float32))
+    high = found.astype(jnp.bfloat16).astype(jnp.float32)
+    pieces = jnp.where(lane // heads % 2 == 0, high, found - high)
+    half, at = tokens // 2, heads * sizes[0]
+    packed = jnp.where(lane[:half] < LANES // 2, pieces[:half], pieces[half:])
+    sent_refs[0][at : at + half, :] = packed.astype(jnp.bfloat16)
+    sent_refs[0][at + half :, :] = jnp.ones((MARKER, LANES), jnp.bfloat16)
 
 
 def guest_attention(query, keys, values, start, sizes, after):
     tokens, width = query.shape
+    heads = width // HS
+    lengths = [heads * size for size in sizes]
+    lengths[0] += tokens // 2 + MARKER
     return pl.pallas_call(
         functools.partial(guest_kernel, start),
         in_specs=[IN_VMEM] * 5 + [IN_PLACE],
         out_specs=[IN_VMEM] * len(sizes),
-        out_shape=[jax.ShapeDtypeStruct((size, width + LANES), jnp.bfloat16) for size in sizes],
+        out_shape=[jax.ShapeDtypeStruct((length, LANES), jnp.bfloat16) for length in lengths],
         compiler_params=pltpu.CompilerParams(vmem_limit_bytes=24 * 2**20),
         cost_estimate=pl.CostEstimate(
             flops=8 * tokens * tokens * width, bytes_accessed=12 * tokens * width, transcendentals=0
@@ -309,52 +314,88 @@
 
 
 def merge_kernel(mean_ref, lse_ref, sent_ref, *rest):
-    out_ref = rest[-1]
-    _, width = mean_ref.shape
+    out_ref, left_refs = (rest[-3], rest[-2:]) if len(rest) > 2 else (rest[-1], ())
+    tokens, width = mean_ref.shape
+    size = out_ref.shape[0]
     heads = width // HS
-    pieces = sent_ref[:, width:].astype(jnp.float32)
-    lse = pieces
-    for piece in range(1, PIECES):
-        lse = lse + pltpu.roll(pieces, LANES - piece * heads, 1)
-    lse = jnp.where(pieces[:, LANES - 1 :] > 0, lse, NEG_FILL)
-    share = 1.0 / (1.0 + jnp.exp(lse_ref[...] - lse))
+    half, at = tokens // 2, heads * size
+    pieces = sent_ref[at : at + half, :].astype(jnp.float32)
+    lse = pieces + pltpu.roll(pieces, LANES - heads, 1)
+    lse = jnp.concatenate([lse, pltpu.roll(lse, LANES // 2, 1)], axis=0)
+    received = sent_ref[at + half : at + half + 1, :].astype(jnp.float32) > 0
+    share = 1.0 / (1.0 + jnp.exp(lse_ref[...] - jnp.where(received, lse, NEG_FILL)))
 
     def one_group(group, share):
         for inner in range(GROUP):
-            at = lanes_of(group * GROUP + inner)
-            own = mean_ref[:, at]
-            guest = sent_ref[:, at].astype(jnp.float32)
-            out_ref[:, at] = (own + share[:, inner : inner + 1] * (guest - own)).astype(jnp.bfloat16)
+            head = group * GROUP + inner
+            lanes = lanes_of(head)
+            part = share[:, inner : inner + 1]
+            own = mean_ref[:size, lanes]
+            guest = sent_ref[rows_of(head, size), :].astype(jnp.float32)
+            out_ref[:, lanes] = (own + part[:size] * (guest - own)).astype(jnp.bfloat16)
+            if left_refs:
+                later = jnp.broadcast_to(part[size:], (tokens - size, HS))
+                own = mean_ref[size:, lanes]
+                left_refs[0][:, lanes] = own - later * own
+                left_refs[1][:, lanes] = later
         return pltpu.roll(share, LANES - GROUP, 1)
 
     lax.fori_loop(0, heads // GROUP, one_group, share)
 
 
-def merge(mean, lse, sent, start, before):
-    tokens, width = mean.shape
-    part_tokens = sent.shape[0]
-
-    def rows(lanes):
-        return pl.BlockSpec((pl.Element(part_tokens), pl.Element(lanes)), lambda i: (start, 0))
-
-    return pl.pallas_call(
+def last_kernel(scaled_ref, share_ref, sent_ref, _, out_ref):
+    size, width = scaled_ref.shape
+    for head in range(width // HS):
+        lanes = slice(head * HS, (head + 1) * HS)
+        guest = sent_ref[head * size : (head + 1) * size, :].astype(jnp.float32)
+        out_ref[:, lanes] = (scaled_ref[:, lanes] + share_ref[:, lanes] * guest).astype(jnp.bfloat16)
+
+
+def token_rows(first, size, width):
+    return pl.BlockSpec((pl.Element(size), pl.Element(width)), lambda i: (first, 0))
+
+
+def whole(shape):
+    return pl.BlockSpec(shape, lambda i: (0, 0))
+
+
+def merge(mean, lse, backs, start, sizes, before):
+    total, width = mean.shape
+    tokens = sum(sizes)
+    size, later = sizes[0], sizes[1:]
+    left = [jax.ShapeDtypeStruct((later[0], width), jnp.float32)] * 2 if later else []
+    result = jax.ShapeDtypeStruct((total, width), jnp.bfloat16)
+    params = pltpu.CompilerParams(vmem_limit_bytes=16 * 2**20)
+    out, *left = pl.pallas_call(
         merge_kernel,
         grid=(1,),
         in_specs=[
-            rows(width),
-            rows(LANES),
-            pl.BlockSpec((part_tokens, width + LANES), lambda i: (0, 0)),
+            token_rows(start, tokens, width),
+            token_rows(start, tokens, LANES),
+            whole(backs[0].shape),
         ]
         + [IN_PLACE] * len(before),
-        out_specs=rows(width),
-        out_shape=jax.ShapeDtypeStruct((tokens, width), jnp.bfloat16),
+        out_specs=[token_rows(start, size, width)] + [whole(part.shape) for part in left],
+        out_shape=[result] + left,
         input_output_aliases={3: 0} if before else {},
-        compiler_params=pltpu.CompilerParams(vmem_limit_bytes=16 * 2**20),
+        compiler_params=params,
         cost_estimate=pl.CostEstimate(
-            flops=4 * part_tokens * width, bytes_accessed=8 * part_tokens * width, transcendentals=0
+            flops=4 * tokens * width, bytes_accessed=8 * tokens * width, transcendentals=0
         ),
         name="merge",
-    )(mean, lse, sent, *before)
+    )(mean, lse, backs[0], *before)
+    if not later:
+        return out
+    return pl.pallas_call(
+        last_kernel,
+        grid=(1,),
+        in_specs=[whole(left[0].shape), whole(left[1].shape), whole(backs[1].shape), IN_PLACE],
+        out_specs=token_rows(start + size, later[0], width),
+        out_shape=result,
+        input_output_aliases={3: 0},
+        compiler_params=params,
+        name="last_merge",
+    )(*left, backs[1], out)
 
 
 def matchings(slots):
@@ -445,16 +486,16 @@
             keys = (key, partner(key, "view", 0))
             values = (value, partner(value, "view", 0))
             mean, lse = own_attention(query, keys, values)
-            backs, start = [], 0
+            returns, start = [], 0
             for guest, rows in zip(guests, RETURN_ROWS):
                 sizes = [row * COLS for row in rows]
-                for sent in guest_attention(guest, keys, values, start, sizes, lse):
-                    backs.append(lax.ppermute(sent, "view", pairs))
+                sent = guest_attention(guest, keys, values, start, sizes, lse)
+                backs = [lax.ppermute(part, "view", pairs) for part in sent]
+                returns.append((backs, start, sizes))
                 start += guest.shape[0]
-            out, start = (), 0
-            for back in backs:
-                out = (merge(mean, lse, back, start, out),)
-                start += back.shape[0]
+            out = ()
+            for backs, start, sizes in returns:
+                out = (merge(mean, lse, backs, start, sizes, out),)
             return out[0]
 
         return run

time: 55 us -> 54.3 us (0.987)
  no operation moved by 1% of the time
where the time goes in v4:
time: 54.3 us; the launch traced here: 54 us
  waiting for transfers between devices  19.6 us (36%)
  starting transfers between devices  18.7 us (34%)
  Pallas kernels  13.9 us (26%)
  local copies, waits for them, and re-layouts  1.09 us (2%)
  between operations  0.66 us (1%)
    ppermute x3, starting transfers between devices, pair_attention(): backs = [lax.ppermute(part, 'view', pairs) for part in sent]  11.2 us
    ppermute x3, waiting for transfers between devices, pair_attention(): backs = [lax.ppermute(part, 'view', pairs) for part in sent]  10 us
    ppermute x1, waiting for transfers between devices, pair_attention(): guests = [lax.ppermute(first_part, 'view', pairs)]  5.02 us
    pallas_call x1, Pallas kernels, own_attention(): pl.pallas_call(own_kernel, out_shape=[jax.ShapeDtypeStruct((tokens, width...  4.54 us
    ppermute x1, waiting for transfers between devices, pair_attention(): guests.append(lax.ppermute(sent, 'view', pairs))  4.54 us
    ppermute x1, starting transfers between devices, pair_attention(): guests = [lax.ppermute(first_part, 'view', pairs)]  4.49 us
    pallas_call x2, Pallas kernels, guest_attention(): pl.pallas_call(functools.partial(guest_kernel, start), in_specs=[IN_VMEM]...  4.35 us
    pallas_call x2, Pallas kernels, merge(): pl.pallas_call(merge_kernel, grid=(1,), in_specs=[token_rows(start, token...  3.08 us
  transfers between devices with their start and end apart: 7, of which 5 were waited for; matrix products, arithmetic and copies ran while one was open for 2% of the time, Pallas kernels for 22%

profile of v4, /device:TPU:10, one launch (start us, length us, event | category | flops | bytes accessed | tf_op | source)
XLA Modules:
  0.0 54.0 jit_solution(17117751336065901048)
XLA Ops:
  0.0 1.2 %prepare.1 = (s32[1]{0:T(128)}, bf16[64,4096]{1,0:T(8,128)(2,1)S(1)}) custom-call(s32[4]{0:T(128)} %request_hbm.1, bf16[128,4096]{1,0:T(8,128)(2,1)} %bitcast.101), custom_call_target="tpu_custom_call" | custom-call | tf_op jit(solution)/shard_map/prepare/pallas_call | solution.py:443
  1.9 52.1 %conditional.1 = (bf16[1,16,8,4096]{3,2,1,0:T(8,128)(2,1)}) conditional(s32[]{:T(128)} %bitcast.28, (bf16[1,16,8,4096]{3,2,1,0:T(8,128)(2,1)}, bf16[1,16,8,4096]{3,2,1,0:T(8,128)(2,1)}, bf16[128,4096]{1,0:T(8,128)(2,1)}, bf16[64,4096]{1,0:T(8,128)(2,1)S(1)}) %tuple.60, (bf16[1,16,8,4096]{3,2,1,0:T(8,128)(2,1)}, ...), branch_computations={%region_0.0_spmd, %region_1.0_spmd, %region_2.0_spmd, %region_3.0_... | conditional | flops 807403520 | bytes 44122456 | solution.py:504
  1.9 0.1 collective-permute-start.15
  2.0 0.5 collective-permute-start.14
  2.5 4.5 %collective-permute-start.18 = (bf16[64,4096]{1,0:T(8,128)(2,1)S(1)}, bf16[64,4096]{1,0:T(8,128)(2,1)S(1)}, u32[]{:S(2)}, u32[]{:S(2)}) collective-permute-start(bf16[64,4096]{1,0:T(8,128)(2,1)S(1)} %get-tuple-element.134), channel_id=1, source_target_pairs={{4,12},{5,13},{6,14},{7,15},{12,4},{13,5},{14,6},{15,7},{20,28},{2... | collective-permute-start | bytes 1572872 | tf_op jit(solution)/shard_map/cond/branch_2_fun/ppermute | solution.py:480
  7.0 1.1 %slice.20 = bf16[64,4096]{1,0:T(8,128)(2,1)S(1)} slice(bf16[128,4096]{1,0:T(8,128)(2,1)} %get-tuple-element.128.query_ref), slice={[64:128], [0:4096]} | slice | bytes 1048576 | tf_op jit(solution)/shard_map/cond/branch_2_fun/slice | solution.py:483
  8.1 0.0 copy-start.2
  8.1 0.0 copy-start.11
  8.1 2.4 %collective-permute-start.16 = (bf16[64,4096]{1,0:T(8,128)(2,1)S(1)}, bf16[64,4096]{1,0:T(8,128)(2,1)S(1)}, u32[]{:S(2)}, u32[]{:S(2)}) collective-permute-start(bf16[64,4096]{1,0:T(8,128)(2,1)S(1)} %slice.20), channel_id=1, source_target_pairs={{4,12},{5,13},{6,14},{7,15},{12,4},{13,5},{14,6},{15,7},{20,28},{2... | collective-permute-start | bytes 1572872 | tf_op jit(solution)/shard_map/cond/branch_2_fun/ppermute | solution.py:484
  10.5 0.0 collective-permute-done.15.second_value
  10.5 0.0 collective-permute-done.14.second_key
  10.5 4.5 %own_attention.11 = (f32[128,4096]{1,0:T(8,128)S(1)}, f32[128,128]{1,0:T(8,128)S(1)}) custom-call(bf16[128,4096]{1,0:T(8,128)(2,1)} %get-tuple-element.128.query_ref, bf16[128,4096]{1,0:T(8,128)(2,1)} %bitcast.38, bf16[128,4096]{1,0:T(8,128)(2,1)S(1)} %collective-permute-done.14.second_key, bf16[128,4096]{1,0:T(8,128)(2,1)} %bitcast.74, ...), custom_call_target="tpu_custom_call" | custom-call | flops 536870912 | bytes 7340032 | tf_op jit(solution)/shard_map/cond/branch_2_fun/own_attention/pallas_call | solution.py:245
  15.0 5.0 %collective-permute-done.18.query_ref = bf16[64,4096]{1,0:T(8,128)(2,1)S(1)} collective-permute-done((bf16[64,4096]{1,0:T(8,128)(2,1)S(1)}, bf16[64,4096]{1,0:T(8,128)(2,1)S(1)}, u32[]{:S(2)}, u32[]{:S(2)}) %collective-permute-start.18) | collective-permute-done | bytes 524320 | tf_op jit(solution)/shard_map/cond/branch_2_fun/ppermute | solution.py:480
  20.1 0.0 copy-done.2
  20.1 0.0 copy-done.11
  20.1 2.2 %guest_attention.23 = bf16[2088,128]{1,0:T(8,128)(2,1)S(1)} custom-call(bf16[64,4096]{1,0:T(8,128)(2,1)S(1)} %collective-permute-done.18.query_ref, bf16[128,4096]{1,0:T(8,128)(2,1)S(1)} %bitcast.39, bf16[128,4096]{1,0:T(8,128)(2,1)S(1)} %collective-permute-done.14.second_key, bf16[128,4096]{1,0:T(8,128)(2,1)S(1)} %bitcast.75, ...), custom_call_target="tpu_custom_call" | custom-call | flops 134217728 | bytes 3145728 | tf_op jit(solution)/shard_map/cond/branch_2_fun/guest_attention/pallas_call | solution.py:303
  22.2 4.5 %collective-permute-start.19 = (bf16[2088,128]{1,0:T(8,128)(2,1)S(1)}, bf16[2088,128]{1,0:T(8,128)(2,1)S(1)}, u32[]{:S(2)}, u32[]{:S(2)}) collective-permute-start(bf16[2088,128]{1,0:T(8,128)(2,1)S(1)} %guest_attention.23), channel_id=1, source_target_pairs={{4,12},{5,13},{6,14},{7,15},{12,4},{13,5},{14,6},{15,7},{20,28},{2... | collective-permute-start | bytes 1603592 | tf_op jit(solution)/shard_map/cond/branch_2_fun/ppermute | solution.py:493
  26.7 4.5 %collective-permute-done.16.query_ref = bf16[64,4096]{1,0:T(8,128)(2,1)S(1)} collective-permute-done((bf16[64,4096]{1,0:T(8,128)(2,1)S(1)}, bf16[64,4096]{1,0:T(8,128)(2,1)S(1)}, u32[]{:S(2)}, u32[]{:S(2)}) %collective-permute-start.16) | collective-permute-done | bytes 524320 | tf_op jit(solution)/shard_map/cond/branch_2_fun/ppermute | solution.py:484
  31.3 2.2 %guest_attention.22 = (bf16[1576,128]{1,0:T(8,128)(2,1)S(1)}, bf16[512,128]{1,0:T(8,128)(2,1)S(1)}) custom-call(bf16[64,4096]{1,0:T(8,128)(2,1)S(1)} %collective-permute-done.16.query_ref, bf16[128,4096]{1,0:T(8,128)(2,1)S(1)} %bitcast.40, bf16[128,4096]{1,0:T(8,128)(2,1)S(1)} %collective-permute-done.14.second_key, bf16[128,4096]{1,0:T(8,128)(2,1)S(1)} %bitcast.76, ...), custom_call_target="tpu_custom_call" | custom-call | flops 134217728 | bytes 3145728 | tf_op jit(solution)/shard_map/cond/branch_2_fun/guest_attention/pallas_call | solution.py:303
  33.5 4.5 %collective-permute-start.17 = (bf16[1576,128]{1,0:T(8,128)(2,1)S(1)}, bf16[1576,128]{1,0:T(8,128)(2,1)S(1)}, u32[]{:S(2)}, u32[]{:S(2)}) collective-permute-start(bf16[1576,128]{1,0:T(8,128)(2,1)S(1)} %get-tuple-element.133), channel_id=1, source_target_pairs={{4,12},{5,13},{6,14},{7,15},{12,4},{13,5},{14,6},{15,7},{20,28},{2... | collective-permute-start | bytes 1210376 | tf_op jit(solution)/shard_map/cond/branch_2_fun/ppermute | solution.py:493
  38.0 2.2 %collective-permute-start.20 = (bf16[512,128]{1,0:T(8,128)(2,1)S(1)}, bf16[512,128]{1,0:T(8,128)(2,1)S(1)}, u32[]{:S(2)}, u32[]{:S(2)}) collective-permute-start(bf16[512,128]{1,0:T(8,128)(2,1)S(1)} %get-tuple-element.137), channel_id=1, source_target_pairs={{4,12},{5,13},{6,14},{7,15},{12,4},{13,5},{14,6},{15,7},{20,28},{2... | collective-permute-start | bytes 393224 | tf_op jit(solution)/shard_map/cond/branch_2_fun/ppermute | solution.py:493
  40.2 2.5 %collective-permute-done.19.sent_ref = bf16[2088,128]{1,0:T(8,128)(2,1)S(1)} collective-permute-done((bf16[2088,128]{1,0:T(8,128)(2,1)S(1)}, bf16[2088,128]{1,0:T(8,128)(2,1)S(1)}, u32[]{:S(2)}, u32[]{:S(2)}) %collective-permute-start.19) | collective-permute-done | bytes 534560 | tf_op jit(solution)/shard_map/cond/branch_2_fun/ppermute | solution.py:493
  42.7 1.6 %merge.22.rest_0_ = bf16[128,4096]{1,0:T(8,128)(2,1)} custom-call(f32[128,4096]{1,0:T(8,128)S(1)} %get-tuple-element.131.mean_ref, f32[128,128]{1,0:T(8,128)S(1)} %get-tuple-element.132._.lse_ref, bf16[2088,128]{1,0:T(8,128)(2,1)S(1)} %collective-permute-done.19.sent_ref), custom_call_target="tpu_custom_call" | custom-call | flops 1048576 | bytes 2097152 | tf_op jit(solution)/shard_map/cond/branch_2_fun/merge/pallas_call | solution.py:369
  44.3 7.1 %collective-permute-done.17.sent_ref = bf16[1576,128]{1,0:T(8,128)(2,1)S(1)} collective-permute-done((bf16[1576,128]{1,0:T(8,128)(2,1)S(1)}, bf16[1576,128]{1,0:T(8,128)(2,1)S(1)}, u32[]{:S(2)}, u32[]{:S(2)}) %collective-permute-start.17) | collective-permute-done | bytes 403488 | tf_op jit(solution)/shard_map/cond/branch_2_fun/ppermute | solution.py:493
  51.4 1.5 %merge.23 = (bf16[128,4096]{1,0:T(8,128)(2,1)}, f32[16,4096]{1,0:T(8,128)S(1)}, f32[16,4096]{1,0:T(8,128)S(1)}) custom-call(f32[128,4096]{1,0:T(8,128)S(1)} %get-tuple-element.131.mean_ref, f32[128,128]{1,0:T(8,128)S(1)} %get-tuple-element.132._.lse_ref, bf16[1576,128]{1,0:T(8,128)(2,1)S(1)} %collective-permute-done.17.sent_ref, ...), custom_call_target="tpu_custom_call", output_to_operand_aliasing={{0}: (3, {})} | custom-call | flops 1048576 | bytes 2097152 | tf_op jit(solution)/shard_map/cond/branch_2_fun/merge/pallas_call | solution.py:369
  52.9 0.4 collective-permute-done.20.sent_ref
  53.3 0.7 %last_merge.11 = bf16[128,4096]{1,0:T(8,128)(2,1)} custom-call(f32[16,4096]{1,0:T(8,128)S(1)} %get-tuple-element.135.scaled_ref, f32[16,4096]{1,0:T(8,128)S(1)} %get-tuple-element.136.share_ref, bf16[512,128]{1,0:T(8,128)(2,1)S(1)} %collective-permute-done.20.sent_ref, bf16[128,4096]{1,0:T(8,128)(2,1)} %get-tuple-element.138._), custom_call_target="tpu_custom_call", output_to_operand_aliasing={{}: (3, {})} | custom-call | tf_op jit(solution)/shard_map/cond/branch_2_fun/last_merge/pallas_call | solution.py:389
Async XLA Ops:
  1.9 8.6 %collective-permute-start.15 = (bf16[128,4096]{1,0:T(8,128)(2,1)}, bf16[128,4096]{1,0:T(8,128)(2,1)S(1)}, u32[]{:S(2)}, u32[]{:S(2)}) collective-permute-start(bf16[128,4096]{1,0:T(8,128)(2,1)} %bitcast.73), channel_id=1, source_target_pairs={{0,1},{1,0},{2,3},{3,2},{4,5},{5,4},{6,7},{7,6},{8,9},{9,8},{10,11... | collective-permute-start | bytes 3145736 | tf_op jit(solution)/shard_map/cond/branch_2_fun/ppermute | solution.py:21
  2.0 8.5 %collective-permute-start.14 = (bf16[128,4096]{1,0:T(8,128)(2,1)}, bf16[128,4096]{1,0:T(8,128)(2,1)S(1)}, u32[]{:S(2)}, u32[]{:S(2)}) collective-permute-start(bf16[128,4096]{1,0:T(8,128)(2,1)} %bitcast.37), channel_id=1, source_target_pairs={{0,1},{1,0},{2,3},{3,2},{4,5},{5,4},{6,7},{7,6},{8,9},{9,8},{10,11... | collective-permute-start | bytes 3145736 | tf_op jit(solution)/shard_map/cond/branch_2_fun/ppermute | solution.py:21
  2.5 17.6 %collective-permute-start.18 = (bf16[64,4096]{1,0:T(8,128)(2,1)S(1)}, bf16[64,4096]{1,0:T(8,128)(2,1)S(1)}, u32[]{:S(2)}, u32[]{:S(2)}) collective-permute-start(bf16[64,4096]{1,0:T(8,128)(2,1)S(1)} %get-tuple-element.134), channel_id=1, source_target_pairs={{4,12},{5,13},{6,14},{7,15},{12,4},{13,5},{14,6},{15,7},{20,28},{2... | collective-permute-start | bytes 1572872 | tf_op jit(solution)/shard_map/cond/branch_2_fun/ppermute | solution.py:480
  8.1 12.0 %copy-start.2 = (bf16[1,16,8,4096]{3,2,1,0:T(8,128)(2,1)S(1)}, bf16[1,16,8,4096]{3,2,1,0:T(8,128)(2,1)}, u32[]{:S(2)}) copy-start(bf16[1,16,8,4096]{3,2,1,0:T(8,128)(2,1)} %get-tuple-element.230) | copy-start | bytes 3145732 | tf_op jit(solution)/shard_map/cond
  8.1 12.0 %copy-start.11 = (bf16[1,16,8,4096]{3,2,1,0:T(8,128)(2,1)S(1)}, bf16[1,16,8,4096]{3,2,1,0:T(8,128)(2,1)}, u32[]{:S(2)}) copy-start(bf16[1,16,8,4096]{3,2,1,0:T(8,128)(2,1)} %get-tuple-element.239) | copy-start | bytes 3145732 | tf_op jit(solution)/shard_map/cond
  8.1 23.2 %collective-permute-start.16 = (bf16[64,4096]{1,0:T(8,128)(2,1)S(1)}, bf16[64,4096]{1,0:T(8,128)(2,1)S(1)}, u32[]{:S(2)}, u32[]{:S(2)}) collective-permute-start(bf16[64,4096]{1,0:T(8,128)(2,1)S(1)} %slice.20), channel_id=1, source_target_pairs={{4,12},{5,13},{6,14},{7,15},{12,4},{13,5},{14,6},{15,7},{20,28},{2... | collective-permute-start | bytes 1572872 | tf_op jit(solution)/shard_map/cond/branch_2_fun/ppermute | solution.py:484
  22.2 20.5 %collective-permute-start.19 = (bf16[2088,128]{1,0:T(8,128)(2,1)S(1)}, bf16[2088,128]{1,0:T(8,128)(2,1)S(1)}, u32[]{:S(2)}, u32[]{:S(2)}) collective-permute-start(bf16[2088,128]{1,0:T(8,128)(2,1)S(1)} %guest_attention.23), channel_id=1, source_target_pairs={{4,12},{5,13},{6,14},{7,15},{12,4},{13,5},{14,6},{15,7},{20,28},{2... | collective-permute-start | bytes 1603592 | tf_op jit(solution)/shard_map/cond/branch_2_fun/ppermute | solution.py:493
  33.5 17.9 %collective-permute-start.17 = (bf16[1576,128]{1,0:T(8,128)(2,1)S(1)}, bf16[1576,128]{1,0:T(8,128)(2,1)S(1)}, u32[]{:S(2)}, u32[]{:S(2)}) collective-permute-start(bf16[1576,128]{1,0:T(8,128)(2,1)S(1)} %get-tuple-element.133), channel_id=1, source_target_pairs={{4,12},{5,13},{6,14},{7,15},{12,4},{13,5},{14,6},{15,7},{20,28},{2... | collective-permute-start | bytes 1210376 | tf_op jit(solution)/shard_map/cond/branch_2_fun/ppermute | solution.py:493
  38.0 15.3 %collective-permute-start.20 = (bf16[512,128]{1,0:T(8,128)(2,1)S(1)}, bf16[512,128]{1,0:T(8,128)(2,1)S(1)}, u32[]{:S(2)}, u32[]{:S(2)}) collective-permute-start(bf16[512,128]{1,0:T(8,128)(2,1)S(1)} %get-tuple-element.137), channel_id=1, source_target_pairs={{4,12},{5,13},{6,14},{7,15},{12,4},{13,5},{14,6},{15,7},{20,28},{2... | collective-permute-start | bytes 393224 | tf_op jit(solution)/shard_map/cond/branch_2_fun/ppermute | solution.py:493

commit v5 on v4

--- a/solution.py
+++ b/solution.py
@@ -181,6 +181,7 @@
 SCALING = HS ** (-0.5)
 LANES = 128
 MARKER = 8
+PIECES = 2
 GROUP = 8
 QUERY_ROWS = (8, 8)
 RETURN_ROWS = ((8,), (6, 2))
@@ -260,7 +261,7 @@
     return pl.ds(pl.multiple_of(head * tokens, tokens), tokens)
 
 
-def guest_kernel(start, query_ref, first_key, second_key, first_value, second_value, _, *sent_refs):
+def guest_kernel(start, matched, query_ref, first_key, second_key, first_value, second_value, _, *sent_refs):
     tokens, width = query_ref.shape
     heads = width // HS
     rows = slice(start, start + tokens)
@@ -292,17 +293,18 @@
     half, at = tokens // 2, heads * sizes[0]
     packed = jnp.where(lane[:half] < LANES // 2, pieces[:half], pieces[half:])
     sent_refs[0][at : at + half, :] = packed.astype(jnp.bfloat16)
-    sent_refs[0][at + half :, :] = jnp.ones((MARKER, LANES), jnp.bfloat16)
-
-
-def guest_attention(query, keys, values, start, sizes, after):
+    marker = jnp.full((MARKER, LANES), matched[0], jnp.int32)
+    sent_refs[0][at + half :, :] = marker.astype(jnp.float32).astype(jnp.bfloat16)
+
+
+def guest_attention(matched, query, keys, values, start, sizes, after):
     tokens, width = query.shape
     heads = width // HS
     lengths = [heads * size for size in sizes]
     lengths[0] += tokens // 2 + MARKER
     return pl.pallas_call(
         functools.partial(guest_kernel, start),
-        in_specs=[IN_VMEM] * 5 + [IN_PLACE],
+        in_specs=[pl.BlockSpec(memory_space=pltpu.SMEM)] + [IN_VMEM] * 5 + [IN_PLACE],
         out_specs=[IN_VMEM] * len(sizes),
         out_shape=[jax.ShapeDtypeStruct((length, LANES), jnp.bfloat16) for length in lengths],
         compiler_params=pltpu.CompilerParams(vmem_limit_bytes=24 * 2**20),
@@ -310,7 +312,7 @@
             flops=8 * tokens * tokens * width, bytes_accessed=12 * tokens * width, transcendentals=0
         ),
         name="guest_attention",
-    )(query, *keys, *values, after)
+    )(matched, query, *keys, *values, after)
 
 
 def merge_kernel(mean_ref, lse_ref, sent_ref, *rest):
@@ -322,8 +324,8 @@
     pieces = sent_ref[at : at + half, :].astype(jnp.float32)
     lse = pieces + pltpu.roll(pieces, LANES - heads, 1)
     lse = jnp.concatenate([lse, pltpu.roll(lse, LANES // 2, 1)], axis=0)
-    received = sent_ref[at + half : at + half + 1, :].astype(jnp.float32) > 0
-    share = 1.0 / (1.0 + jnp.exp(lse_ref[...] - jnp.where(received, lse, NEG_FILL)))
+    matched = sent_ref[at + half : at + half + 1, :].astype(jnp.float32) > 0
+    share = 1.0 / (1.0 + jnp.exp(lse_ref[...] - jnp.where(matched, lse, NEG_FILL)))
 
     def one_group(group, share):
         for inner in range(GROUP):
@@ -409,25 +411,37 @@
     return found
 
 
-def device_pairs(matching, slot_devices):
-    ways = [way for pair in matching for way in (pair, pair[::-1])]
-    return [
-        (source * slot_devices + inner, target * slot_devices + inner)
-        for source, target in ways
-        for inner in range(slot_devices)
-    ]
+def device_pairs(matching, slot_count, slot_devices):
+    other = {slot: slot for slot in range(slot_count)}
+    for one, two in matching:
+        other[one], other[two] = two, one
+    pairs = []
+    for slot in range(slot_count):
+        for inner in range(slot_devices):
+            target = inner if other[slot] != slot else inner ^ 1
+            pairs.append((slot * slot_devices + inner, other[slot] * slot_devices + target))
+    return pairs
 
 
 def prepare(request_of_slot, query, every):
     width = query.shape[1]
     part = QUERY_ROWS[0] * COLS
 
-    def kernel(request_hbm, query_hbm, number_hbm, part_ref, request_ref, number_ref, sems):
+    def kernel(request_hbm, query_hbm, number_hbm, part_hbm, request_ref, number_ref, held, sems):
         asked = pltpu.make_async_copy(request_hbm, request_ref, sems.at[0])
-        taken = pltpu.make_async_copy(query_hbm.at[pl.ds(0, part)], part_ref, sems.at[1])
-        told = pltpu.make_async_copy(number_ref, number_hbm, sems.at[2])
+        told = pltpu.make_async_copy(number_ref, number_hbm, sems.at[1])
+        pieces = [pl.ds(piece * (part // PIECES), part // PIECES) for piece in range(PIECES)]
+        takes = [
+            pltpu.make_async_copy(query_hbm.at[rows], held.at[rows], sems.at[2 + piece])
+            for piece, rows in enumerate(pieces)
+        ]
+        puts = [
+            pltpu.make_async_copy(held.at[rows], part_hbm.at[rows], sems.at[2 + PIECES + piece])
+            for piece, rows in enumerate(pieces)
+        ]
         asked.start()
-        taken.start()
+        for take in takes:
+            take.start()
         asked.wait()
         chosen = jnp.int32(0)
         for number, matching in enumerate(every):
@@ -437,13 +451,17 @@
             chosen = jnp.where(fits, jnp.int32(number), chosen)
         number_ref[0] = chosen
         told.start()
-        taken.wait()
+        for take, put in zip(takes, puts):
+            take.wait()
+            put.start()
+        for put in puts:
+            put.wait()
         told.wait()
 
     number, first_part = pl.pallas_call(
         kernel,
         in_specs=[IN_PLACE] * 2,
-        out_specs=[IN_PLACE, IN_VMEM],
+        out_specs=[IN_PLACE] * 2,
         out_shape=[
             jax.ShapeDtypeStruct((1,), jnp.int32),
             jax.ShapeDtypeStruct((part, width), query.dtype),
@@ -451,7 +469,8 @@
         scratch_shapes=[
             pltpu.SMEM(request_of_slot.shape, jnp.int32),
             pltpu.SMEM((1,), jnp.int32),
-            pltpu.SemaphoreType.DMA((3,)),
+            pltpu.VMEM((part, width), query.dtype),
+            pltpu.SemaphoreType.DMA((2 + 2 * PIECES,)),
         ],
         name="prepare",
     )(request_of_slot, query)
@@ -468,10 +487,12 @@
     key = key_vectors.reshape(token_count, width)
     value = value_vectors.reshape(token_count, width)
     every = [matching for matching in matchings(list(range(slot_count))) if matching]
+    my_slot = lax.axis_index("view") // slot_devices
     branch, first_part = prepare(request_of_slot, query, every)
 
     def exchange(matching):
-        pairs = device_pairs(matching, slot_devices)
+        pairs = device_pairs(matching, slot_count, slot_devices)
+        members = [slot for pair in matching for slot in pair]
 
         def run(key, value, query, first_part):
             return pair_attention(key, value, query, first_part)
@@ -486,10 +507,12 @@
             keys = (key, partner(key, "view", 0))
             values = (value, partner(value, "view", 0))
             mean, lse = own_attention(query, keys, values)
+            matched = functools.reduce(jnp.logical_or, [my_slot == slot for slot in members])
+            matched = matched.astype(jnp.int32).reshape(1)
             returns, start = [], 0
             for guest, rows in zip(guests, RETURN_ROWS):
                 sizes = [row * COLS for row in rows]
-                sent = guest_attention(guest, keys, values, start, sizes, lse)
+                sent = guest_attention(matched, guest, keys, values, start, sizes, lse)
                 backs = [lax.ppermute(part, "view", pairs) for part in sent]
                 returns.append((backs, start, sizes))
                 start += guest.shape[0]

time: 54.3 us -> 53.1 us (0.978)
  starting transfers between devices: 18.7 us -> 9.15 us
  waiting for transfers between devices: 19.6 us -> 26.6 us
  local copies, waits for them, and re-layouts: 1.09 us -> 1.87 us
  Pallas kernels: 13.9 us -> 14.6 us
    ppermute x3, starting transfers between devices: 11.2 us -> 5.65 us  [pair_attention(): backs = [lax.ppermute(part, 'view', pairs) for part in sent]]
    ppermute x3, waiting for transfers between devices: 10 us -> 13.8 us  [pair_attention(): backs = [lax.ppermute(part, 'view', pairs) for part in sent]]
    ppermute x1, starting transfers between devices: 2.38 us -> 0.34 us  [pair_attention(): guests.append(lax.ppermute(sent, 'view', pairs))]
    ppermute x1, starting transfers between devices: 4.49 us -> 2.59 us  [pair_attention(): guests = [lax.ppermute(first_part, 'view', pairs)]]
    ppermute x1, waiting for transfers between devices: 4.54 us -> 6.39 us  [pair_attention(): guests.append(lax.ppermute(sent, 'view', pairs))]
    ppermute x1, waiting for transfers between devices: 5.02 us -> 6.4 us  [pair_attention(): guests = [lax.ppermute(first_part, 'view', pairs)]]
    slice x1, local copies, waits for them, and re-layouts: 1.08 us -> 1.87 us  [pair_attention(): sent = lax.slice_in_dim(query, start, start + rows * COLS)]
    pallas_call x3, Pallas kernels: 5.56 us -> 6.17 us  [the longest x2 4.35 us: guest_attention(): pl.pallas_call(functools.partial(guest_kernel, start), in_specs=[pl.Block...]
  transfers between devices with their start and end apart: 7 -> 7, of which waited for: 5 -> 5; matrix products, arithmetic and copies ran while one was open for 2% -> 4% of each run, Pallas kernels for 22% -> 23%
where the time goes in v5:
time: 53.1 us; the launch traced here: 52.9 us
  waiting for transfers between devices  26.6 us (50%)
  Pallas kernels  14.6 us (27%)
  starting transfers between devices  9.15 us (17%)
  local copies, waits for them, and re-layouts  1.87 us (4%)
  between operations  0.66 us (1%)
    ppermute x3, waiting for transfers between devices, pair_attention(): backs = [lax.ppermute(part, 'view', pairs) for part in sent]  13.8 us
    ppermute x1, waiting for transfers between devices, pair_attention(): guests = [lax.ppermute(first_part, 'view', pairs)]  6.4 us
    ppermute x1, waiting for transfers between devices, pair_attention(): guests.append(lax.ppermute(sent, 'view', pairs))  6.39 us
    ppermute x3, starting transfers between devices, pair_attention(): backs = [lax.ppermute(part, 'view', pairs) for part in sent]  5.65 us
    pallas_call x1, Pallas kernels, own_attention(): pl.pallas_call(own_kernel, out_shape=[jax.ShapeDtypeStruct((tokens, width...  4.69 us
    pallas_call x2, Pallas kernels, guest_attention(): pl.pallas_call(functools.partial(guest_kernel, start), in_specs=[pl.Block...  4.35 us
    pallas_call x2, Pallas kernels, merge(): pl.pallas_call(merge_kernel, grid=(1,), in_specs=[token_rows(start, token...  3.08 us
    ppermute x1, starting transfers between devices, pair_attention(): guests = [lax.ppermute(first_part, 'view', pairs)]  2.59 us
  transfers between devices with their start and end apart: 7, of which 5 were waited for; matrix products, arithmetic and copies ran while one was open for 4% of the time, Pallas kernels for 23%

profile of v5, /device:TPU:10, one launch (start us, length us, event | category | flops | bytes accessed | tf_op | source)
XLA Modules:
  0.0 52.9 jit_solution(2190147008097049369)
XLA Ops:
  0.0 1.8 %prepare.1 = (s32[1]{0:T(128)}, bf16[64,4096]{1,0:T(8,128)(2,1)}) custom-call(s32[4]{0:T(128)} %request_hbm.1, bf16[128,4096]{1,0:T(8,128)(2,1)} %bitcast.110), custom_call_target="tpu_custom_call" | custom-call | tf_op jit(solution)/shard_map/prepare/pallas_call | solution.py:461
  2.5 50.5 %conditional.1 = (bf16[1,16,8,4096]{3,2,1,0:T(8,128)(2,1)}) conditional(s32[]{:T(128)} %bitcast.37, (bf16[1,16,8,4096]{3,2,1,0:T(8,128)(2,1)}, bf16[1,16,8,4096]{3,2,1,0:T(8,128)(2,1)}, bf16[128,4096]{1,0:T(8,128)(2,1)}, s32[]{:T(128)}, s32[]{:T(128)}, /*index=5*/bf16[64,4096]{1,0:T(8,128)(2,1)}, ()) %tuple.119, ...), branch_computations={%region_0.1_spmd, %region_1.2_spmd, %region_2.3_spmd, %region_3.4_... | conditional | flops 807403520 | bytes 44122656 | solution.py:527
  2.5 0.1 collective-permute-start.14
  2.6 0.5 collective-permute-start.15
  3.1 2.6 %collective-permute-start.18 = (bf16[64,4096]{1,0:T(8,128)(2,1)}, bf16[64,4096]{1,0:T(8,128)(2,1)S(1)}, u32[]{:S(2)}, u32[]{:S(2)}) collective-permute-start(bf16[64,4096]{1,0:T(8,128)(2,1)} %get-tuple-element.419), channel_id=1, source_target_pairs={{0,1},{1,0},{2,3},{3,2},{4,12},{5,13},{6,14},{7,15},{8,9},{9,8},{1... | collective-permute-start | bytes 1572872 | tf_op jit(solution)/shard_map/cond/branch_2_fun/ppermute | solution.py:501
  5.7 1.9 %slice.20 = bf16[64,4096]{1,0:T(8,128)(2,1)} slice(bf16[128,4096]{1,0:T(8,128)(2,1)} %get-tuple-element.411.query_ref), slice={[64:128], [0:4096]} | slice | bytes 1048576 | tf_op jit(solution)/shard_map/cond/branch_2_fun/slice | solution.py:504
  7.5 0.3 collective-permute-start.16
  7.9 0.0 copy-start.2
  7.9 0.0 copy-start.11
  7.9 0.0 collective-permute-done.14.second_key
  7.9 0.0 collective-permute-done.15.second_value
  7.9 4.7 %own_attention.11 = (f32[128,4096]{1,0:T(8,128)S(1)}, f32[128,128]{1,0:T(8,128)S(1)}) custom-call(bf16[128,4096]{1,0:T(8,128)(2,1)} %get-tuple-element.411.query_ref, bf16[128,4096]{1,0:T(8,128)(2,1)} %bitcast.47, bf16[128,4096]{1,0:T(8,128)(2,1)S(1)} %collective-permute-done.14.second_key, bf16[128,4096]{1,0:T(8,128)(2,1)} %bitcast.83, ...), custom_call_target="tpu_custom_call" | custom-call | flops 536870912 | bytes 7340032 | tf_op jit(solution)/shard_map/cond/branch_2_fun/own_attention/pallas_call | solution.py:246
  12.6 6.4 %collective-permute-done.18.query_ref = bf16[64,4096]{1,0:T(8,128)(2,1)S(1)} collective-permute-done((bf16[64,4096]{1,0:T(8,128)(2,1)}, bf16[64,4096]{1,0:T(8,128)(2,1)S(1)}, u32[]{:S(2)}, u32[]{:S(2)}) %collective-permute-start.18) | collective-permute-done | bytes 524320 | tf_op jit(solution)/shard_map/cond/branch_2_fun/ppermute | solution.py:501
  19.0 0.0 copy-done.2
  19.0 0.0 copy-done.11
  19.0 2.2 %guest_attention.23 = bf16[2088,128]{1,0:T(8,128)(2,1)S(1)} custom-call(s32[1]{0:T(128)} %bitcast.10.matched, bf16[64,4096]{1,0:T(8,128)(2,1)S(1)} %collective-permute-done.18.query_ref, bf16[128,4096]{1,0:T(8,128)(2,1)S(1)} %bitcast.48, bf16[128,4096]{1,0:T(8,128)(2,1)S(1)} %collective-permute-done.14.second_key, bf16[128,4096]{1,0:T(8,128)(2,1)S(1)} %bitcast.84, ...), custom_call_target="tpu_custom_call" | custom-call | flops 134217728 | bytes 3145728 | tf_op jit(solution)/shard_map/cond/branch_2_fun/guest_attention/pallas_call | solution.py:305
  21.2 2.7 %collective-permute-start.19 = (bf16[2088,128]{1,0:T(8,128)(2,1)S(1)}, bf16[2088,128]{1,0:T(8,128)(2,1)S(1)}, u32[]{:S(2)}, u32[]{:S(2)}) collective-permute-start(bf16[2088,128]{1,0:T(8,128)(2,1)S(1)} %guest_attention.23), channel_id=1, source_target_pairs={{0,1},{1,0},{2,3},{3,2},{4,12},{5,13},{6,14},{7,15},{8,9},{9,8},{1... | collective-permute-start | bytes 1603592 | tf_op jit(solution)/shard_map/cond/branch_2_fun/ppermute | solution.py:516
  23.8 6.4 %collective-permute-done.16.query_ref = bf16[64,4096]{1,0:T(8,128)(2,1)S(1)} collective-permute-done((bf16[64,4096]{1,0:T(8,128)(2,1)}, bf16[64,4096]{1,0:T(8,128)(2,1)S(1)}, u32[]{:S(2)}, u32[]{:S(2)}) %collective-permute-start.16) | collective-permute-done | bytes 524320 | tf_op jit(solution)/shard_map/cond/branch_2_fun/ppermute | solution.py:505
  30.2 2.2 %guest_attention.22 = (bf16[1576,128]{1,0:T(8,128)(2,1)S(1)}, bf16[512,128]{1,0:T(8,128)(2,1)S(1)}) custom-call(s32[1]{0:T(128)} %bitcast.10.matched, bf16[64,4096]{1,0:T(8,128)(2,1)S(1)} %collective-permute-done.16.query_ref, bf16[128,4096]{1,0:T(8,128)(2,1)S(1)} %bitcast.49, bf16[128,4096]{1,0:T(8,128)(2,1)S(1)} %collective-permute-done.14.second_key, ...), custom_call_target="tpu_custom_call" | custom-call | flops 134217728 | bytes 3145728 | tf_op jit(solution)/shard_map/cond/branch_2_fun/guest_attention/pallas_call | solution.py:305
  32.4 2.7 %collective-permute-start.17 = (bf16[1576,128]{1,0:T(8,128)(2,1)S(1)}, bf16[1576,128]{1,0:T(8,128)(2,1)S(1)}, u32[]{:S(2)}, u32[]{:S(2)}) collective-permute-start(bf16[1576,128]{1,0:T(8,128)(2,1)S(1)} %get-tuple-element.418), channel_id=1, source_target_pairs={{0,1},{1,0},{2,3},{3,2},{4,12},{5,13},{6,14},{7,15},{8,9},{9,8},{1... | collective-permute-start | bytes 1210376 | tf_op jit(solution)/shard_map/cond/branch_2_fun/ppermute | solution.py:516
  35.1 0.3 collective-permute-start.20
  35.4 6.3 %collective-permute-done.19.sent_ref = bf16[2088,128]{1,0:T(8,128)(2,1)S(1)} collective-permute-done((bf16[2088,128]{1,0:T(8,128)(2,1)S(1)}, bf16[2088,128]{1,0:T(8,128)(2,1)S(1)}, u32[]{:S(2)}, u32[]{:S(2)}) %collective-permute-start.19) | collective-permute-done | bytes 534560 | tf_op jit(solution)/shard_map/cond/branch_2_fun/ppermute | solution.py:516
  41.7 1.6 %merge.22.rest_0_ = bf16[128,4096]{1,0:T(8,128)(2,1)} custom-call(f32[128,4096]{1,0:T(8,128)S(1)} %get-tuple-element.414.mean_ref, f32[128,128]{1,0:T(8,128)S(1)} %get-tuple-element.415._.lse_ref, bf16[2088,128]{1,0:T(8,128)(2,1)S(1)} %collective-permute-done.19.sent_ref), custom_call_target="tpu_custom_call" | custom-call | flops 1048576 | bytes 2097152 | tf_op jit(solution)/shard_map/cond/branch_2_fun/merge/pallas_call | solution.py:371
  43.2 7.1 %collective-permute-done.17.sent_ref = bf16[1576,128]{1,0:T(8,128)(2,1)S(1)} collective-permute-done((bf16[1576,128]{1,0:T(8,128)(2,1)S(1)}, bf16[1576,128]{1,0:T(8,128)(2,1)S(1)}, u32[]{:S(2)}, u32[]{:S(2)}) %collective-permute-start.17) | collective-permute-done | bytes 403488 | tf_op jit(solution)/shard_map/cond/branch_2_fun/ppermute | solution.py:516
  50.3 1.5 %merge.23 = (bf16[128,4096]{1,0:T(8,128)(2,1)}, f32[16,4096]{1,0:T(8,128)S(1)}, f32[16,4096]{1,0:T(8,128)S(1)}) custom-call(f32[128,4096]{1,0:T(8,128)S(1)} %get-tuple-element.414.mean_ref, f32[128,128]{1,0:T(8,128)S(1)} %get-tuple-element.415._.lse_ref, bf16[1576,128]{1,0:T(8,128)(2,1)S(1)} %collective-permute-done.17.sent_ref, ...), custom_call_target="tpu_custom_call", output_to_operand_aliasing={{0}: (3, {})} | custom-call | flops 1048576 | bytes 2097152 | tf_op jit(solution)/shard_map/cond/branch_2_fun/merge/pallas_call | solution.py:371
  51.9 0.4 collective-permute-done.20.sent_ref
  52.2 0.7 %last_merge.11 = bf16[128,4096]{1,0:T(8,128)(2,1)} custom-call(f32[16,4096]{1,0:T(8,128)S(1)} %get-tuple-element.420.scaled_ref, f32[16,4096]{1,0:T(8,128)S(1)} %get-tuple-element.421.share_ref, bf16[512,128]{1,0:T(8,128)(2,1)S(1)} %collective-permute-done.20.sent_ref, bf16[128,4096]{1,0:T(8,128)(2,1)} %get-tuple-element.423._), custom_call_target="tpu_custom_call", output_to_operand_aliasing={{}: (3, {})} | custom-call | tf_op jit(solution)/shard_map/cond/branch_2_fun/last_merge/pallas_call | solution.py:391
Async XLA Ops:
  2.5 5.4 %collective-permute-start.14 = (bf16[128,4096]{1,0:T(8,128)(2,1)}, bf16[128,4096]{1,0:T(8,128)(2,1)S(1)}, u32[]{:S(2)}, u32[]{:S(2)}) collective-permute-start(bf16[128,4096]{1,0:T(8,128)(2,1)} %bitcast.46), channel_id=1, source_target_pairs={{0,1},{1,0},{2,3},{3,2},{4,5},{5,4},{6,7},{7,6},{8,9},{9,8},{10,11... | collective-permute-start | bytes 3145736 | tf_op jit(solution)/shard_map/cond/branch_2_fun/ppermute | solution.py:21
  2.6 5.3 %collective-permute-start.15 = (bf16[128,4096]{1,0:T(8,128)(2,1)}, bf16[128,4096]{1,0:T(8,128)(2,1)S(1)}, u32[]{:S(2)}, u32[]{:S(2)}) collective-permute-start(bf16[128,4096]{1,0:T(8,128)(2,1)} %bitcast.82), channel_id=1, source_target_pairs={{0,1},{1,0},{2,3},{3,2},{4,5},{5,4},{6,7},{7,6},{8,9},{9,8},{10,11... | collective-permute-start | bytes 3145736 | tf_op jit(solution)/shard_map/cond/branch_2_fun/ppermute | solution.py:21
  3.1 15.9 %collective-permute-start.18 = (bf16[64,4096]{1,0:T(8,128)(2,1)}, bf16[64,4096]{1,0:T(8,128)(2,1)S(1)}, u32[]{:S(2)}, u32[]{:S(2)}) collective-permute-start(bf16[64,4096]{1,0:T(8,128)(2,1)} %get-tuple-element.419), channel_id=1, source_target_pairs={{0,1},{1,0},{2,3},{3,2},{4,12},{5,13},{6,14},{7,15},{8,9},{9,8},{1... | collective-permute-start | bytes 1572872 | tf_op jit(solution)/shard_map/cond/branch_2_fun/ppermute | solution.py:501
  7.5 22.7 %collective-permute-start.16 = (bf16[64,4096]{1,0:T(8,128)(2,1)}, bf16[64,4096]{1,0:T(8,128)(2,1)S(1)}, u32[]{:S(2)}, u32[]{:S(2)}) collective-permute-start(bf16[64,4096]{1,0:T(8,128)(2,1)} %slice.20), channel_id=1, source_target_pairs={{0,1},{1,0},{2,3},{3,2},{4,12},{5,13},{6,14},{7,15},{8,9},{9,8},{1... | collective-permute-start | bytes 1572872 | tf_op jit(solution)/shard_map/cond/branch_2_fun/ppermute | solution.py:505
  7.9 11.1 %copy-start.2 = (bf16[1,16,8,4096]{3,2,1,0:T(8,128)(2,1)S(1)}, bf16[1,16,8,4096]{3,2,1,0:T(8,128)(2,1)}, u32[]{:S(2)}) copy-start(bf16[1,16,8,4096]{3,2,1,0:T(8,128)(2,1)} %get-tuple-element.545) | copy-start | bytes 3145732 | tf_op jit(solution)/shard_map/cond
  7.9 11.1 %copy-start.11 = (bf16[1,16,8,4096]{3,2,1,0:T(8,128)(2,1)S(1)}, bf16[1,16,8,4096]{3,2,1,0:T(8,128)(2,1)}, u32[]{:S(2)}) copy-start(bf16[1,16,8,4096]{3,2,1,0:T(8,128)(2,1)} %get-tuple-element.554) | copy-start | bytes 3145732 | tf_op jit(solution)/shard_map/cond
  21.2 20.5 %collective-permute-start.19 = (bf16[2088,128]{1,0:T(8,128)(2,1)S(1)}, bf16[2088,128]{1,0:T(8,128)(2,1)S(1)}, u32[]{:S(2)}, u32[]{:S(2)}) collective-permute-start(bf16[2088,128]{1,0:T(8,128)(2,1)S(1)} %guest_attention.23), channel_id=1, source_target_pairs={{0,1},{1,0},{2,3},{3,2},{4,12},{5,13},{6,14},{7,15},{8,9},{9,8},{1... | collective-permute-start | bytes 1603592 | tf_op jit(solution)/shard_map/cond/branch_2_fun/ppermute | solution.py:516
  32.4 17.9 %collective-permute-start.17 = (bf16[1576,128]{1,0:T(8,128)(2,1)S(1)}, bf16[1576,128]{1,0:T(8,128)(2,1)S(1)}, u32[]{:S(2)}, u32[]{:S(2)}) collective-permute-start(bf16[1576,128]{1,0:T(8,128)(2,1)S(1)} %get-tuple-element.418), channel_id=1, source_target_pairs={{0,1},{1,0},{2,3},{3,2},{4,12},{5,13},{6,14},{7,15},{8,9},{9,8},{1... | collective-permute-start | bytes 1210376 | tf_op jit(solution)/shard_map/cond/branch_2_fun/ppermute | solution.py:516
  35.1 17.2 %collective-permute-start.20 = (bf16[512,128]{1,0:T(8,128)(2,1)S(1)}, bf16[512,128]{1,0:T(8,128)(2,1)S(1)}, u32[]{:S(2)}, u32[]{:S(2)}) collective-permute-start(bf16[512,128]{1,0:T(8,128)(2,1)S(1)} %get-tuple-element.422), channel_id=1, source_target_pairs={{0,1},{1,0},{2,3},{3,2},{4,12},{5,13},{6,14},{7,15},{8,9},{9,8},{1... | collective-permute-start | bytes 393224 | tf_op jit(solution)/shard_map/cond/branch_2_fun/ppermute | solution.py:516

commit v6 on v5

--- a/solution.py
+++ b/solution.py
@@ -181,7 +181,6 @@
 SCALING = HS ** (-0.5)
 LANES = 128
 MARKER = 8
-PIECES = 2
 GROUP = 8
 QUERY_ROWS = (8, 8)
 RETURN_ROWS = ((8,), (6, 2))
@@ -424,24 +423,18 @@
 
 
 def prepare(request_of_slot, query, every):
-    width = query.shape[1]
+    slot_count, width = request_of_slot.shape[0], query.shape[1]
     part = QUERY_ROWS[0] * COLS
-
-    def kernel(request_hbm, query_hbm, number_hbm, part_hbm, request_ref, number_ref, held, sems):
+    slot_devices = lax.axis_size("view") // slot_count
+
+    def kernel(request_hbm, query_hbm, number_hbm, matched_hbm, part_ref, request_ref, numbers, matched, sems):
         asked = pltpu.make_async_copy(request_hbm, request_ref, sems.at[0])
-        told = pltpu.make_async_copy(number_ref, number_hbm, sems.at[1])
-        pieces = [pl.ds(piece * (part // PIECES), part // PIECES) for piece in range(PIECES)]
-        takes = [
-            pltpu.make_async_copy(query_hbm.at[rows], held.at[rows], sems.at[2 + piece])
-            for piece, rows in enumerate(pieces)
-        ]
-        puts = [
-            pltpu.make_async_copy(held.at[rows], part_hbm.at[rows], sems.at[2 + PIECES + piece])
-            for piece, rows in enumerate(pieces)
-        ]
+        taken = pltpu.make_async_copy(query_hbm.at[pl.ds(0, part)], part_ref, sems.at[1])
+        told = pltpu.make_async_copy(numbers, number_hbm, sems.at[2])
+        noted = pltpu.make_async_copy(matched, matched_hbm, sems.at[3])
         asked.start()
-        for take in takes:
-            take.start()
+        taken.start()
+        my_slot = lax.axis_index("view") // slot_devices
         asked.wait()
         chosen = jnp.int32(0)
         for number, matching in enumerate(every):
@@ -449,32 +442,34 @@
                 jnp.logical_and, [request_ref[one] == request_ref[other] for one, other in matching]
             )
             chosen = jnp.where(fits, jnp.int32(number), chosen)
-        number_ref[0] = chosen
+        numbers[0] = chosen
         told.start()
-        for take, put in zip(takes, puts):
-            take.wait()
-            put.start()
-        for put in puts:
-            put.wait()
+        mine = request_ref[my_slot]
+        sharing = [(request_ref[slot] == mine).astype(jnp.int32) for slot in range(slot_count)]
+        matched[0] = sum(sharing) - 1
+        noted.start()
+        taken.wait()
         told.wait()
-
-    number, first_part = pl.pallas_call(
+        noted.wait()
+
+    number, matched, first_part = pl.pallas_call(
         kernel,
         in_specs=[IN_PLACE] * 2,
-        out_specs=[IN_PLACE] * 2,
+        out_specs=[IN_PLACE, IN_PLACE, IN_VMEM],
         out_shape=[
+            jax.ShapeDtypeStruct((1,), jnp.int32),
             jax.ShapeDtypeStruct((1,), jnp.int32),
             jax.ShapeDtypeStruct((part, width), query.dtype),
         ],
         scratch_shapes=[
             pltpu.SMEM(request_of_slot.shape, jnp.int32),
             pltpu.SMEM((1,), jnp.int32),
-            pltpu.VMEM((part, width), query.dtype),
-            pltpu.SemaphoreType.DMA((2 + 2 * PIECES,)),
+            pltpu.SMEM((1,), jnp.int32),
+            pltpu.SemaphoreType.DMA((4,)),
         ],
         name="prepare",
     )(request_of_slot, query)
-    return number[0], first_part
+    return number[0], matched, first_part
 
 
 def few_slots(query_vectors, key_vectors, value_vectors, request_of_slot):
@@ -487,17 +482,15 @@
     key = key_vectors.reshape(token_count, width)
     value = value_vectors.reshape(token_count, width)
     every = [matching for matching in matchings(list(range(slot_count))) if matching]
-    my_slot = lax.axis_index("view") // slot_devices
-    branch, first_part = prepare(request_of_slot, query, every)
+    branch, matched, first_part = prepare(request_of_slot, query, every)
 
     def exchange(matching):
         pairs = device_pairs(matching, slot_count, slot_devices)
-        members = [slot for pair in matching for slot in pair]
-
-        def run(key, value, query, first_part):
-            return pair_attention(key, value, query, first_part)
-
-        def pair_attention(key, value, query, first_part):
+
+        def run(key, value, query, first_part, matched):
+            return pair_attention(key, value, query, first_part, matched)
+
+        def pair_attention(key, value, query, first_part, matched):
             guests = [lax.ppermute(first_part, "view", pairs)]
             start = first_part.shape[0]
             for rows in QUERY_ROWS[1:]:
@@ -507,8 +500,6 @@
             keys = (key, partner(key, "view", 0))
             values = (value, partner(value, "view", 0))
             mean, lse = own_attention(query, keys, values)
-            matched = functools.reduce(jnp.logical_or, [my_slot == slot for slot in members])
-            matched = matched.astype(jnp.int32).reshape(1)
             returns, start = [], 0
             for guest, rows in zip(guests, RETURN_ROWS):
                 sizes = [row * COLS for row in rows]
@@ -524,7 +515,7 @@
         return run
 
     branches = [exchange(matching) for matching in every]
-    attended = lax.switch(branch, branches, key, value, query, first_part)
+    attended = lax.switch(branch, branches, key, value, query, first_part, matched)
     return attended.reshape(1, ROWS, COLS, HEADS * HS)
 
 

time: 53.1 us -> 52.4 us (0.987)
  waiting for transfers between devices: 26.6 us -> 25.7 us
  Pallas kernels: 14.6 us -> 15.4 us
  local copies, waits for them, and re-layouts: 1.87 us -> 1.09 us
    pallas_call x2, Pallas kernels: 4.35 us -> 5.62 us  [guest_attention(): pl.pallas_call(functools.partial(guest_kernel, start), in_specs=[pl.Block...]
    slice x1, local copies, waits for them, and re-layouts: 1.87 us -> 1.08 us  [pair_attention(): sent = lax.slice_in_dim(query, start, start + rows * COLS)]
    ppermute x1, waiting for transfers between devices: 6.39 us -> 5.75 us  [pair_attention(): guests.append(lax.ppermute(sent, 'view', pairs))]
    ppermute x3, waiting for transfers between devices: 13.8 us -> 13.1 us  [pair_attention(): backs = [lax.ppermute(part, 'view', pairs) for part in sent]]
    pallas_call x1, Pallas kernels: 1.82 us -> 1.23 us  [prepare(): pl.pallas_call(kernel, in_specs=[IN_PLACE] * 2, out_specs=[IN_PLACE, IN_P...]
  transfers between devices with their start and end apart: 7 -> 7, of which waited for: 5 -> 5; matrix products, arithmetic and copies ran while one was open for 4% -> 2% of each run, Pallas kernels for 23% -> 26%
where the time goes in v6:
time: 52.4 us; the launch traced here: 52.1 us
  waiting for transfers between devices  25.7 us (49%)
  Pallas kernels  15.4 us (29%)
  starting transfers between devices  9.2 us (18%)
  local copies, waits for them, and re-layouts  1.09 us (2%)
  between operations  0.66 us (1%)
    ppermute x3, waiting for transfers between devices, pair_attention(): backs = [lax.ppermute(part, 'view', pairs) for part in sent]  13.1 us
    ppermute x1, waiting for transfers between devices, pair_attention(): guests = [lax.ppermute(first_part, 'view', pairs)]  6.85 us
    ppermute x1, waiting for transfers between devices, pair_attention(): guests.append(lax.ppermute(sent, 'view', pairs))  5.75 us
    ppermute x3, starting transfers between devices, pair_attention(): backs = [lax.ppermute(part, 'view', pairs) for part in sent]  5.65 us
    pallas_call x2, Pallas kernels, guest_attention(): pl.pallas_call(functools.partial(guest_kernel, start), in_specs=[pl.Block...  5.62 us
    pallas_call x1, Pallas kernels, own_attention(): pl.pallas_call(own_kernel, out_shape=[jax.ShapeDtypeStruct((tokens, width...  4.74 us
    pallas_call x2, Pallas kernels, merge(): pl.pallas_call(merge_kernel, grid=(1,), in_specs=[token_rows(start, token...  3.08 us
    ppermute x1, starting transfers between devices, pair_attention(): guests = [lax.ppermute(first_part, 'view', pairs)]  2.59 us
  transfers between devices with their start and end apart: 7, of which 5 were waited for; matrix products, arithmetic and copies ran while one was open for 2% of the time, Pallas kernels for 26%

profile of v6, /device:TPU:10, one launch (start us, length us, event | category | flops | bytes accessed | tf_op | source)
XLA Modules:
  0.0 52.1 jit_solution(6928002607626598099)
XLA Ops:
  0.0 1.2 %prepare.1 = (s32[1]{0:T(128)}, s32[1]{0:T(128)}, bf16[64,4096]{1,0:T(8,128)(2,1)S(1)}) custom-call(s32[4]{0:T(128)} %request_hbm.1, bf16[128,4096]{1,0:T(8,128)(2,1)} %bitcast.101), custom_call_target="tpu_custom_call" | custom-call | tf_op jit(solution)/shard_map/prepare/pallas_call | solution.py:455
  1.9 50.3 %conditional.1 = (bf16[1,16,8,4096]{3,2,1,0:T(8,128)(2,1)}) conditional(s32[]{:T(128)} %bitcast.28, (bf16[1,16,8,4096]{3,2,1,0:T(8,128)(2,1)}, bf16[1,16,8,4096]{3,2,1,0:T(8,128)(2,1)}, bf16[128,4096]{1,0:T(8,128)(2,1)}, s32[1]{0:T(128)}, bf16[64,4096]{1,0:T(8,128)(2,1)S(1)}) %tuple.60, ...), branch_computations={%region_0.0_spmd, %region_1.0_spmd, %region_2.0_spmd, %region_3.0_... | conditional | flops 807403520 | bytes 44122456 | solution.py:518
  1.9 0.1 collective-permute-start.15
  2.0 0.5 collective-permute-start.14
  2.5 2.6 %collective-permute-start.18 = (bf16[64,4096]{1,0:T(8,128)(2,1)S(1)}, bf16[64,4096]{1,0:T(8,128)(2,1)S(1)}, u32[]{:S(2)}, u32[]{:S(2)}) collective-permute-start(bf16[64,4096]{1,0:T(8,128)(2,1)S(1)} %get-tuple-element.155), channel_id=1, source_target_pairs={{0,1},{1,0},{2,3},{3,2},{4,12},{5,13},{6,14},{7,15},{8,9},{9,8},{1... | collective-permute-start | bytes 1572872 | tf_op jit(solution)/shard_map/cond/branch_2_fun/ppermute | solution.py:494
  5.1 1.1 %slice.20 = bf16[64,4096]{1,0:T(8,128)(2,1)S(1)} slice(bf16[128,4096]{1,0:T(8,128)(2,1)} %get-tuple-element.148.query_ref), slice={[64:128], [0:4096]} | slice | bytes 1048576 | tf_op jit(solution)/shard_map/cond/branch_2_fun/slice | solution.py:497
  6.2 0.0 copy-start.2
  6.2 0.0 copy-start.11
  6.2 0.4 collective-permute-start.16
  6.6 0.0 collective-permute-done.15.second_value
  6.6 0.0 collective-permute-done.14.second_key
  6.6 4.7 %own_attention.11 = (f32[128,4096]{1,0:T(8,128)S(1)}, f32[128,128]{1,0:T(8,128)S(1)}) custom-call(bf16[128,4096]{1,0:T(8,128)(2,1)} %get-tuple-element.148.query_ref, bf16[128,4096]{1,0:T(8,128)(2,1)} %bitcast.38, bf16[128,4096]{1,0:T(8,128)(2,1)S(1)} %collective-permute-done.14.second_key, bf16[128,4096]{1,0:T(8,128)(2,1)} %bitcast.74, ...), custom_call_target="tpu_custom_call" | custom-call | flops 536870912 | bytes 7340032 | tf_op jit(solution)/shard_map/cond/branch_2_fun/own_attention/pallas_call | solution.py:245
  11.3 6.8 %collective-permute-done.18.query_ref = bf16[64,4096]{1,0:T(8,128)(2,1)S(1)} collective-permute-done((bf16[64,4096]{1,0:T(8,128)(2,1)S(1)}, bf16[64,4096]{1,0:T(8,128)(2,1)S(1)}, u32[]{:S(2)}, u32[]{:S(2)}) %collective-permute-start.18) | collective-permute-done | bytes 524320 | tf_op jit(solution)/shard_map/cond/branch_2_fun/ppermute | solution.py:494
  18.2 0.0 copy-done.2
  18.2 0.0 copy-done.11
  18.2 2.8 %guest_attention.23 = bf16[2088,128]{1,0:T(8,128)(2,1)S(1)} custom-call(s32[1]{0:T(128)} %get-tuple-element.153.matched, bf16[64,4096]{1,0:T(8,128)(2,1)S(1)} %collective-permute-done.18.query_ref, bf16[128,4096]{1,0:T(8,128)(2,1)S(1)} %bitcast.39, bf16[128,4096]{1,0:T(8,128)(2,1)S(1)} %collective-permute-done.14.second_key, bf16[128,4096]{1,0:T(8,128)(2,1)S(1)} %bitcast.75, ...), custom_call_target="tpu_custom_call" | custom-call | flops 134217728 | bytes 3145728 | tf_op jit(solution)/shard_map/cond/branch_2_fun/guest_attention/pallas_call | solution.py:304
  21.0 2.7 %collective-permute-start.19 = (bf16[2088,128]{1,0:T(8,128)(2,1)S(1)}, bf16[2088,128]{1,0:T(8,128)(2,1)S(1)}, u32[]{:S(2)}, u32[]{:S(2)}) collective-permute-start(bf16[2088,128]{1,0:T(8,128)(2,1)S(1)} %guest_attention.23), channel_id=1, source_target_pairs={{0,1},{1,0},{2,3},{3,2},{4,12},{5,13},{6,14},{7,15},{8,9},{9,8},{1... | collective-permute-start | bytes 1603592 | tf_op jit(solution)/shard_map/cond/branch_2_fun/ppermute | solution.py:507
  23.7 5.8 %collective-permute-done.16.query_ref = bf16[64,4096]{1,0:T(8,128)(2,1)S(1)} collective-permute-done((bf16[64,4096]{1,0:T(8,128)(2,1)S(1)}, bf16[64,4096]{1,0:T(8,128)(2,1)S(1)}, u32[]{:S(2)}, u32[]{:S(2)}) %collective-permute-start.16) | collective-permute-done | bytes 524320 | tf_op jit(solution)/shard_map/cond/branch_2_fun/ppermute | solution.py:498
  29.4 2.8 %guest_attention.22 = (bf16[1576,128]{1,0:T(8,128)(2,1)S(1)}, bf16[512,128]{1,0:T(8,128)(2,1)S(1)}) custom-call(s32[1]{0:T(128)} %get-tuple-element.153.matched, bf16[64,4096]{1,0:T(8,128)(2,1)S(1)} %collective-permute-done.16.query_ref, bf16[128,4096]{1,0:T(8,128)(2,1)S(1)} %bitcast.40, bf16[128,4096]{1,0:T(8,128)(2,1)S(1)} %collective-permute-done.14.second_key, ...), custom_call_target="tpu_custom_call" | custom-call | flops 134217728 | bytes 3145728 | tf_op jit(solution)/shard_map/cond/branch_2_fun/guest_attention/pallas_call | solution.py:304
  32.2 2.7 %collective-permute-start.17 = (bf16[1576,128]{1,0:T(8,128)(2,1)S(1)}, bf16[1576,128]{1,0:T(8,128)(2,1)S(1)}, u32[]{:S(2)}, u32[]{:S(2)}) collective-permute-start(bf16[1576,128]{1,0:T(8,128)(2,1)S(1)} %get-tuple-element.154), channel_id=1, source_target_pairs={{0,1},{1,0},{2,3},{3,2},{4,12},{5,13},{6,14},{7,15},{8,9},{9,8},{1... | collective-permute-start | bytes 1210376 | tf_op jit(solution)/shard_map/cond/branch_2_fun/ppermute | solution.py:507
  34.9 0.3 collective-permute-start.20
  35.2 5.6 %collective-permute-done.19.sent_ref = bf16[2088,128]{1,0:T(8,128)(2,1)S(1)} collective-permute-done((bf16[2088,128]{1,0:T(8,128)(2,1)S(1)}, bf16[2088,128]{1,0:T(8,128)(2,1)S(1)}, u32[]{:S(2)}, u32[]{:S(2)}) %collective-permute-start.19) | collective-permute-done | bytes 534560 | tf_op jit(solution)/shard_map/cond/branch_2_fun/ppermute | solution.py:507
  40.9 1.6 %merge.22.rest_0_ = bf16[128,4096]{1,0:T(8,128)(2,1)} custom-call(f32[128,4096]{1,0:T(8,128)S(1)} %get-tuple-element.151.mean_ref, f32[128,128]{1,0:T(8,128)S(1)} %get-tuple-element.152._.lse_ref, bf16[2088,128]{1,0:T(8,128)(2,1)S(1)} %collective-permute-done.19.sent_ref), custom_call_target="tpu_custom_call" | custom-call | flops 1048576 | bytes 2097152 | tf_op jit(solution)/shard_map/cond/branch_2_fun/merge/pallas_call | solution.py:370
  42.4 7.1 %collective-permute-done.17.sent_ref = bf16[1576,128]{1,0:T(8,128)(2,1)S(1)} collective-permute-done((bf16[1576,128]{1,0:T(8,128)(2,1)S(1)}, bf16[1576,128]{1,0:T(8,128)(2,1)S(1)}, u32[]{:S(2)}, u32[]{:S(2)}) %collective-permute-start.17) | collective-permute-done | bytes 403488 | tf_op jit(solution)/shard_map/cond/branch_2_fun/ppermute | solution.py:507
  49.5 1.5 %merge.23 = (bf16[128,4096]{1,0:T(8,128)(2,1)}, f32[16,4096]{1,0:T(8,128)S(1)}, f32[16,4096]{1,0:T(8,128)S(1)}) custom-call(f32[128,4096]{1,0:T(8,128)S(1)} %get-tuple-element.151.mean_ref, f32[128,128]{1,0:T(8,128)S(1)} %get-tuple-element.152._.lse_ref, bf16[1576,128]{1,0:T(8,128)(2,1)S(1)} %collective-permute-done.17.sent_ref, ...), custom_call_target="tpu_custom_call", output_to_operand_aliasing={{0}: (3, {})} | custom-call | flops 1048576 | bytes 2097152 | tf_op jit(solution)/shard_map/cond/branch_2_fun/merge/pallas_call | solution.py:370
  51.0 0.4 collective-permute-done.20.sent_ref
  51.4 0.7 %last_merge.11 = bf16[128,4096]{1,0:T(8,128)(2,1)} custom-call(f32[16,4096]{1,0:T(8,128)S(1)} %get-tuple-element.156.scaled_ref, f32[16,4096]{1,0:T(8,128)S(1)} %get-tuple-element.157.share_ref, bf16[512,128]{1,0:T(8,128)(2,1)S(1)} %collective-permute-done.20.sent_ref, bf16[128,4096]{1,0:T(8,128)(2,1)} %get-tuple-element.159._), custom_call_target="tpu_custom_call", output_to_operand_aliasing={{}: (3, {})} | custom-call | tf_op jit(solution)/shard_map/cond/branch_2_fun/last_merge/pallas_call | solution.py:390
Async XLA Ops:
  1.9 4.7 %collective-permute-start.15 = (bf16[128,4096]{1,0:T(8,128)(2,1)}, bf16[128,4096]{1,0:T(8,128)(2,1)S(1)}, u32[]{:S(2)}, u32[]{:S(2)}) collective-permute-start(bf16[128,4096]{1,0:T(8,128)(2,1)} %bitcast.73), channel_id=1, source_target_pairs={{0,1},{1,0},{2,3},{3,2},{4,5},{5,4},{6,7},{7,6},{8,9},{9,8},{10,11... | collective-permute-start | bytes 3145736 | tf_op jit(solution)/shard_map/cond/branch_2_fun/ppermute | solution.py:21
  2.0 4.6 %collective-permute-start.14 = (bf16[128,4096]{1,0:T(8,128)(2,1)}, bf16[128,4096]{1,0:T(8,128)(2,1)S(1)}, u32[]{:S(2)}, u32[]{:S(2)}) collective-permute-start(bf16[128,4096]{1,0:T(8,128)(2,1)} %bitcast.37), channel_id=1, source_target_pairs={{0,1},{1,0},{2,3},{3,2},{4,5},{5,4},{6,7},{7,6},{8,9},{9,8},{10,11... | collective-permute-start | bytes 3145736 | tf_op jit(solution)/shard_map/cond/branch_2_fun/ppermute | solution.py:21
  2.5 15.7 %collective-permute-start.18 = (bf16[64,4096]{1,0:T(8,128)(2,1)S(1)}, bf16[64,4096]{1,0:T(8,128)(2,1)S(1)}, u32[]{:S(2)}, u32[]{:S(2)}) collective-permute-start(bf16[64,4096]{1,0:T(8,128)(2,1)S(1)} %get-tuple-element.155), channel_id=1, source_target_pairs={{0,1},{1,0},{2,3},{3,2},{4,12},{5,13},{6,14},{7,15},{8,9},{9,8},{1... | collective-permute-start | bytes 1572872 | tf_op jit(solution)/shard_map/cond/branch_2_fun/ppermute | solution.py:494
  6.2 12.0 %copy-start.2 = (bf16[1,16,8,4096]{3,2,1,0:T(8,128)(2,1)S(1)}, bf16[1,16,8,4096]{3,2,1,0:T(8,128)(2,1)}, u32[]{:S(2)}) copy-start(bf16[1,16,8,4096]{3,2,1,0:T(8,128)(2,1)} %get-tuple-element.259) | copy-start | bytes 3145732 | tf_op jit(solution)/shard_map/cond
  6.2 12.0 %copy-start.11 = (bf16[1,16,8,4096]{3,2,1,0:T(8,128)(2,1)S(1)}, bf16[1,16,8,4096]{3,2,1,0:T(8,128)(2,1)}, u32[]{:S(2)}) copy-start(bf16[1,16,8,4096]{3,2,1,0:T(8,128)(2,1)} %get-tuple-element.268) | copy-start | bytes 3145732 | tf_op jit(solution)/shard_map/cond
  6.2 23.2 %collective-permute-start.16 = (bf16[64,4096]{1,0:T(8,128)(2,1)S(1)}, bf16[64,4096]{1,0:T(8,128)(2,1)S(1)}, u32[]{:S(2)}, u32[]{:S(2)}) collective-permute-start(bf16[64,4096]{1,0:T(8,128)(2,1)S(1)} %slice.20), channel_id=1, source_target_pairs={{0,1},{1,0},{2,3},{3,2},{4,12},{5,13},{6,14},{7,15},{8,9},{9,8},{1... | collective-permute-start | bytes 1572872 | tf_op jit(solution)/shard_map/cond/branch_2_fun/ppermute | solution.py:498
  21.0 19.9 %collective-permute-start.19 = (bf16[2088,128]{1,0:T(8,128)(2,1)S(1)}, bf16[2088,128]{1,0:T(8,128)(2,1)S(1)}, u32[]{:S(2)}, u32[]{:S(2)}) collective-permute-start(bf16[2088,128]{1,0:T(8,128)(2,1)S(1)} %guest_attention.23), channel_id=1, source_target_pairs={{0,1},{1,0},{2,3},{3,2},{4,12},{5,13},{6,14},{7,15},{8,9},{9,8},{1... | collective-permute-start | bytes 1603592 | tf_op jit(solution)/shard_map/cond/branch_2_fun/ppermute | solution.py:507
  32.2 17.3 %collective-permute-start.17 = (bf16[1576,128]{1,0:T(8,128)(2,1)S(1)}, bf16[1576,128]{1,0:T(8,128)(2,1)S(1)}, u32[]{:S(2)}, u32[]{:S(2)}) collective-permute-start(bf16[1576,128]{1,0:T(8,128)(2,1)S(1)} %get-tuple-element.154), channel_id=1, source_target_pairs={{0,1},{1,0},{2,3},{3,2},{4,12},{5,13},{6,14},{7,15},{8,9},{9,8},{1... | collective-permute-start | bytes 1210376 | tf_op jit(solution)/shard_map/cond/branch_2_fun/ppermute | solution.py:507
  34.9 16.5 %collective-permute-start.20 = (bf16[512,128]{1,0:T(8,128)(2,1)S(1)}, bf16[512,128]{1,0:T(8,128)(2,1)S(1)}, u32[]{:S(2)}, u32[]{:S(2)}) collective-permute-start(bf16[512,128]{1,0:T(8,128)(2,1)S(1)} %get-tuple-element.158), channel_id=1, source_target_pairs={{0,1},{1,0},{2,3},{3,2},{4,12},{5,13},{6,14},{7,15},{8,9},{9,8},{1... | collective-permute-start | bytes 393224 | tf_op jit(solution)/shard_map/cond/branch_2_fun/ppermute | solution.py:507

commit v7 on v6

--- a/solution.py
+++ b/solution.py
@@ -180,7 +180,6 @@
 
 SCALING = HS ** (-0.5)
 LANES = 128
-MARKER = 8
 GROUP = 8
 QUERY_ROWS = (8, 8)
 RETURN_ROWS = ((8,), (6, 2))
@@ -287,20 +286,19 @@
         return found
 
     found = lax.fori_loop(0, heads // GROUP, one_group, jnp.zeros((tokens, LANES), jnp.float32))
+    found = jnp.where(jnp.full(found.shape, matched[0], jnp.int32) > 0, found, NEG_FILL)
     high = found.astype(jnp.bfloat16).astype(jnp.float32)
     pieces = jnp.where(lane // heads % 2 == 0, high, found - high)
     half, at = tokens // 2, heads * sizes[0]
     packed = jnp.where(lane[:half] < LANES // 2, pieces[:half], pieces[half:])
     sent_refs[0][at : at + half, :] = packed.astype(jnp.bfloat16)
-    marker = jnp.full((MARKER, LANES), matched[0], jnp.int32)
-    sent_refs[0][at + half :, :] = marker.astype(jnp.float32).astype(jnp.bfloat16)
 
 
 def guest_attention(matched, query, keys, values, start, sizes, after):
     tokens, width = query.shape
     heads = width // HS
     lengths = [heads * size for size in sizes]
-    lengths[0] += tokens // 2 + MARKER
+    lengths[0] += tokens // 2
     return pl.pallas_call(
         functools.partial(guest_kernel, start),
         in_specs=[pl.BlockSpec(memory_space=pltpu.SMEM)] + [IN_VMEM] * 5 + [IN_PLACE],
@@ -323,8 +321,7 @@
     pieces = sent_ref[at : at + half, :].astype(jnp.float32)
     lse = pieces + pltpu.roll(pieces, LANES - heads, 1)
     lse = jnp.concatenate([lse, pltpu.roll(lse, LANES // 2, 1)], axis=0)
-    matched = sent_ref[at + half : at + half + 1, :].astype(jnp.float32) > 0
-    share = 1.0 / (1.0 + jnp.exp(lse_ref[...] - jnp.where(matched, lse, NEG_FILL)))
+    share = 1.0 / (1.0 + jnp.exp(lse_ref[...] - lse))
 
     def one_group(group, share):
         for inner in range(GROUP):
@@ -482,6 +479,8 @@
     key = key_vectors.reshape(token_count, width)
     value = value_vectors.reshape(token_count, width)
     every = [matching for matching in matchings(list(range(slot_count))) if matching]
+    half = slot_count // 2
+    every.sort(key=lambda pairs: (len(pairs), sum(abs(two - one - half) for one, two in pairs)))
     branch, matched, first_part = prepare(request_of_slot, query, every)
 
     def exchange(matching):

time: 52.4 us -> 52.3 us (level)
  no operation moved by 1% of the time
where the time goes in v7:
time: 52.3 us; the launch traced here: 52.1 us
  waiting for transfers between devices  25.6 us (49%)
  Pallas kernels  15.4 us (29%)
  starting transfers between devices  9.2 us (18%)
  local copies, waits for them, and re-layouts  1.09 us (2%)
  between operations  0.66 us (1%)
    ppermute x3, waiting for transfers between devices, pair_attention(): backs = [lax.ppermute(part, 'view', pairs) for part in sent]  13 us
    ppermute x1, waiting for transfers between devices, pair_attention(): guests = [lax.ppermute(first_part, 'view', pairs)]  6.85 us
    ppermute x1, waiting for transfers between devices, pair_attention(): guests.append(lax.ppermute(sent, 'view', pairs))  5.75 us
    ppermute x3, starting transfers between devices, pair_attention(): backs = [lax.ppermute(part, 'view', pairs) for part in sent]  5.64 us
    pallas_call x2, Pallas kernels, guest_attention(): pl.pallas_call(functools.partial(guest_kernel, start), in_specs=[pl.Block...  5.63 us
    pallas_call x1, Pallas kernels, own_attention(): pl.pallas_call(own_kernel, out_shape=[jax.ShapeDtypeStruct((tokens, width...  4.74 us
    pallas_call x2, Pallas kernels, merge(): pl.pallas_call(merge_kernel, grid=(1,), in_specs=[token_rows(start, token...  3.08 us
    ppermute x1, starting transfers between devices, pair_attention(): guests = [lax.ppermute(first_part, 'view', pairs)]  2.59 us
  transfers between devices with their start and end apart: 7, of which 5 were waited for; matrix products, arithmetic and copies ran while one was open for 2% of the time, Pallas kernels for 26%

profile of v7, /device:TPU:10, one launch (start us, length us, event | category | flops | bytes accessed | tf_op | source)
XLA Modules:
  0.0 52.1 jit_solution(3185124184826589584)
XLA Ops:
  0.0 1.2 %prepare.1 = (s32[1]{0:T(128)}, s32[1]{0:T(128)}, bf16[64,4096]{1,0:T(8,128)(2,1)S(1)}) custom-call(s32[4]{0:T(128)} %request_hbm.1, bf16[128,4096]{1,0:T(8,128)(2,1)} %bitcast.101), custom_call_target="tpu_custom_call" | custom-call | tf_op jit(solution)/shard_map/prepare/pallas_call | solution.py:452
  1.9 50.2 %conditional.1 = (bf16[1,16,8,4096]{3,2,1,0:T(8,128)(2,1)}) conditional(s32[]{:T(128)} %bitcast.28, (bf16[1,16,8,4096]{3,2,1,0:T(8,128)(2,1)}, bf16[1,16,8,4096]{3,2,1,0:T(8,128)(2,1)}, bf16[128,4096]{1,0:T(8,128)(2,1)}, s32[1]{0:T(128)}, bf16[64,4096]{1,0:T(8,128)(2,1)S(1)}) %tuple.60, ...), branch_computations={%region_0.0_spmd, %region_1.0_spmd, %region_2.0_spmd, %region_3.0_... | conditional | flops 807403520 | bytes 44106072 | solution.py:517
  1.9 0.1 collective-permute-start.1
  2.0 0.5 collective-permute-start
  2.5 2.6 %collective-permute-start.4 = (bf16[64,4096]{1,0:T(8,128)(2,1)S(1)}, bf16[64,4096]{1,0:T(8,128)(2,1)S(1)}, u32[]{:S(2)}, u32[]{:S(2)}) collective-permute-start(bf16[64,4096]{1,0:T(8,128)(2,1)S(1)} %get-tuple-element.131), channel_id=1, source_target_pairs={{0,1},{1,0},{2,3},{3,2},{4,12},{5,13},{6,14},{7,15},{8,9},{9,8},{1... | collective-permute-start | bytes 1572872 | tf_op jit(solution)/shard_map/cond/branch_0_fun/ppermute | solution.py:493
  5.1 1.1 %slice.18 = bf16[64,4096]{1,0:T(8,128)(2,1)S(1)} slice(bf16[128,4096]{1,0:T(8,128)(2,1)} %get-tuple-element.124.query_ref), slice={[64:128], [0:4096]} | slice | bytes 1048576 | tf_op jit(solution)/shard_map/cond/branch_0_fun/slice | solution.py:496
  6.2 0.0 copy-start
  6.2 0.0 copy-start.9
  6.2 0.4 collective-permute-start.2
  6.6 0.0 collective-permute-done.1.second_value
  6.6 0.0 collective-permute-done.second_key
  6.6 4.7 %own_attention.9 = (f32[128,4096]{1,0:T(8,128)S(1)}, f32[128,128]{1,0:T(8,128)S(1)}) custom-call(bf16[128,4096]{1,0:T(8,128)(2,1)} %get-tuple-element.124.query_ref, bf16[128,4096]{1,0:T(8,128)(2,1)} %bitcast.30, bf16[128,4096]{1,0:T(8,128)(2,1)S(1)} %collective-permute-done.second_key, bf16[128,4096]{1,0:T(8,128)(2,1)} %bitcast.66, ...), custom_call_target="tpu_custom_call" | custom-call | flops 536870912 | bytes 7340032 | tf_op jit(solution)/shard_map/cond/branch_0_fun/own_attention/pallas_call | solution.py:244
  11.3 6.8 %collective-permute-done.4.query_ref = bf16[64,4096]{1,0:T(8,128)(2,1)S(1)} collective-permute-done((bf16[64,4096]{1,0:T(8,128)(2,1)S(1)}, bf16[64,4096]{1,0:T(8,128)(2,1)S(1)}, u32[]{:S(2)}, u32[]{:S(2)}) %collective-permute-start.4) | collective-permute-done | bytes 524320 | tf_op jit(solution)/shard_map/cond/branch_0_fun/ppermute | solution.py:493
  18.2 0.0 copy-done
  18.2 0.0 copy-done.9
  18.2 2.8 %guest_attention.19 = bf16[2080,128]{1,0:T(8,128)(2,1)S(1)} custom-call(s32[1]{0:T(128)} %get-tuple-element.129.matched, bf16[64,4096]{1,0:T(8,128)(2,1)S(1)} %collective-permute-done.4.query_ref, bf16[128,4096]{1,0:T(8,128)(2,1)S(1)} %bitcast.31, bf16[128,4096]{1,0:T(8,128)(2,1)S(1)} %collective-permute-done.second_key, bf16[128,4096]{1,0:T(8,128)(2,1)S(1)} %bitcast.67, ...), custom_call_target="tpu_custom_call" | custom-call | flops 134217728 | bytes 3145728 | tf_op jit(solution)/shard_map/cond/branch_0_fun/guest_attention/pallas_call | solution.py:302
  21.0 2.7 %collective-permute-start.5 = (bf16[2080,128]{1,0:T(8,128)(2,1)S(1)}, bf16[2080,128]{1,0:T(8,128)(2,1)S(1)}, u32[]{:S(2)}, u32[]{:S(2)}) collective-permute-start(bf16[2080,128]{1,0:T(8,128)(2,1)S(1)} %guest_attention.19), channel_id=1, source_target_pairs={{0,1},{1,0},{2,3},{3,2},{4,12},{5,13},{6,14},{7,15},{8,9},{9,8},{1... | collective-permute-start | bytes 1597448 | tf_op jit(solution)/shard_map/cond/branch_0_fun/ppermute | solution.py:506
  23.7 5.8 %collective-permute-done.2.query_ref = bf16[64,4096]{1,0:T(8,128)(2,1)S(1)} collective-permute-done((bf16[64,4096]{1,0:T(8,128)(2,1)S(1)}, bf16[64,4096]{1,0:T(8,128)(2,1)S(1)}, u32[]{:S(2)}, u32[]{:S(2)}) %collective-permute-start.2) | collective-permute-done | bytes 524320 | tf_op jit(solution)/shard_map/cond/branch_0_fun/ppermute | solution.py:497
  29.4 2.8 %guest_attention.18 = (bf16[1568,128]{1,0:T(8,128)(2,1)S(1)}, bf16[512,128]{1,0:T(8,128)(2,1)S(1)}) custom-call(s32[1]{0:T(128)} %get-tuple-element.129.matched, bf16[64,4096]{1,0:T(8,128)(2,1)S(1)} %collective-permute-done.2.query_ref, bf16[128,4096]{1,0:T(8,128)(2,1)S(1)} %bitcast.32, bf16[128,4096]{1,0:T(8,128)(2,1)S(1)} %collective-permute-done.second_key, ...), custom_call_target="tpu_custom_call" | custom-call | flops 134217728 | bytes 3145728 | tf_op jit(solution)/shard_map/cond/branch_0_fun/guest_attention/pallas_call | solution.py:302
  32.2 2.7 %collective-permute-start.3 = (bf16[1568,128]{1,0:T(8,128)(2,1)S(1)}, bf16[1568,128]{1,0:T(8,128)(2,1)S(1)}, u32[]{:S(2)}, u32[]{:S(2)}) collective-permute-start(bf16[1568,128]{1,0:T(8,128)(2,1)S(1)} %get-tuple-element.130), channel_id=1, source_target_pairs={{0,1},{1,0},{2,3},{3,2},{4,12},{5,13},{6,14},{7,15},{8,9},{9,8},{1... | collective-permute-start | bytes 1204232 | tf_op jit(solution)/shard_map/cond/branch_0_fun/ppermute | solution.py:506
  34.9 0.3 collective-permute-start.6
  35.2 5.6 %collective-permute-done.5.sent_ref = bf16[2080,128]{1,0:T(8,128)(2,1)S(1)} collective-permute-done((bf16[2080,128]{1,0:T(8,128)(2,1)S(1)}, bf16[2080,128]{1,0:T(8,128)(2,1)S(1)}, u32[]{:S(2)}, u32[]{:S(2)}) %collective-permute-start.5) | collective-permute-done | bytes 532512 | tf_op jit(solution)/shard_map/cond/branch_0_fun/ppermute | solution.py:506
  40.8 1.6 %merge.18.rest_0_ = bf16[128,4096]{1,0:T(8,128)(2,1)} custom-call(f32[128,4096]{1,0:T(8,128)S(1)} %get-tuple-element.127.mean_ref, f32[128,128]{1,0:T(8,128)S(1)} %get-tuple-element.128._.lse_ref, bf16[2080,128]{1,0:T(8,128)(2,1)S(1)} %collective-permute-done.5.sent_ref), custom_call_target="tpu_custom_call" | custom-call | flops 1048576 | bytes 2097152 | tf_op jit(solution)/shard_map/cond/branch_0_fun/merge/pallas_call | solution.py:367
  42.4 7.0 %collective-permute-done.3.sent_ref = bf16[1568,128]{1,0:T(8,128)(2,1)S(1)} collective-permute-done((bf16[1568,128]{1,0:T(8,128)(2,1)S(1)}, bf16[1568,128]{1,0:T(8,128)(2,1)S(1)}, u32[]{:S(2)}, u32[]{:S(2)}) %collective-permute-start.3) | collective-permute-done | bytes 401440 | tf_op jit(solution)/shard_map/cond/branch_0_fun/ppermute | solution.py:506
  49.4 1.5 %merge.19 = (bf16[128,4096]{1,0:T(8,128)(2,1)}, f32[16,4096]{1,0:T(8,128)S(1)}, f32[16,4096]{1,0:T(8,128)S(1)}) custom-call(f32[128,4096]{1,0:T(8,128)S(1)} %get-tuple-element.127.mean_ref, f32[128,128]{1,0:T(8,128)S(1)} %get-tuple-element.128._.lse_ref, bf16[1568,128]{1,0:T(8,128)(2,1)S(1)} %collective-permute-done.3.sent_ref, ...), custom_call_target="tpu_custom_call", output_to_operand_aliasing={{0}: (3, {})} | custom-call | flops 1048576 | bytes 2097152 | tf_op jit(solution)/shard_map/cond/branch_0_fun/merge/pallas_call | solution.py:367
  51.0 0.4 collective-permute-done.6.sent_ref
  51.4 0.7 %last_merge.9 = bf16[128,4096]{1,0:T(8,128)(2,1)} custom-call(f32[16,4096]{1,0:T(8,128)S(1)} %get-tuple-element.132.scaled_ref, f32[16,4096]{1,0:T(8,128)S(1)} %get-tuple-element.133.share_ref, bf16[512,128]{1,0:T(8,128)(2,1)S(1)} %collective-permute-done.6.sent_ref, bf16[128,4096]{1,0:T(8,128)(2,1)} %get-tuple-element.135._), custom_call_target="tpu_custom_call", output_to_operand_aliasing={{}: (3, {})} | custom-call | tf_op jit(solution)/shard_map/cond/branch_0_fun/last_merge/pallas_call | solution.py:387
Async XLA Ops:
  1.9 4.7 %collective-permute-start.1 = (bf16[128,4096]{1,0:T(8,128)(2,1)}, bf16[128,4096]{1,0:T(8,128)(2,1)S(1)}, u32[]{:S(2)}, u32[]{:S(2)}) collective-permute-start(bf16[128,4096]{1,0:T(8,128)(2,1)} %bitcast.65), channel_id=1, source_target_pairs={{0,1},{1,0},{2,3},{3,2},{4,5},{5,4},{6,7},{7,6},{8,9},{9,8},{10,11... | collective-permute-start | bytes 3145736 | tf_op jit(solution)/shard_map/cond/branch_0_fun/ppermute | solution.py:21
  2.0 4.6 %collective-permute-start = (bf16[128,4096]{1,0:T(8,128)(2,1)}, bf16[128,4096]{1,0:T(8,128)(2,1)S(1)}, u32[]{:S(2)}, u32[]{:S(2)}) collective-permute-start(bf16[128,4096]{1,0:T(8,128)(2,1)} %bitcast.29), channel_id=1, source_target_pairs={{0,1},{1,0},{2,3},{3,2},{4,5},{5,4},{6,7},{7,6},{8,9},{9,8},{10,11... | collective-permute-start | bytes 3145736 | tf_op jit(solution)/shard_map/cond/branch_0_fun/ppermute | solution.py:21
  2.5 15.7 %collective-permute-start.4 = (bf16[64,4096]{1,0:T(8,128)(2,1)S(1)}, bf16[64,4096]{1,0:T(8,128)(2,1)S(1)}, u32[]{:S(2)}, u32[]{:S(2)}) collective-permute-start(bf16[64,4096]{1,0:T(8,128)(2,1)S(1)} %get-tuple-element.131), channel_id=1, source_target_pairs={{0,1},{1,0},{2,3},{3,2},{4,12},{5,13},{6,14},{7,15},{8,9},{9,8},{1... | collective-permute-start | bytes 1572872 | tf_op jit(solution)/shard_map/cond/branch_0_fun/ppermute | solution.py:493
  6.2 12.0 %copy-start = (bf16[1,16,8,4096]{3,2,1,0:T(8,128)(2,1)S(1)}, bf16[1,16,8,4096]{3,2,1,0:T(8,128)(2,1)}, u32[]{:S(2)}) copy-start(bf16[1,16,8,4096]{3,2,1,0:T(8,128)(2,1)} %get-tuple-element.257) | copy-start | bytes 3145732 | tf_op jit(solution)/shard_map/cond
  6.2 12.0 %copy-start.9 = (bf16[1,16,8,4096]{3,2,1,0:T(8,128)(2,1)S(1)}, bf16[1,16,8,4096]{3,2,1,0:T(8,128)(2,1)}, u32[]{:S(2)}) copy-start(bf16[1,16,8,4096]{3,2,1,0:T(8,128)(2,1)} %get-tuple-element.266) | copy-start | bytes 3145732 | tf_op jit(solution)/shard_map/cond
  6.2 23.2 %collective-permute-start.2 = (bf16[64,4096]{1,0:T(8,128)(2,1)S(1)}, bf16[64,4096]{1,0:T(8,128)(2,1)S(1)}, u32[]{:S(2)}, u32[]{:S(2)}) collective-permute-start(bf16[64,4096]{1,0:T(8,128)(2,1)S(1)} %slice.18), channel_id=1, source_target_pairs={{0,1},{1,0},{2,3},{3,2},{4,12},{5,13},{6,14},{7,15},{8,9},{9,8},{1... | collective-permute-start | bytes 1572872 | tf_op jit(solution)/shard_map/cond/branch_0_fun/ppermute | solution.py:497
  21.0 19.8 %collective-permute-start.5 = (bf16[2080,128]{1,0:T(8,128)(2,1)S(1)}, bf16[2080,128]{1,0:T(8,128)(2,1)S(1)}, u32[]{:S(2)}, u32[]{:S(2)}) collective-permute-start(bf16[2080,128]{1,0:T(8,128)(2,1)S(1)} %guest_attention.19), channel_id=1, source_target_pairs={{0,1},{1,0},{2,3},{3,2},{4,12},{5,13},{6,14},{7,15},{8,9},{9,8},{1... | collective-permute-start | bytes 1597448 | tf_op jit(solution)/shard_map/cond/branch_0_fun/ppermute | solution.py:506
  32.2 17.2 %collective-permute-start.3 = (bf16[1568,128]{1,0:T(8,128)(2,1)S(1)}, bf16[1568,128]{1,0:T(8,128)(2,1)S(1)}, u32[]{:S(2)}, u32[]{:S(2)}) collective-permute-start(bf16[1568,128]{1,0:T(8,128)(2,1)S(1)} %get-tuple-element.130), channel_id=1, source_target_pairs={{0,1},{1,0},{2,3},{3,2},{4,12},{5,13},{6,14},{7,15},{8,9},{9,8},{1... | collective-permute-start | bytes 1204232 | tf_op jit(solution)/shard_map/cond/branch_0_fun/ppermute | solution.py:506
  34.9 16.5 %collective-permute-start.6 = (bf16[512,128]{1,0:T(8,128)(2,1)S(1)}, bf16[512,128]{1,0:T(8,128)(2,1)S(1)}, u32[]{:S(2)}, u32[]{:S(2)}) collective-permute-start(bf16[512,128]{1,0:T(8,128)(2,1)S(1)} %get-tuple-element.134), channel_id=1, source_target_pairs={{0,1},{1,0},{2,3},{3,2},{4,12},{5,13},{6,14},{7,15},{8,9},{9,8},{1... | collective-permute-start | bytes 393224 | tf_op jit(solution)/shard_map/cond/branch_0_fun/ppermute | solution.py:506

commit v8 on v4

--- a/solution.py
+++ b/solution.py
@@ -180,7 +180,6 @@
 
 SCALING = HS ** (-0.5)
 LANES = 128
-MARKER = 8
 GROUP = 8
 QUERY_ROWS = (8, 8)
 RETURN_ROWS = ((8,), (6, 2))
@@ -260,7 +259,7 @@
     return pl.ds(pl.multiple_of(head * tokens, tokens), tokens)
 
 
-def guest_kernel(start, query_ref, first_key, second_key, first_value, second_value, _, *sent_refs):
+def guest_kernel(start, members, slot_devices, query_ref, first_key, second_key, first_value, second_value, _, *sent_refs):
     tokens, width = query_ref.shape
     heads = width // HS
     rows = slice(start, start + tokens)
@@ -287,21 +286,23 @@
         return found
 
     found = lax.fori_loop(0, heads // GROUP, one_group, jnp.zeros((tokens, LANES), jnp.float32))
+    my_slot = jnp.full(found.shape, lax.axis_index("view") // slot_devices, jnp.int32)
+    matched = functools.reduce(jnp.logical_or, [my_slot == slot for slot in members])
+    found = jnp.where(matched, found, NEG_FILL)
     high = found.astype(jnp.bfloat16).astype(jnp.float32)
     pieces = jnp.where(lane // heads % 2 == 0, high, found - high)
     half, at = tokens // 2, heads * sizes[0]
     packed = jnp.where(lane[:half] < LANES // 2, pieces[:half], pieces[half:])
     sent_refs[0][at : at + half, :] = packed.astype(jnp.bfloat16)
-    sent_refs[0][at + half :, :] = jnp.ones((MARKER, LANES), jnp.bfloat16)
-
-
-def guest_attention(query, keys, values, start, sizes, after):
+
+
+def guest_attention(query, keys, values, start, sizes, members, slot_devices, after):
     tokens, width = query.shape
     heads = width // HS
     lengths = [heads * size for size in sizes]
-    lengths[0] += tokens // 2 + MARKER
+    lengths[0] += tokens // 2
     return pl.pallas_call(
-        functools.partial(guest_kernel, start),
+        functools.partial(guest_kernel, start, members, slot_devices),
         in_specs=[IN_VMEM] * 5 + [IN_PLACE],
         out_specs=[IN_VMEM] * len(sizes),
         out_shape=[jax.ShapeDtypeStruct((length, LANES), jnp.bfloat16) for length in lengths],
@@ -322,8 +323,7 @@
     pieces = sent_ref[at : at + half, :].astype(jnp.float32)
     lse = pieces + pltpu.roll(pieces, LANES - heads, 1)
     lse = jnp.concatenate([lse, pltpu.roll(lse, LANES // 2, 1)], axis=0)
-    received = sent_ref[at + half : at + half + 1, :].astype(jnp.float32) > 0
-    share = 1.0 / (1.0 + jnp.exp(lse_ref[...] - jnp.where(received, lse, NEG_FILL)))
+    share = 1.0 / (1.0 + jnp.exp(lse_ref[...] - lse))
 
     def one_group(group, share):
         for inner in range(GROUP):
@@ -409,13 +409,16 @@
     return found
 
 
-def device_pairs(matching, slot_devices):
-    ways = [way for pair in matching for way in (pair, pair[::-1])]
-    return [
-        (source * slot_devices + inner, target * slot_devices + inner)
-        for source, target in ways
-        for inner in range(slot_devices)
-    ]
+def device_pairs(matching, slot_count, slot_devices):
+    other = {slot: slot for slot in range(slot_count)}
+    for one, two in matching:
+        other[one], other[two] = two, one
+    pairs = []
+    for slot in range(slot_count):
+        for inner in range(slot_devices):
+            target = inner if other[slot] != slot else inner ^ 1
+            pairs.append((slot * slot_devices + inner, other[slot] * slot_devices + target))
+    return pairs
 
 
 def prepare(request_of_slot, query, every):
@@ -468,10 +471,13 @@
     key = key_vectors.reshape(token_count, width)
     value = value_vectors.reshape(token_count, width)
     every = [matching for matching in matchings(list(range(slot_count))) if matching]
+    half = slot_count // 2
+    every.sort(key=lambda pairs: (len(pairs), sum(abs(two - one - half) for one, two in pairs)))
     branch, first_part = prepare(request_of_slot, query, every)
 
     def exchange(matching):
-        pairs = device_pairs(matching, slot_devices)
+        pairs = device_pairs(matching, slot_count, slot_devices)
+        members = [slot for pair in matching for slot in pair]
 
         def run(key, value, query, first_part):
             return pair_attention(key, value, query, first_part)
@@ -489,7 +495,7 @@
             returns, start = [], 0
             for guest, rows in zip(guests, RETURN_ROWS):
                 sizes = [row * COLS for row in rows]
-                sent = guest_attention(guest, keys, values, start, sizes, lse)
+                sent = guest_attention(guest, keys, values, start, sizes, members, slot_devices, lse)
                 backs = [lax.ppermute(part, "view", pairs) for part in sent]
                 returns.append((backs, start, sizes))
                 start += guest.shape[0]

time: 54.3 us -> 52.2 us (0.961)
  starting transfers between devices: 18.7 us -> 9.2 us
  waiting for transfers between devices: 19.6 us -> 26.9 us
    ppermute x3, starting transfers between devices: 11.2 us -> 5.64 us  [pair_attention(): backs = [lax.ppermute(part, 'view', pairs) for part in sent]]
    ppermute x3, waiting for transfers between devices: 10 us -> 13.7 us  [pair_attention(): backs = [lax.ppermute(part, 'view', pairs) for part in sent]]
    ppermute x1, starting transfers between devices: 2.38 us -> 0.4 us  [pair_attention(): guests.append(lax.ppermute(sent, 'view', pairs))]
    ppermute x1, starting transfers between devices: 4.49 us -> 2.59 us  [pair_attention(): guests = [lax.ppermute(first_part, 'view', pairs)]]
    ppermute x1, waiting for transfers between devices: 4.54 us -> 6.38 us  [pair_attention(): guests.append(lax.ppermute(sent, 'view', pairs))]
    ppermute x1, waiting for transfers between devices: 5.02 us -> 6.85 us  [pair_attention(): guests = [lax.ppermute(first_part, 'view', pairs)]]
  transfers between devices with their start and end apart: 7 -> 7, of which waited for: 5 -> 5; matrix products, arithmetic and copies ran while one was open for 2% -> 2% of each run, Pallas kernels for 22% -> 23%
where the time goes in v8:
time: 52.2 us; the launch traced here: 52 us
  waiting for transfers between devices  26.9 us (52%)
  Pallas kernels  14.1 us (27%)
  starting transfers between devices  9.2 us (18%)
  local copies, waits for them, and re-layouts  1.09 us (2%)
  between operations  0.66 us (1%)
    ppermute x3, waiting for transfers between devices, pair_attention(): backs = [lax.ppermute(part, 'view', pairs) for part in sent]  13.7 us
    ppermute x1, waiting for transfers between devices, pair_attention(): guests = [lax.ppermute(first_part, 'view', pairs)]  6.85 us
    ppermute x1, waiting for transfers between devices, pair_attention(): guests.append(lax.ppermute(sent, 'view', pairs))  6.38 us
    ppermute x3, starting transfers between devices, pair_attention(): backs = [lax.ppermute(part, 'view', pairs) for part in sent]  5.64 us
    pallas_call x1, Pallas kernels, own_attention(): pl.pallas_call(own_kernel, out_shape=[jax.ShapeDtypeStruct((tokens, width...  4.74 us
    pallas_call x2, Pallas kernels, guest_attention(): pl.pallas_call(functools.partial(guest_kernel, start, members, slot_devic...  4.37 us
    pallas_call x2, Pallas kernels, merge(): pl.pallas_call(merge_kernel, grid=(1,), in_specs=[token_rows(start, token...  3.08 us
    ppermute x1, starting transfers between devices, pair_attention(): guests = [lax.ppermute(first_part, 'view', pairs)]  2.59 us
  transfers between devices with their start and end apart: 7, of which 5 were waited for; matrix products, arithmetic and copies ran while one was open for 2% of the time, Pallas kernels for 23%

profile of v8, /device:TPU:10, one launch (start us, length us, event | category | flops | bytes accessed | tf_op | source)
XLA Modules:
  0.0 52.0 jit_solution(162045367472649087)
XLA Ops:
  0.0 1.2 %prepare.1 = (s32[1]{0:T(128)}, bf16[64,4096]{1,0:T(8,128)(2,1)S(1)}) custom-call(s32[4]{0:T(128)} %request_hbm.1, bf16[128,4096]{1,0:T(8,128)(2,1)} %bitcast.101), custom_call_target="tpu_custom_call" | custom-call | tf_op jit(solution)/shard_map/prepare/pallas_call | solution.py:446
  1.9 50.2 %conditional.1 = (bf16[1,16,8,4096]{3,2,1,0:T(8,128)(2,1)}) conditional(s32[]{:T(128)} %bitcast.28, (bf16[1,16,8,4096]{3,2,1,0:T(8,128)(2,1)}, bf16[1,16,8,4096]{3,2,1,0:T(8,128)(2,1)}, bf16[128,4096]{1,0:T(8,128)(2,1)}, bf16[64,4096]{1,0:T(8,128)(2,1)S(1)}) %tuple.60, (bf16[1,16,8,4096]{3,2,1,0:T(8,128)(2,1)}, ...), branch_computations={%region_0.0_spmd, %region_1.0_spmd, %region_2.0_spmd, %region_3.0_... | conditional | flops 807403520 | bytes 44106072 | solution.py:510
  1.9 0.1 collective-permute-start.1
  2.0 0.5 collective-permute-start
  2.5 2.6 %collective-permute-start.4 = (bf16[64,4096]{1,0:T(8,128)(2,1)S(1)}, bf16[64,4096]{1,0:T(8,128)(2,1)S(1)}, u32[]{:S(2)}, u32[]{:S(2)}) collective-permute-start(bf16[64,4096]{1,0:T(8,128)(2,1)S(1)} %get-tuple-element.112), channel_id=1, source_target_pairs={{0,1},{1,0},{2,3},{3,2},{4,12},{5,13},{6,14},{7,15},{8,9},{9,8},{1... | collective-permute-start | bytes 1572872 | tf_op jit(solution)/shard_map/cond/branch_0_fun/ppermute | solution.py:486
  5.1 1.1 %slice.18 = bf16[64,4096]{1,0:T(8,128)(2,1)S(1)} slice(bf16[128,4096]{1,0:T(8,128)(2,1)} %get-tuple-element.106.query_ref), slice={[64:128], [0:4096]} | slice | bytes 1048576 | tf_op jit(solution)/shard_map/cond/branch_0_fun/slice | solution.py:489
  6.1 0.0 copy-start
  6.1 0.0 copy-start.9
  6.2 0.4 collective-permute-start.2
  6.6 0.0 collective-permute-done.1.second_value
  6.6 0.0 collective-permute-done.second_key
  6.6 4.7 %own_attention.9 = (f32[128,4096]{1,0:T(8,128)S(1)}, f32[128,128]{1,0:T(8,128)S(1)}) custom-call(bf16[128,4096]{1,0:T(8,128)(2,1)} %get-tuple-element.106.query_ref, bf16[128,4096]{1,0:T(8,128)(2,1)} %bitcast.30, bf16[128,4096]{1,0:T(8,128)(2,1)S(1)} %collective-permute-done.second_key, bf16[128,4096]{1,0:T(8,128)(2,1)} %bitcast.66, ...), custom_call_target="tpu_custom_call" | custom-call | flops 536870912 | bytes 7340032 | tf_op jit(solution)/shard_map/cond/branch_0_fun/own_attention/pallas_call | solution.py:244
  11.3 6.8 %collective-permute-done.4.query_ref = bf16[64,4096]{1,0:T(8,128)(2,1)S(1)} collective-permute-done((bf16[64,4096]{1,0:T(8,128)(2,1)S(1)}, bf16[64,4096]{1,0:T(8,128)(2,1)S(1)}, u32[]{:S(2)}, u32[]{:S(2)}) %collective-permute-start.4) | collective-permute-done | bytes 524320 | tf_op jit(solution)/shard_map/cond/branch_0_fun/ppermute | solution.py:486
  18.2 0.0 copy-done
  18.2 0.0 copy-done.9
  18.2 2.2 %guest_attention.19 = bf16[2080,128]{1,0:T(8,128)(2,1)S(1)} custom-call(bf16[64,4096]{1,0:T(8,128)(2,1)S(1)} %collective-permute-done.4.query_ref, bf16[128,4096]{1,0:T(8,128)(2,1)S(1)} %bitcast.31, bf16[128,4096]{1,0:T(8,128)(2,1)S(1)} %collective-permute-done.second_key, bf16[128,4096]{1,0:T(8,128)(2,1)S(1)} %bitcast.67, ...), custom_call_target="tpu_custom_call" | custom-call | flops 134217728 | bytes 3145728 | tf_op jit(solution)/shard_map/cond/branch_0_fun/guest_attention/pallas_call | solution.py:304
  20.4 2.7 %collective-permute-start.5 = (bf16[2080,128]{1,0:T(8,128)(2,1)S(1)}, bf16[2080,128]{1,0:T(8,128)(2,1)S(1)}, u32[]{:S(2)}, u32[]{:S(2)}) collective-permute-start(bf16[2080,128]{1,0:T(8,128)(2,1)S(1)} %guest_attention.19), channel_id=1, source_target_pairs={{0,1},{1,0},{2,3},{3,2},{4,12},{5,13},{6,14},{7,15},{8,9},{9,8},{1... | collective-permute-start | bytes 1597448 | tf_op jit(solution)/shard_map/cond/branch_0_fun/ppermute | solution.py:499
  23.0 6.4 %collective-permute-done.2.query_ref = bf16[64,4096]{1,0:T(8,128)(2,1)S(1)} collective-permute-done((bf16[64,4096]{1,0:T(8,128)(2,1)S(1)}, bf16[64,4096]{1,0:T(8,128)(2,1)S(1)}, u32[]{:S(2)}, u32[]{:S(2)}) %collective-permute-start.2) | collective-permute-done | bytes 524320 | tf_op jit(solution)/shard_map/cond/branch_0_fun/ppermute | solution.py:490
  29.4 2.2 %guest_attention.18 = (bf16[1568,128]{1,0:T(8,128)(2,1)S(1)}, bf16[512,128]{1,0:T(8,128)(2,1)S(1)}) custom-call(bf16[64,4096]{1,0:T(8,128)(2,1)S(1)} %collective-permute-done.2.query_ref, bf16[128,4096]{1,0:T(8,128)(2,1)S(1)} %bitcast.32, bf16[128,4096]{1,0:T(8,128)(2,1)S(1)} %collective-permute-done.second_key, bf16[128,4096]{1,0:T(8,128)(2,1)S(1)} %bitcast.68, ...), custom_call_target="tpu_custom_call" | custom-call | flops 134217728 | bytes 3145728 | tf_op jit(solution)/shard_map/cond/branch_0_fun/guest_attention/pallas_call | solution.py:304
  31.6 2.7 %collective-permute-start.3 = (bf16[1568,128]{1,0:T(8,128)(2,1)S(1)}, bf16[1568,128]{1,0:T(8,128)(2,1)S(1)}, u32[]{:S(2)}, u32[]{:S(2)}) collective-permute-start(bf16[1568,128]{1,0:T(8,128)(2,1)S(1)} %get-tuple-element.111), channel_id=1, source_target_pairs={{0,1},{1,0},{2,3},{3,2},{4,12},{5,13},{6,14},{7,15},{8,9},{9,8},{1... | collective-permute-start | bytes 1204232 | tf_op jit(solution)/shard_map/cond/branch_0_fun/ppermute | solution.py:499
  34.2 0.3 collective-permute-start.6
  34.6 6.2 %collective-permute-done.5.sent_ref = bf16[2080,128]{1,0:T(8,128)(2,1)S(1)} collective-permute-done((bf16[2080,128]{1,0:T(8,128)(2,1)S(1)}, bf16[2080,128]{1,0:T(8,128)(2,1)S(1)}, u32[]{:S(2)}, u32[]{:S(2)}) %collective-permute-start.5) | collective-permute-done | bytes 532512 | tf_op jit(solution)/shard_map/cond/branch_0_fun/ppermute | solution.py:499
  40.8 1.6 %merge.18.rest_0_ = bf16[128,4096]{1,0:T(8,128)(2,1)} custom-call(f32[128,4096]{1,0:T(8,128)S(1)} %get-tuple-element.109.mean_ref, f32[128,128]{1,0:T(8,128)S(1)} %get-tuple-element.110._.lse_ref, bf16[2080,128]{1,0:T(8,128)(2,1)S(1)} %collective-permute-done.5.sent_ref), custom_call_target="tpu_custom_call" | custom-call | flops 1048576 | bytes 2097152 | tf_op jit(solution)/shard_map/cond/branch_0_fun/merge/pallas_call | solution.py:369
  42.4 7.0 %collective-permute-done.3.sent_ref = bf16[1568,128]{1,0:T(8,128)(2,1)S(1)} collective-permute-done((bf16[1568,128]{1,0:T(8,128)(2,1)S(1)}, bf16[1568,128]{1,0:T(8,128)(2,1)S(1)}, u32[]{:S(2)}, u32[]{:S(2)}) %collective-permute-start.3) | collective-permute-done | bytes 401440 | tf_op jit(solution)/shard_map/cond/branch_0_fun/ppermute | solution.py:499
  49.4 1.5 %merge.19 = (bf16[128,4096]{1,0:T(8,128)(2,1)}, f32[16,4096]{1,0:T(8,128)S(1)}, f32[16,4096]{1,0:T(8,128)S(1)}) custom-call(f32[128,4096]{1,0:T(8,128)S(1)} %get-tuple-element.109.mean_ref, f32[128,128]{1,0:T(8,128)S(1)} %get-tuple-element.110._.lse_ref, bf16[1568,128]{1,0:T(8,128)(2,1)S(1)} %collective-permute-done.3.sent_ref, ...), custom_call_target="tpu_custom_call", output_to_operand_aliasing={{0}: (3, {})} | custom-call | flops 1048576 | bytes 2097152 | tf_op jit(solution)/shard_map/cond/branch_0_fun/merge/pallas_call | solution.py:369
  50.9 0.4 collective-permute-done.6.sent_ref
  51.3 0.7 %last_merge.9 = bf16[128,4096]{1,0:T(8,128)(2,1)} custom-call(f32[16,4096]{1,0:T(8,128)S(1)} %get-tuple-element.113.scaled_ref, f32[16,4096]{1,0:T(8,128)S(1)} %get-tuple-element.114.share_ref, bf16[512,128]{1,0:T(8,128)(2,1)S(1)} %collective-permute-done.6.sent_ref, bf16[128,4096]{1,0:T(8,128)(2,1)} %get-tuple-element.116._), custom_call_target="tpu_custom_call", output_to_operand_aliasing={{}: (3, {})} | custom-call | tf_op jit(solution)/shard_map/cond/branch_0_fun/last_merge/pallas_call | solution.py:389
Async XLA Ops:
  1.9 4.7 %collective-permute-start.1 = (bf16[128,4096]{1,0:T(8,128)(2,1)}, bf16[128,4096]{1,0:T(8,128)(2,1)S(1)}, u32[]{:S(2)}, u32[]{:S(2)}) collective-permute-start(bf16[128,4096]{1,0:T(8,128)(2,1)} %bitcast.65), channel_id=1, source_target_pairs={{0,1},{1,0},{2,3},{3,2},{4,5},{5,4},{6,7},{7,6},{8,9},{9,8},{10,11... | collective-permute-start | bytes 3145736 | tf_op jit(solution)/shard_map/cond/branch_0_fun/ppermute | solution.py:21
  2.0 4.6 %collective-permute-start = (bf16[128,4096]{1,0:T(8,128)(2,1)}, bf16[128,4096]{1,0:T(8,128)(2,1)S(1)}, u32[]{:S(2)}, u32[]{:S(2)}) collective-permute-start(bf16[128,4096]{1,0:T(8,128)(2,1)} %bitcast.29), channel_id=1, source_target_pairs={{0,1},{1,0},{2,3},{3,2},{4,5},{5,4},{6,7},{7,6},{8,9},{9,8},{10,11... | collective-permute-start | bytes 3145736 | tf_op jit(solution)/shard_map/cond/branch_0_fun/ppermute | solution.py:21
  2.5 15.7 %collective-permute-start.4 = (bf16[64,4096]{1,0:T(8,128)(2,1)S(1)}, bf16[64,4096]{1,0:T(8,128)(2,1)S(1)}, u32[]{:S(2)}, u32[]{:S(2)}) collective-permute-start(bf16[64,4096]{1,0:T(8,128)(2,1)S(1)} %get-tuple-element.112), channel_id=1, source_target_pairs={{0,1},{1,0},{2,3},{3,2},{4,12},{5,13},{6,14},{7,15},{8,9},{9,8},{1... | collective-permute-start | bytes 1572872 | tf_op jit(solution)/shard_map/cond/branch_0_fun/ppermute | solution.py:486
  6.1 12.0 %copy-start = (bf16[1,16,8,4096]{3,2,1,0:T(8,128)(2,1)S(1)}, bf16[1,16,8,4096]{3,2,1,0:T(8,128)(2,1)}, u32[]{:S(2)}) copy-start(bf16[1,16,8,4096]{3,2,1,0:T(8,128)(2,1)} %get-tuple-element.228) | copy-start | bytes 3145732 | tf_op jit(solution)/shard_map/cond
  6.1 12.0 %copy-start.9 = (bf16[1,16,8,4096]{3,2,1,0:T(8,128)(2,1)S(1)}, bf16[1,16,8,4096]{3,2,1,0:T(8,128)(2,1)}, u32[]{:S(2)}) copy-start(bf16[1,16,8,4096]{3,2,1,0:T(8,128)(2,1)} %get-tuple-element.237) | copy-start | bytes 3145732 | tf_op jit(solution)/shard_map/cond
  6.2 23.2 %collective-permute-start.2 = (bf16[64,4096]{1,0:T(8,128)(2,1)S(1)}, bf16[64,4096]{1,0:T(8,128)(2,1)S(1)}, u32[]{:S(2)}, u32[]{:S(2)}) collective-permute-start(bf16[64,4096]{1,0:T(8,128)(2,1)S(1)} %slice.18), channel_id=1, source_target_pairs={{0,1},{1,0},{2,3},{3,2},{4,12},{5,13},{6,14},{7,15},{8,9},{9,8},{1... | collective-permute-start | bytes 1572872 | tf_op jit(solution)/shard_map/cond/branch_0_fun/ppermute | solution.py:490
  20.4 20.4 %collective-permute-start.5 = (bf16[2080,128]{1,0:T(8,128)(2,1)S(1)}, bf16[2080,128]{1,0:T(8,128)(2,1)S(1)}, u32[]{:S(2)}, u32[]{:S(2)}) collective-permute-start(bf16[2080,128]{1,0:T(8,128)(2,1)S(1)} %guest_attention.19), channel_id=1, source_target_pairs={{0,1},{1,0},{2,3},{3,2},{4,12},{5,13},{6,14},{7,15},{8,9},{9,8},{1... | collective-permute-start | bytes 1597448 | tf_op jit(solution)/shard_map/cond/branch_0_fun/ppermute | solution.py:499
  31.6 17.8 %collective-permute-start.3 = (bf16[1568,128]{1,0:T(8,128)(2,1)S(1)}, bf16[1568,128]{1,0:T(8,128)(2,1)S(1)}, u32[]{:S(2)}, u32[]{:S(2)}) collective-permute-start(bf16[1568,128]{1,0:T(8,128)(2,1)S(1)} %get-tuple-element.111), channel_id=1, source_target_pairs={{0,1},{1,0},{2,3},{3,2},{4,12},{5,13},{6,14},{7,15},{8,9},{9,8},{1... | collective-permute-start | bytes 1204232 | tf_op jit(solution)/shard_map/cond/branch_0_fun/ppermute | solution.py:499
  34.2 17.1 %collective-permute-start.6 = (bf16[512,128]{1,0:T(8,128)(2,1)S(1)}, bf16[512,128]{1,0:T(8,128)(2,1)S(1)}, u32[]{:S(2)}, u32[]{:S(2)}) collective-permute-start(bf16[512,128]{1,0:T(8,128)(2,1)S(1)} %get-tuple-element.115), channel_id=1, source_target_pairs={{0,1},{1,0},{2,3},{3,2},{4,12},{5,13},{6,14},{7,15},{8,9},{9,8},{1... | collective-permute-start | bytes 393224 | tf_op jit(solution)/shard_map/cond/branch_0_fun/ppermute | solution.py:499
